TPU v7x, 32 devices: a whole 2x2x4 slice. The times are simulated.
32 devices in a mesh: cols: 2 (over core), space: 16 (over z, y, x).
Axes of the slice: x: 2, y: 2, z: 4, core: 2. Of those that a mesh axis runs over, the one named last changes fastest.
Arguments:
- mean_state: float32 [6, 256, 256], P(None, 'space', 'cols'), may hold values from -2 to 2
- covariance: float32 [128, 6, 256, 256], P('cols', None, 'space'), may hold values from -2 to 2
- land_mask: int32 [256, 256], replicated, may hold values 0 or 1
- stations: int32 [2048], P('space'), may hold values from 0 to 65535, as said below
- observed: float32 [2048], P('space'), may hold values from -5 to 5
- obs_weight: float32 [2048], P('space'), may hold values from 0.5 to 4
Outputs:
- mean_analysis: float32 [6, 256, 256], P(None, 'space', 'cols')
- covariance_analysis: float32 [128, 6, 256, 256], P('cols', None, 'space')
Inputs may be any that keep to these rules, and one draw needn't show every extreme that they name: Stations b * 128 to (b + 1) * 128 - 1 lie in grid rows b * 16 to (b + 1) * 16 - 1; several stations may share a cell.
All inputs are finite; a program needn't handle non-finite values.
Results may differ from a plain program's by a relative error of at most 0.0053.
Values may be sent and summed in bfloat16 or wider, within the bound.
No kernel may reach another device: no remote copies, remote signals or barrier semaphores. Data moves between devices by JAX's collectives and lax.ppermute only.
A program may use at most 128 MiB of HBM per device.

v0:
```python
import jax
import jax.numpy as jnp
from jax import lax
from jax.sharding import PartitionSpec as P

ITERS = 4


time_step = 0.5
gravity = 1.0
reduced_gravity = 0.125
coriolis = 0.3
friction = 0.05
layer_depths = (1.0, 2.0)


def padded_2(block, sides, width):
    for axis, dim in sides:
        count = lax.axis_size(axis)
        forward = [(i, i + 1) for i in range(count - 1)]
        backward = [(target, source) for source, target in forward]
        low = lax.ppermute(
            lax.slice_in_dim(block, block.shape[dim] - width, None, axis=dim), axis, forward
        )
        high = lax.ppermute(lax.slice_in_dim(block, 0, width, axis=dim), axis, backward)
        block = jnp.concatenate([low, block, high], axis=dim)
    return block


def diff_rows(values):
    return 0.5 * (values[..., 2:, 1:-1] - values[..., :-2, 1:-1])


def diff_cols(values):
    return 0.5 * (values[..., 1:-1, 2:] - values[..., 1:-1, :-2])


def inner(values):
    return values[..., 1:-1, 1:-1]


def velocities(field, wet_cells):
    wet_inner = inner(wet_cells)
    surface = field[..., 0, :, :] + field[..., 3, :, :]
    pressure_top = gravity * surface
    pressure_pair = (pressure_top, pressure_top - reduced_gravity * field[..., 0, :, :])
    velocity_pairs = []
    for layer_index in range(2):
        zonal = inner(field[..., 3 * layer_index + 1, :, :])
        north = inner(field[..., 3 * layer_index + 2, :, :])
        pressure = pressure_pair[layer_index]
        zonal_new = wet_inner * (
            zonal + time_step * (-diff_rows(pressure) + coriolis * north - friction * zonal)
        )
        north_new = wet_inner * (
            north + time_step * (-diff_cols(pressure) - coriolis * zonal - friction * north)
        )
        velocity_pairs.append((zonal_new, north_new))
    return velocity_pairs


def mean_core(padded, wet_cells):
    velocity_pairs = velocities(padded, wet_cells)
    fields = []
    carried = []
    for layer_index in range(2):
        thickness = padded[3 * layer_index]
        column_depth = layer_depths[layer_index] + inner(thickness)
        zonal_new, north_new = velocity_pairs[layer_index]
        updated = thickness[2:-2, 2:-2] - time_step * (
            diff_rows(column_depth * zonal_new) + diff_cols(column_depth * north_new)
        )
        fields += [updated, zonal_new[1:-1, 1:-1], north_new[1:-1, 1:-1]]
        carried += [thickness[1:-1, 2:-2], zonal_new[:, 1:-1], north_new[:, 1:-1]]
    return (jnp.stack(fields), jnp.stack(carried))


def tangent_core(padded, carried, wet_cells):
    beside_all = jnp.pad(carried, ((0, 0), (0, 0), (1, 1)))
    velocity_pairs = velocities(padded, wet_cells)
    fields = []
    for layer_index in range(2):
        thickness = padded[..., 3 * layer_index, :, :]
        column_depth = layer_depths[layer_index] + beside_all[3 * layer_index]
        zonal_new, north_new = velocity_pairs[layer_index]
        flux_rows = column_depth * zonal_new + inner(thickness) * beside_all[3 * layer_index + 1]
        flux_cols = column_depth * north_new + inner(thickness) * beside_all[3 * layer_index + 2]
        updated = thickness[..., 2:-2, 2:-2] - time_step * (
            diff_rows(flux_rows) + diff_cols(flux_cols)
        )
        fields += [updated, zonal_new[..., 1:-1, 1:-1], north_new[..., 1:-1, 1:-1]]
    return jnp.stack(fields, axis=-3)


def local(mean_state, covariance, land_mask, stations, observed, obs_weight):
    local_cols = covariance.shape[0]
    tile_rows = covariance.shape[2]
    grid_cols = covariance.shape[3]
    piece_cols = mean_state.shape[2]
    total_cols = local_cols * lax.axis_size("cols")
    space_index = lax.axis_index("space")
    column_index = lax.axis_index("cols")
    land_float = land_mask.astype(jnp.float32)
    first_row = space_index * tile_rows
    columns = covariance
    depth = 2 * ITERS
    grid_rows = tile_rows * lax.axis_size("space")
    mean_now = lax.all_gather(mean_state, "cols", axis=2, tiled=True)
    mean_now = padded_2(mean_now, (("space", 1),), depth)
    columns = padded_2(columns, (("space", 2),), depth)
    wet_deep = jnp.pad(land_float, ((depth, depth), (2, 2)))
    rows_here = first_row - depth + jnp.arange(tile_rows + 2 * depth, dtype=jnp.int32)
    inside = jnp.logical_and(rows_here >= 0, rows_here < grid_rows).astype(jnp.float32)
    for step_index in range(ITERS):
        extent = depth - 2 * step_index
        shrink = 2 * step_index
        wet_cells = lax.dynamic_slice_in_dim(
            wet_deep, first_row + shrink, tile_rows + 2 * extent, 0
        )
        padded_mean = jnp.pad(mean_now, ((0, 0), (0, 0), (2, 2)))
        mean_next, carried = mean_core(padded_mean, wet_cells)
        padded_columns = jnp.pad(columns, ((0, 0), (0, 0), (0, 0), (2, 2)))
        columns_next = tangent_core(padded_columns, carried, wet_cells)
        keep = inside[shrink + 2 : shrink + 2 + tile_rows + 2 * (extent - 2)]
        mean_now = mean_next * keep[None, :, None]
        columns = columns_next * keep[:, None]
    mean_piece = lax.dynamic_slice_in_dim(mean_now, column_index * piece_cols, piece_cols, 2)
    surface = mean_now[0] + mean_now[3]
    offset_stations = stations - first_row * grid_cols
    column_surface = (columns[:, 0] + columns[:, 3]).reshape(local_cols, tile_rows * grid_cols)
    sensed_local = jnp.take(column_surface, offset_stations, axis=1) * obs_weight[None, :]
    innovation = obs_weight * (observed - jnp.take(surface.reshape(-1), offset_stations))
    sensed = lax.all_gather(sensed_local, "cols", axis=0, tiled=True)
    products = jnp.dot(
        sensed, sensed.T, precision=lax.Precision.HIGHEST, preferred_element_type=jnp.float32
    )
    target_part = jnp.dot(
        sensed, innovation, precision=lax.Precision.HIGHEST, preferred_element_type=jnp.float32
    )
    gram_sum, target = lax.psum((products, target_part), "space")
    identity = jnp.eye(total_cols, dtype=jnp.float32)
    gram_matrix = identity + gram_sum
    lower_factor = lax.linalg.cholesky(gram_matrix)
    halfway = lax.linalg.triangular_solve(lower_factor, target[:, None], left_side=True, lower=True)
    weights = lax.linalg.triangular_solve(
        lower_factor, halfway, left_side=True, lower=True, transpose_a=True
    )[:, 0]
    inverse = lax.linalg.triangular_solve(lower_factor, identity, left_side=True, lower=True)
    transform_low = inverse.T.astype(jnp.bfloat16)
    weights_local = lax.dynamic_slice_in_dim(weights, column_index * local_cols, local_cols)
    increment_terms = jnp.einsum(
        "k,kfrc->frc", weights_local, columns, precision=lax.Precision.HIGHEST
    )
    increment_total = lax.psum(increment_terms, "cols")
    increment = lax.dynamic_slice_in_dim(increment_total, column_index * piece_cols, piece_cols, 2)
    columns_low = columns.astype(jnp.bfloat16)
    shard_piece = lax.all_gather(columns_low, "cols", axis=0, tiled=True)
    transform_part = lax.dynamic_slice(
        transform_low, (0, column_index * local_cols), (shard_piece.shape[0], local_cols)
    )
    updated = jnp.einsum(
        "kj,kfrc->jfrc", transform_part, shard_piece, preferred_element_type=jnp.float32
    )
    return (mean_piece + increment, updated)


def solution(mesh):
    return jax.shard_map(
        local,
        mesh=mesh,
        in_specs=(
            P(None, "space", "cols"),
            P("cols", None, "space", None),
            P(),
            P("space"),
            P("space"),
            P("space"),
        ),
        out_specs=(P(None, "space", "cols"), P("cols", None, "space", None)),
        check_vma=False,
    )
```

profile of v0, /device:TPU:0, one launch (start us, length us, event | category | flops | bytes accessed | tf_op | source)
XLA Modules:
  0.0 518.6 jit_solution(15029220077060353122)
XLA Ops:
  7.2 6.4 %copy.20 = f32[64,6,16,256]{3,0,2,1:T(8,128)S(1)} copy(f32[64,6,16,256]{3,2,1,0:T(8,128)} %param.7) | data formatting | bytes 12582912 | tf_op args[1]
  13.6 2.6 fusion.460
  18.5 7.3 %collective-permute-start.2 = (f32[64,6,8,256]{3,0,2,1:T(8,128)S(1)}, f32[64,6,8,256]{3,0,2,1:T(8,128)}, u32[]{:S(2)}, u32[]{:S(2)}) collective-permute-start(f32[64,6,8,256]{3,0,2,1:T(8,128)S(1)} %get-tuple-element.128), channel_id=1, source_target_pairs={{0,1},{1,2},{2,3},{3,4},{4,5},{5,6},{6,7},{7,8},{8,9},{9,10},{10,1... | collective-permute-start | bytes 9437192 | tf_op jit(solution)/shard_map/ppermute | solution.py:22
  25.8 1.9 all_gather.9
  29.6 5.2 collective-permute-start
  39.9 119.6 %collective-permute-done.1 = f32[6,8,256]{2,1,0:T(8,128)} collective-permute-done((f32[6,8,256]{2,1,0:T(8,128)}, f32[6,8,256]{2,1,0:T(8,128)}, u32[]{:S(2)}, u32[]{:S(2)}) %collective-permute-start.1) | collective-permute-done | bytes 49184 | tf_op jit(solution)/shard_map/ppermute | solution.py:25
  168.1 2.1 gather_fusion.1
  170.3 1.6 fusion.298
  171.9 1.6 fusion.306
  181.6 9.8 %select_maximum_fusion = f32[64,6,32,260]{3,0,2,1:T(8,128)S(1)} fusion(f32[64,6,8,256]{3,0,2,1:T(8,128)} %collective-permute-done.3, f32[64,6,16,256]{3,0,2,1:T(8,128)} %copy-done, f32[64,6,8,256]{3,0,2,1:T(8,128)} %collective-permute-done.2), kind=kLoop, calls=%fused_computation.16 | loop fusion | flops 25559040 | bytes 25362432 | tf_op jit(solution)/shard_map/concatenate | solution.py:26
  191.5 6.6 %slice_bitcast_fusion = (f32[64,32,260]{2,0,1:T(8,128)}, f32[64,32,260]{2,0,1:T(8,128)}, f32[64,32,260]{2,0,1:T(8,128)}, f32[64,32,260]{2,0,1:T(8,128)}, f32[64,32,260]{2,0,1:T(8,128)}, /*index=5*/f32[64,32,260]{2,0,1:T(8,128)}) fusion(f32[64,6,32,260]{3,0,2,1:T(8,128)S(1)} %select_maximum_fusion), kind=kLoop, calls=%fused_computation.28 | loop fusion | bytes 25559040 | tf_op jit(solution)/shard_map/squeeze | solution.py:50
  198.2 2.2 multiply_subtract_fusion
  200.4 12.8 %multiply_add_fusion.3 = (f32[64,30,258]{2,0,1:T(8,128)S(1)}, f32[64,30,258]{2,0,1:T(8,128)}, f32[64,30,258]{2,0,1:T(8,128)S(1)}, f32[64,30,258]{2,0,1:T(8,128)S(1)}) fusion(f32[64,32,260]{2,0,1:T(8,128)} %get-tuple-element.85, f32[30,258]{1,0:T(8,128)S(1)} %copy-done.51, f32[30,258]{1,0:T(8,128)S(1)} %copy-done.53, f32[64,32,260]{2,0,1:T(8,128)} %get-tuple-element.82, ...), kind=kLoop, calls=%fused_computation.71 | loop fusion | flops 12879360 | bytes 21919680 | tf_op jit(solution)/shard_map/add | solution.py:86
  213.3 3.2 fusion.116
  216.5 1.8 fusion.111
  218.3 1.8 fusion.110
  221.0 6.6 %multiply_add_fusion.1 = (f32[64,30,258]{2,0,1:T(8,128)S(1)}, f32[64,30,258]{2,0,1:T(8,128)}, f32[64,30,258]{2,0,1:T(8,128)S(1)}, f32[64,30,258]{2,0,1:T(8,128)S(1)}) fusion(f32[64,32,260]{2,0,1:T(8,128)S(1)} %copy-done.2, f32[30,258]{1,0:T(8,128)S(1)} %copy-done.48, f32[30,258]{1,0:T(8,128)S(1)} %copy-done.49, f32[64,32,260]{2,0,1:T(8,128)S(1)} %copy-done.4, ...), kind=kLoop, calls=%fused_computation.69 | loop fusion | flops 12879360 | bytes 21919680 | tf_op jit(solution)/shard_map/add | solution.py:86
  227.6 3.3 fusion.109
  230.9 1.8 fusion.104
  232.7 1.8 fusion.103
  234.5 6.5 %broadcast_multiply_fusion = f32[64,6,28,256]{3,0,2,1:T(8,128)S(1)} fusion(f32[64,6,28,256]{3,0,2,1:T(8,128)} %fusion.103, f32[28]{0:T(128)S(1)} %copy-done.73), kind=kLoop, calls=%fused_computation.25 | loop fusion | flops 2752512 | bytes 22020208 | tf_op jit(solution)/shard_map/mul | solution.py:126
  241.0 6.7 %fusion.34 = (f32[64,28,260]{2,0,1:T(8,128)}, f32[64,28,260]{2,0,1:T(8,128)}, f32[64,28,260]{2,0,1:T(8,128)S(1)}, f32[64,28,260]{2,0,1:T(8,128)}, f32[64,28,260]{2,0,1:T(8,128)}, /*index=5*/f32[64,28,260]{2,0,1:T(8,128)S(1)}) fusion(f32[64,6,28,256]{3,0,2,1:T(8,128)S(1)} %broadcast_multiply_fusion), kind=kLoop, calls=%fused_computation.77 | loop fusion | bytes 22192128 | tf_op jit(solution)/shard_map/squeeze | solution.py:50
  247.7 2.9 multiply_subtract_fusion.1
  250.6 7.8 %multiply_add_fusion.7 = (f32[64,26,258]{2,0,1:T(8,128)S(1)}, f32[64,26,258]{2,0,1:T(8,128)}, f32[64,26,258]{2,0,1:T(8,128)S(1)}, f32[64,26,258]{2,0,1:T(8,128)}) fusion(f32[64,28,260]{2,0,1:T(8,128)S(1)} %get-tuple-element.101, f32[26,258]{1,0:T(8,128)S(1)} %copy-done.45, f32[26,258]{1,0:T(8,128)S(1)} %copy-done.47, f32[64,28,260]{2,0,1:T(8,128)} %get-tuple-element.99, ...), kind=kLoop, calls=%fused_computation.114 | loop fusion | flops 11162112 | bytes 18997056 | tf_op jit(solution)/shard_map/add | solution.py:86
  258.5 1.8 fusion.158
  263.0 5.8 %multiply_add_fusion.5 = (f32[64,26,258]{2,0,1:T(8,128)S(1)}, f32[64,26,258]{2,0,1:T(8,128)}, f32[64,26,258]{2,0,1:T(8,128)S(1)}, f32[64,26,258]{2,0,1:T(8,128)}) fusion(f32[64,28,260]{2,0,1:T(8,128)S(1)} %get-tuple-element.98, f32[26,258]{1,0:T(8,128)S(1)} %get-tuple-element.142, f32[26,258]{1,0:T(8,128)S(1)} %get-tuple-element.145, ...), kind=kLoop, calls=%fused_computation.112 | loop fusion | flops 11162112 | bytes 18997056 | tf_op jit(solution)/shard_map/add | solution.py:86
  268.8 1.7 fusion.151
  272.7 2.1 broadcast_multiply_fusion.1
  274.8 4.0 fusion.68
  278.9 2.5 multiply_subtract_fusion.2
  281.4 5.8 %multiply_add_fusion.11 = (f32[64,22,258]{2,0,1:T(8,128)S(1)}, f32[64,22,258]{2,0,1:T(8,128)}, f32[64,22,258]{2,0,1:T(8,128)S(1)}, f32[64,22,258]{2,0,1:T(8,128)}) fusion(f32[64,24,260]{2,0,1:T(8,128)S(1)} %get-tuple-element.113, f32[22,258]{1,0:T(8,128)S(1)} %copy-done.57, f32[22,258]{1,0:T(8,128)} %get-tuple-element.185, ...), kind=kLoop, calls=%fused_computation.157 | loop fusion | flops 9444864 | bytes 16074432 | tf_op jit(solution)/shard_map/add | solution.py:86
  290.7 4.1 multiply_add_fusion.9
  298.4 7.0 %fusion.102 = (f32[64,20,260]{2,0,1:T(8,128)}, f32[64,20,260]{2,0,1:T(8,128)}, f32[64,20,260]{2,0,1:T(8,128)S(1)}, f32[64,20,260]{2,0,1:T(8,128)}, f32[64,20,260]{2,0,1:T(8,128)}, /*index=5*/f32[64,20,260]{2,0,1:T(8,128)}) fusion(f32[64,6,20,256]{3,0,2,1:T(8,128)S(1)} %broadcast_multiply_fusion.2), kind=kLoop, calls=%fused_computation.163 | loop fusion | bytes 15851520 | tf_op jit(solution)/shard_map/squeeze | solution.py:50
  305.4 2.1 multiply_subtract_fusion.3
  308.1 3.0 multiply_add_fusion.15
  314.5 3.3 multiply_add_fusion.13
  319.6 3.2 fusion.427
  322.9 2.7 copy-done.1
  327.3 1.9 all_gather.10
  330.4 41.4 %psum.22 = f32[128]{0:T(128)S(1)} all-reduce(f32[128]{0:T(128)S(1)} %convolution_bitcast_fusion.2), channel_id=1, replica_groups=mesh['cols'=2,'space'=16] {'space'}, use_global_device_ids=true, to_apply=%region_3.4 | all-reduce | flops 128 | bytes 1024 | tf_op jit(solution)/shard_map/psum | solution.py:140
  371.8 62.5 %all-reduce.16.cloned.1.call-done = f32[128,128]{1,0:T(8,128)} async-done(((f32[128,128]{1,0:T(8,128)}), f32[128,128]{1,0:T(8,128)}) %all-reduce.16.cloned.1.call-update) | async-done | bytes 65552 | tf_op jit(solution)/shard_map/psum | solution.py:140
  436.1 11.7 %cholesky.18 = f32[128,128]{1,0:T(8,128)S(1)} custom-call(f32[128,128]{1,0:T(8,128)S(1)} %fusion.193), custom_call_target="Cholesky" | custom-call | tf_op jit(solution)/shard_map/cholesky | solution.py:143
  449.2 9.8 %custom-call.9 = f32[1,128,128]{1,2,0:T(8,128)S(1)} custom-call(f32[1,128,128]{2,1,0:T(8,128)S(1)} %fusion.188), custom_call_target="InvertDiagBlocksLowerTriangular" | custom-call | tf_op jit(solution)/shard_map/triangular_solve | solution.py:145
  459.3 5.1 fusion.409
  466.1 16.0 %all-reduce.18.cloned.1.call-done = f32[6,16,256]{2,1,0:T(8,128)} async-done(((f32[6,16,256]{2,1,0:T(8,128)}), f32[6,16,256]{2,1,0:T(8,128)}) %all-reduce.18.cloned.1.call-update) | async-done | bytes 98320 | tf_op jit(solution)/shard_map/psum | solution.py:154
  483.6 18.1 %all-gather.2.cloned.1.call-done = bf16[128,6,16,256]{3,0,2,1:T(8,128)(2,1)} async-done(((bf16[64,6,16,256]{3,0,2,1:T(8,128)(2,1)}), bf16[128,6,16,256]{3,0,2,1:T(8,128)(2,1)}) %all-gather.2.cloned.1.call-update) | async-done | bytes 6291472 | tf_op jit(solution)/shard_map/all_gather | solution.py:157
  501.7 3.8 fusion.397
  505.5 6.3 %copy.27 = f32[64,6,16,256]{3,2,1,0:T(8,128)} copy(f32[64,6,16,256]{3,0,2,1:T(8,128)S(1)} %fusion.397) | data formatting | bytes 12582912
  (289 shorter events, 53.8 us)
Async XLA Ops:
  7.2 427.1 %all-reduce.16.cloned.1.call-start = ((), (), s32[]{:S(2)}) async-start(), calls=%async_computation | async-start | bytes 131072 | tf_op jit(solution)/shard_map/psum | solution.py:140
  13.6 3.7 copy-start
  13.6 12.2 %copy-start.65 = (f32[6,16,128]{2,1,0:T(8,128)S(1)}, f32[6,16,128]{2,1,0:T(8,128)}, u32[]{:S(2)}) copy-start(f32[6,16,128]{2,1,0:T(8,128)} %param.6) | copy-start | bytes 147460
  13.6 21.1 %copy-start.80 = (s32[128]{0:T(128)S(1)}, s32[128]{0:T(128)}, u32[]{:S(2)}) copy-start(s32[128]{0:T(128)} %param.9) | copy-start | bytes 1540
  17.2 164.4 %collective-permute-start.3 = (f32[64,6,8,256]{3,0,2,1:T(8,128)}, f32[64,6,8,256]{3,0,2,1:T(8,128)}, u32[]{:S(2)}, u32[]{:S(2)}) collective-permute-start(f32[64,6,8,256]{3,0,2,1:T(8,128)} %get-tuple-element.129), channel_id=1, source_target_pairs={{1,0},{2,1},{3,2},{4,3},{5,4},{6,5},{7,6},{8,7},{9,8},{10,9},{11,1... | collective-permute-start | bytes 9437192 | tf_op jit(solution)/shard_map/ppermute | solution.py:25
  18.5 163.1 %collective-permute-start.2 = (f32[64,6,8,256]{3,0,2,1:T(8,128)S(1)}, f32[64,6,8,256]{3,0,2,1:T(8,128)}, u32[]{:S(2)}, u32[]{:S(2)}) collective-permute-start(f32[64,6,8,256]{3,0,2,1:T(8,128)S(1)} %get-tuple-element.128), channel_id=1, source_target_pairs={{0,1},{1,2},{2,3},{3,4},{4,5},{5,6},{6,7},{7,8},{8,9},{9,10},{10,1... | collective-permute-start | bytes 9437192 | tf_op jit(solution)/shard_map/ppermute | solution.py:22
  28.3 131.2 %collective-permute-start.1 = (f32[6,8,256]{2,1,0:T(8,128)}, f32[6,8,256]{2,1,0:T(8,128)}, u32[]{:S(2)}, u32[]{:S(2)}) collective-permute-start(f32[6,8,256]{2,1,0:T(8,128)} %get-tuple-element.195), channel_id=1, source_target_pairs={{1,0},{2,1},{3,2},{4,3},{5,4},{6,5},{7,6},{8,7},{9,8},{10,9},{11,1... | collective-permute-start | bytes 147464 | tf_op jit(solution)/shard_map/ppermute | solution.py:25
  29.6 131.3 %collective-permute-start = (f32[6,8,256]{2,1,0:T(8,128)S(1)}, f32[6,8,256]{2,1,0:T(8,128)}, u32[]{:S(2)}, u32[]{:S(2)}) collective-permute-start(f32[6,8,256]{2,1,0:T(8,128)S(1)} %get-tuple-element.194), channel_id=1, source_target_pairs={{0,1},{1,2},{2,3},{3,4},{4,5},{5,6},{6,7},{7,8},{8,9},{9,10},{10,1... | collective-permute-start | bytes 147464 | tf_op jit(solution)/shard_map/ppermute | solution.py:22
  39.9 123.0 %copy-start.72 = (f32[28]{0:T(128)S(1)}, f32[28]{0:T(128)}, u32[]{:S(2)}) copy-start(f32[28]{0:T(128)} %slice.1097) | copy-start | bytes 340
  163.4 2.6 copy-start.41
  163.7 3.0 copy-start.36
  163.7 3.0 copy-start.38
  163.7 3.0 copy-start.40
  164.4 3.1 copy-start.68
  166.5 12.3 %copy-start.29 = (f32[28,260]{1,0:T(8,128)S(1)}, f32[28,260]{1,0:T(8,128)}, u32[]{:S(2)}) copy-start(f32[28,260]{1,0:T(8,128)} %copy-done.28) | copy-start | bytes 87364
  166.7 13.0 %copy-start.39 = (f32[26,258]{1,0:T(8,128)S(1)}, f32[26,258]{1,0:T(8,128)}, u32[]{:S(2)}) copy-start(f32[26,258]{1,0:T(8,128)} %copy-done.38) | copy-start | bytes 80500
  166.7 14.1 %copy-start.37 = (f32[26,258]{1,0:T(8,128)S(1)}, f32[26,258]{1,0:T(8,128)}, u32[]{:S(2)}) copy-start(f32[26,258]{1,0:T(8,128)} %copy-done.36) | copy-start | bytes 80500
  167.7 14.0 %copy-start.30 = (f32[6,16,256]{2,1,0:T(8,128)}, f32[6,16,256]{2,1,0:T(8,128)S(1)}, u32[]{:S(2)}) copy-start(f32[6,16,256]{2,1,0:T(8,128)S(1)} %broadcast_multiply_fusion.7) | copy-start | bytes 294916
  200.4 12.8 %copy-start.3 = (f32[64,32,260]{2,0,1:T(8,128)S(1)}, f32[64,32,260]{2,0,1:T(8,128)}, u32[]{:S(2)}) copy-start(f32[64,32,260]{2,0,1:T(8,128)} %get-tuple-element.85) | copy-start | bytes 6389764
  213.3 3.2 copy-start.10
  213.3 6.8 %copy-start.5 = (f32[64,32,260]{2,0,1:T(8,128)S(1)}, f32[64,32,260]{2,0,1:T(8,128)}, u32[]{:S(2)}) copy-start(f32[64,32,260]{2,0,1:T(8,128)} %get-tuple-element.81) | copy-start | bytes 6389764
  216.5 3.6 copy-start.4
  218.3 2.7 copy-start.2
  218.3 2.7 copy-start.48
  218.3 2.7 copy-start.49
  218.3 2.7 copy-start.50
  227.6 3.3 copy-start.9
  247.7 2.9 copy-start.45
  247.7 2.9 copy-start.46
  247.7 2.9 copy-start.47
  258.5 2.5 copy-start.16
  260.3 2.7 copy-start.8
  260.3 2.7 copy-start.44
  278.8 2.5 copy-start.24
  278.8 2.5 copy-start.57
  278.9 2.5 copy-start.58
  305.3 2.7 copy-start.14
  305.3 2.7 copy-start.26
  305.3 2.7 copy-start.62
  305.4 2.7 copy-start.63
  305.4 2.7 copy-start.64
  322.9 2.7 copy-start.1
  325.7 4.4 copy-start.67
  325.7 4.4 copy-start.78
  325.7 4.4 copy-start.79
  330.1 152.1 %all-reduce.18.cloned.1.call-start = ((), (), s32[]{:S(2)}) async-start(), calls=%async_computation.1 | async-start | bytes 196608 | tf_op jit(solution)/shard_map/psum | solution.py:154
  464.5 17.7 %copy-start.31 = (f32[6,16,256]{2,1,0:T(8,128)S(1)}, f32[6,16,256]{2,1,0:T(8,128)}, u32[]{:S(2)}) copy-start(f32[6,16,256]{2,1,0:T(8,128)} %copy-done.30) | copy-start | bytes 294916
  465.1 36.6 %all-gather.2.cloned.1.call-start = ((), (), s32[]{:S(2)}) async-start(), calls=%async_computation.2 | async-start | bytes 9437184 | tf_op jit(solution)/shard_map/all_gather | solution.py:157
  (40 other events, 73.3 us)
Sparse Core Ops, SparseCore 0:
  330.2 104.0 all-reduce.15
  465.3 16.8 all-reduce.17
  483.7 17.9 all-gather.1
where the time goes:
time: 526 us; the launch traced here: 519 us
  waiting for transfers between devices  218 us (41%)
  other arithmetic  134 us (25%)
  local copies, waits for them, and re-layouts  80.2 us (15%)
  blocking collectives  45.1 us (9%)
  starting transfers between devices  15.3 us (3%)
  between operations  15.2 us (3%)
  matrix products  10.6 us (2%)
    ppermute x2, waiting for transfers between devices, padded_2(): lax.ppermute(lax.slice_in_dim(block, 0, width, axis=dim), axis, backward)  120 us
    psum x1, waiting for transfers between devices, local(): gram_sum, target = lax.psum((products, target_part), 'space')  62.5 us
    add x8, other arithmetic, tangent_core(): column_depth * zonal_new  49.2 us
    psum x1, blocking collectives, local(): gram_sum, target = lax.psum((products, target_part), 'space')  41.4 us
    unnamed x209, local copies, waits for them, and re-layouts  41.1 us
    squeeze x4, local copies, waits for them, and re-layouts, velocities(): north = inner(field[..., 3 * layer_index + 2, :, :])  24.4 us
    all_gather x1, waiting for transfers between devices, local(): shard_piece = lax.all_gather(columns_low, 'cols', axis=0, tiled=True)  18.1 us
    psum x1, waiting for transfers between devices, local(): increment_total = lax.psum(increment_terms, 'cols')  16 us
  transfers between devices with their start and end apart: 7, of which 5 were waited for; matrix products, arithmetic and copies ran while one was open for 5% of the time, Pallas kernels for 0%

commit v1 on v0

v1 whole, which is shorter than its diff:
```python
import functools

import jax
import jax.numpy as jnp
from jax import lax
from jax.experimental import pallas as pl
from jax.experimental.pallas import tpu as pltpu
from jax.sharding import PartitionSpec as P

ITERS = 4
DEPTH = 2 * ITERS
GROUP = 16

time_step = 0.5
gravity = 1.0
reduced_gravity = 0.125
coriolis = 0.3
friction = 0.05
layer_depths = (1.0, 2.0)

keep_part = 1.0 - time_step * friction
turn_part = time_step * coriolis
slope_part = 0.5 * time_step

f32 = jnp.float32
bf16 = jnp.bfloat16


def halo_rows():
    rows = []
    for layer in range(2):
        rows += [(3 * layer, d) for d in range(DEPTH, 0, -1)]
    for layer in range(2):
        rows += [(3 * layer + 1, d) for d in range(DEPTH - 1, 0, -1)]
        rows += [(3 * layer + 2, d) for d in range(DEPTH - 2, 0, -1)]
    return rows


def pack_kernel(*refs, tile_rows):
    cov_refs, up_ref, down_ref = refs[:-2], refs[-2], refs[-1]
    stride = 6 * tile_rows

    def row(field, r):
        return jnp.concatenate(
            [ref[pl.ds(field * tile_rows + r, GROUP, stride=stride), :] for ref in cov_refs],
            axis=1,
        )

    for i, (field, d) in enumerate(halo_rows()):
        for ref, r in ((up_ref, tile_rows - d), (down_ref, d - 1)):
            value = row(field, r)
            if d == DEPTH - 1 and field % 3 == 1:
                value = value + (turn_part / keep_part) * row(field + 1, r)
            ref[i] = value.astype(bf16)


def lane_steps(parts, lane):
    n = len(parts)
    right = [pltpu.roll(p, 1, 1) for p in parts]
    left = [pltpu.roll(p, 127, 1) for p in parts]
    out = []
    for i in range(n):
        before = jnp.where(lane == 0, right[i - 1] if i > 0 else 0.0, right[i])
        after = jnp.where(lane == 127, left[i + 1] if i < n - 1 else 0.0, left[i])
        out.append(after - before)
    return out


def station_hits(stations_ref, r, cells):
    position = lax.broadcasted_iota(jnp.int32, (cells, stations_ref.shape[1]), 0) + r * cells
    return position == stations_ref[...]


def mean_kernel(
    where_ref, mean_ref, mask_ref, stations_ref, observed_ref, weight_ref,
    wet_out, coef_out, final_out, innov_out, *, tile_rows, grid_rows,
):
    first_row = where_ref[0]
    ext, cells = mean_ref.shape[1:]
    wets = []
    for i in range(ext // 8):
        g = first_row - DEPTH + 8 * i
        inside = jnp.logical_and(g >= 0, g < grid_rows).astype(f32)
        start = pl.multiple_of(jnp.clip(g, 0, grid_rows - 8), 8)
        wets.append(mask_ref[pl.ds(start, 8), :].astype(f32) * inside)
    wet = jnp.concatenate(wets, axis=0)
    g_all = first_row - DEPTH + lax.broadcasted_iota(jnp.int32, (ext, cells), 0)
    keep = jnp.logical_and(g_all >= 0, g_all < grid_rows).astype(f32)
    lane_all = lax.broadcasted_iota(jnp.int32, (ext, cells), 1)

    def put(ref, index, value):
        rows = ref.shape[0] // (cells // 128)
        for c in range(cells // 128):
            ref[pl.ds(c * rows + index * ext, ext), :] = value[:, 128 * c : 128 * c + 128]

    put(wet_out, 0, wet * keep_part)
    put(wet_out, 1, wet * turn_part)
    put(wet_out, 2, wet * slope_part)

    def diff_rows(a):
        return 0.5 * (pltpu.roll(a, ext - 1, 0) - pltpu.roll(a, 1, 0))

    def diff_cols(a):
        after = jnp.where(lane_all == cells - 1, 0.0, pltpu.roll(a, cells - 1, 1))
        before = jnp.where(lane_all == 0, 0.0, pltpu.roll(a, 1, 1))
        return 0.5 * (after - before)

    state = [mean_ref[f] for f in range(6)]
    for t in range(ITERS):
        pressure_top = gravity * (state[0] + state[3])
        pressures = (pressure_top, pressure_top - reduced_gravity * state[0])
        fresh = []
        for layer in range(2):
            h, u, v = state[3 * layer : 3 * layer + 3]
            p = pressures[layer]
            u_new = wet * (u + time_step * (-diff_rows(p) + coriolis * v - friction * u))
            v_new = wet * (v + time_step * (-diff_cols(p) - coriolis * u - friction * v))
            depth = layer_depths[layer] + h
            h_new = h - time_step * (diff_rows(depth * u_new) + diff_cols(depth * v_new))
            for q, value in enumerate((depth, u_new, v_new)):
                put(coef_out, t * 6 + 3 * layer + q, slope_part * value)
            fresh += [h_new * keep, u_new, v_new]
        state = fresh
    for f in range(6):
        final_out[f] = state[f][DEPTH : DEPTH + tile_rows, :]
    surface = (state[0] + state[3])[DEPTH : DEPTH + tile_rows, :]
    n_stations = stations_ref.shape[1]
    sublane = lax.broadcasted_iota(jnp.int32, (8, n_stations), 0)
    picked = jnp.zeros((8, n_stations), f32)
    for r in range(tile_rows):
        hits = station_hits(stations_ref, r, cells).astype(f32)
        block = surface[r // 8 * 8 : r // 8 * 8 + 8, :]
        values = jnp.dot(block, hits, precision=lax.Precision.HIGHEST, preferred_element_type=f32)
        picked = picked + jnp.where(sublane == r % 8, values, 0.0)
    at_station = jnp.sum(picked, axis=0, keepdims=True)
    innovation = weight_ref[...] * (observed_ref[...] - at_station)
    innov_out[...] = jnp.where(sublane == 0, innovation, 0.0)


def window_kernel(
    where_ref, low_ref, high_ref, wet_ref, coef_ref, stations_ref, *refs,
    tile_rows, grid_rows,
):
    cov_refs, (pf_out, sensed_out, st) = refs[:-3], refs[-3:]
    first_row = where_ref[0]
    ext = tile_rows + 2 * DEPTH
    groups = len(cov_refs)
    cells = 128 * groups
    stride = 6 * tile_rows

    def fill(r, carry):
        for f in range(6):
            for c in range(groups):
                st[f, DEPTH + r, :, pl.ds(128 * c, 128)] = cov_refs[c][
                    pl.ds(f * tile_rows + r, GROUP, stride=stride), :
                ]
        return carry

    lax.fori_loop(0, tile_rows, fill, 0)
    for i, (field, d) in enumerate(halo_rows()):
        st[field, DEPTH - d] = low_ref[i].astype(f32)
        st[field, DEPTH + tile_rows + d - 1] = high_ref[i].astype(f32)
    for layer in range(2):
        for r in (1, ext - 2):
            st[3 * layer + 2, r] = jnp.zeros((GROUP, cells), f32)
    lane = lax.broadcasted_iota(jnp.int32, (8, 128), 1)

    for t in range(ITERS):
        shrink = 2 * t
        for kg in range(GROUP // 8):

            def load(field, r, kg=kg):
                return [
                    st[field, r, pl.ds(8 * kg, 8), pl.ds(128 * c, 128)] for c in range(groups)
                ]

            def store(field, r, parts, kg=kg):
                for c in range(groups):
                    st[field, r, pl.ds(8 * kg, 8), pl.ds(128 * c, 128)] = parts[c]

            def spread(ref, index, r):
                rows = ref.shape[0] // groups
                return [
                    ref[pl.ds(c * rows + index * ext + r, 8, stride=0), :] for c in range(groups)
                ]

            def pressures(h):
                top = [a + b for a, b in zip(h[0], h[1])]
                return [top, [p - reduced_gravity * a for p, a in zip(top, h[0])]]

            def body(r, carry, t=t, load=load, store=store):
                p_prev, p_here, h_here, flux_2, flux_1, part_1 = carry
                h_next = [load(0, r + 1), load(3, r + 1)]
                p_next = pressures(h_next)
                wet_a, wet_b, wet_c = (spread(wet_ref, q, r) for q in range(3))
                g = first_row - DEPTH + r - 1
                keep = jnp.where(jnp.logical_and(g >= 0, g < grid_rows), 1.0, 0.0).astype(f32)
                flux_0, part_0 = [], []
                for layer in range(2):
                    u, v = load(3 * layer + 1, r), load(3 * layer + 2, r)
                    depth, mu, mv = (
                        spread(coef_ref, t * 6 + 3 * layer + q, r) for q in range(3)
                    )
                    slope = lane_steps(p_here[layer], lane)
                    u_new, v_new, flux, cross = [], [], [], []
                    for c in range(groups):
                        u_c = (
                            wet_a[c] * u[c]
                            + wet_b[c] * v[c]
                            - wet_c[c] * (p_next[layer][c] - p_prev[layer][c])
                        )
                        v_c = wet_a[c] * v[c] - wet_b[c] * u[c] - wet_c[c] * slope[c]
                        h = h_here[layer][c]
                        u_new.append(u_c)
                        v_new.append(v_c)
                        flux.append(depth[c] * u_c + h * mu[c])
                        cross.append(depth[c] * v_c + h * mv[c])
                    store(3 * layer + 1, r, u_new)
                    store(3 * layer + 2, r, v_new)
                    cross = lane_steps(cross, lane)
                    part_0.append([h_here[layer][c] - cross[c] for c in range(groups)])
                    flux_0.append(flux)
                    store(
                        3 * layer,
                        r - 1,
                        [
                            keep * (part_1[layer][c] - (flux[c] - flux_2[layer][c]))
                            for c in range(groups)
                        ],
                    )
                return (p_here, p_next, h_next, flux_1, flux_0, part_0)

            h_a = [load(0, shrink), load(3, shrink)]
            h_b = [load(0, shrink + 1), load(3, shrink + 1)]
            nothing = [[a - a for a in h] for h in h_a]
            lax.fori_loop(
                shrink + 1,
                ext - shrink - 1,
                body,
                (pressures(h_a), pressures(h_b), h_b, nothing, nothing, nothing),
                unroll=2,
            )

    n_stations = stations_ref.shape[1]
    total = jnp.zeros((3 * GROUP, n_stations), f32)
    for r in range(tile_rows):
        for f in range(6):
            pf_out[f, r] = st[f, DEPTH + r].astype(bf16)
        surface = st[0, DEPTH + r] + st[3, DEPTH + r]
        high = surface.astype(bf16)
        rest = surface - high.astype(f32)
        middle = rest.astype(bf16)
        low = (rest - middle.astype(f32)).astype(bf16)
        pieces = jnp.concatenate([high, middle, low], axis=0)
        hits = station_hits(stations_ref, r, cells).astype(f32).astype(bf16)
        total = total + jnp.dot(pieces, hits, preferred_element_type=f32)
    sensed_out[...] = (
        total[:GROUP] + (total[GROUP : 2 * GROUP] + total[2 * GROUP : 3 * GROUP])
    )


def gram_kernel(where_ref, weight_ref, innov_ref, *refs, columns):
    sensed_refs, out_ref, both = refs[:-2], refs[-2], refs[-1]
    index = where_ref[1]
    count = len(sensed_refs)
    for d in range(count):
        start = pl.multiple_of(lax.rem(index + d, count) * columns, 8)
        both[pl.ds(start, columns), :] = sensed_refs[d][...] * weight_ref[...]
    total = count * columns
    both[pl.ds(total, 8), :] = innov_ref[...]
    out_ref[...] = lax.dot_general(
        both[...],
        both[pl.ds(0, total), :],
        (((1,), (1,)), ((), ())),
        precision=lax.Precision.HIGHEST,
        preferred_element_type=f32,
    )


def factor_kernel(where_ref, gram_ref, mix_out, scr, *, columns):
    index = where_ref[1]
    total = gram_ref.shape[1]
    blocks = total // 8
    lane = lax.broadcasted_iota(jnp.int32, (8, total), 1)
    sub = lax.broadcasted_iota(jnp.int32, (8, total), 0)
    eye = [(lane == sub + 8 * b).astype(f32) for b in range(blocks)]
    m = [gram_ref[pl.ds(8 * b, 8), :] + eye[b] for b in range(blocks)]
    w = list(eye)
    pivots = [jnp.ones((8, total), f32) for _ in range(blocks)]
    for j in range(total):
        b, i = j // 8, j % 8
        heads = {q: jnp.broadcast_to(m[q][:, j : j + 1], (8, total)) for q in range(b, blocks)}
        pivot = jnp.broadcast_to(heads[b][i : i + 1, :], (8, total))
        pivots[b] = jnp.where(sub == i, pivot, pivots[b])
        inverse = 1.0 / pivot
        row_m = jnp.broadcast_to(m[b][i : i + 1, :], (8, total)) * inverse
        row_w = jnp.broadcast_to(w[b][i : i + 1, :], (8, total)) * inverse
        for q in range(b, blocks):
            head = jnp.where(sub > i, heads[q], 0.0) if q == b else heads[q]
            m[q] = m[q] - head * row_m
            w[q] = w[q] - head * row_w
    target = gram_ref[pl.ds(total, 1), :]
    weights = jnp.zeros((1, total), f32)
    for b in range(blocks):
        inv = w[b] / jnp.sqrt(pivots[b])
        scr[pl.ds(8 * b, 8), :] = inv
        half = jnp.sum(inv * target, axis=1, keepdims=True)
        weights = weights + jnp.sum(inv * half, axis=0, keepdims=True)
    shift = lax.rem(total - index * columns, total)
    mine = scr[pl.ds(pl.multiple_of(index * columns, 8), columns), :]
    mix_out[pl.ds(0, columns), :] = pltpu.roll(mine, shift, 1).astype(bf16)
    weights = pltpu.roll(jnp.broadcast_to(weights, (8, total)), shift, 1)
    high = weights.astype(bf16)
    low = (weights - high.astype(f32)).astype(bf16)
    pad = jnp.zeros((8, total), f32)
    rows = jnp.where(sub == 0, high.astype(f32), jnp.where(sub == 1, low.astype(f32), 0.0))
    mix_out[pl.ds(columns, 16), :] = jnp.concatenate([rows, pad], axis=0).astype(bf16)


def mix_kernel(where_ref, mix_ref, mean_ref, *refs, columns):
    piece_refs, cov_out, mean_out, scr = refs[:-3], refs[-3], refs[-2], refs[-1]
    tile_rows, cells = mean_ref.shape[1:]
    piece = mean_out.shape[2]
    group = pl.program_id(1)
    mix = mix_ref[...]
    for r in range(tile_rows):
        stack = jnp.concatenate([ref[0, r] for ref in piece_refs], axis=0)
        result = jnp.dot(mix, stack, preferred_element_type=f32)
        cov_out[:, 0, r, :] = result[:columns]
        scr[group, pl.ds(r, 1), :] = (
            result[columns : columns + 1] + result[columns + 1 : columns + 2]
        )

    @pl.when(group == pl.num_programs(1) - 1)
    def _():
        change = jnp.concatenate([scr[c] for c in range(cells // 128)], axis=1)
        whole = mean_ref[0] + change
        shift = lax.rem(cells - where_ref[1] * piece, cells)
        mean_out[0] = pltpu.roll(whole, shift, 1)[:, :piece]


def spread_sum(value, axis):
    count = lax.axis_size(axis)
    if count & (count - 1):
        return lax.psum(value, axis)
    step = 1
    while step < count:
        value = value + lax.ppermute(value, axis, [(i, i ^ step) for i in range(count)])
        step *= 2
    return value


def shifted(value, axis):
    count = lax.axis_size(axis)
    return [value] + [
        lax.ppermute(value, axis, [((i + d) % count, i) for i in range(count)])
        for d in range(1, count)
    ]


def whole_spec(shape):
    return pl.BlockSpec(shape, lambda *_: (0,) * len(shape))


def local(mean_state, covariance, land_mask, stations, observed, obs_weight):
    columns, _, tile_rows, cells = covariance.shape
    piece = mean_state.shape[2]
    n_space = lax.axis_size("space")
    n_cols = lax.axis_size("cols")
    total = columns * n_cols
    grid_rows = tile_rows * n_space
    ext = tile_rows + 2 * DEPTH
    n_stations = stations.shape[0]
    chunks = columns // GROUP
    n_halo = len(halo_rows())
    groups = cells // 128
    space_index = lax.axis_index("space")
    column_index = lax.axis_index("cols")
    first_row = space_index * tile_rows
    where = jnp.stack([first_row, column_index]).astype(jnp.int32)
    up = [(i, i + 1) for i in range(n_space - 1)]
    down = [(i + 1, i) for i in range(n_space - 1)]
    smem = pl.BlockSpec(memory_space=pltpu.SMEM)

    mean_low = lax.ppermute(mean_state[:, tile_rows - DEPTH :, :], "space", up)
    mean_high = lax.ppermute(mean_state[:, :DEPTH, :], "space", down)
    mean_ext = jnp.concatenate([mean_low, mean_state, mean_high], axis=1)
    mean_ext = lax.all_gather(mean_ext, "cols", axis=2, tiled=True)

    flat = covariance.reshape(columns * 6 * tile_rows, cells)
    span = GROUP * 6 * tile_rows


    def cov_specs(c):
        return [pl.BlockSpec((span, 128), lambda i, g=g: (c, g)) for g in range(groups)]

    lows, highs = [], []
    for c in range(chunks):
        halo_shape = jax.ShapeDtypeStruct((n_halo, GROUP, cells), bf16)
        going_up, going_down = pl.pallas_call(
            functools.partial(pack_kernel, tile_rows=tile_rows),
            grid=(1,),
            in_specs=cov_specs(c),
            out_specs=[whole_spec((n_halo, GROUP, cells))] * 2,
            out_shape=[halo_shape, halo_shape],
            name=f"pack_{c}",
        )(*[flat] * groups)
        lows.append(lax.ppermute(going_up, "space", up))
        highs.append(lax.ppermute(going_down, "space", down))

    station_row = (stations - first_row * cells).astype(jnp.int32)[None, :]
    weight_row = obs_weight[None, :]
    wet, coef, mean_final, innovation = pl.pallas_call(
        functools.partial(mean_kernel, tile_rows=tile_rows, grid_rows=grid_rows),
        in_specs=[smem] + [pl.BlockSpec(memory_space=pltpu.VMEM)] * 5,
        out_specs=[pl.BlockSpec(memory_space=pltpu.VMEM)] * 4,
        out_shape=[
            jax.ShapeDtypeStruct((groups * 3 * ext, 128), f32),
            jax.ShapeDtypeStruct((groups * ITERS * 6 * ext, 128), f32),
            jax.ShapeDtypeStruct((6, tile_rows, cells), f32),
            jax.ShapeDtypeStruct((8, n_stations), f32),
        ],
        name="mean_window",
    )(where, mean_ext, land_mask, station_row, observed[None, :], weight_row)

    forecasts, sensed = [], []
    for c in range(chunks):
        pf, s = pl.pallas_call(
            functools.partial(window_kernel, tile_rows=tile_rows, grid_rows=grid_rows),
            grid=(1,),
            in_specs=[
                smem,
                whole_spec((n_halo, GROUP, cells)),
                whole_spec((n_halo, GROUP, cells)),
                whole_spec((groups * 3 * ext, 128)),
                whole_spec((groups * ITERS * 6 * ext, 128)),
                whole_spec((1, n_stations)),
            ]
            + cov_specs(c),
            out_specs=[
                whole_spec((6, tile_rows, GROUP, cells)),
                whole_spec((GROUP, n_stations)),
            ],
            out_shape=[
                jax.ShapeDtypeStruct((6, tile_rows, GROUP, cells), bf16),
                jax.ShapeDtypeStruct((GROUP, n_stations), f32),
            ],
            scratch_shapes=[pltpu.VMEM((6, ext, GROUP, cells), f32)],
            name=f"window_{c}",
        )(where, lows[c], highs[c], wet, coef, station_row, *[flat] * groups)
        forecasts.append(shifted(pf, "cols"))
        sensed.append(s)

    sensed_all = shifted(jnp.concatenate(sensed, axis=0), "cols")
    gram = pl.pallas_call(
        functools.partial(gram_kernel, columns=columns),
        in_specs=[smem] + [pl.BlockSpec(memory_space=pltpu.VMEM)] * (2 + n_cols),
        out_specs=pl.BlockSpec(memory_space=pltpu.VMEM),
        out_shape=jax.ShapeDtypeStruct((total + 8, total), f32),
        scratch_shapes=[pltpu.VMEM((total + 8, n_stations), f32)],
        name="gram",
    )(where, weight_row, innovation, *sensed_all)
    gram = spread_sum(gram, "space")
    mix = pl.pallas_call(
        functools.partial(factor_kernel, columns=columns),
        in_specs=[smem, pl.BlockSpec(memory_space=pltpu.VMEM)],
        out_specs=pl.BlockSpec(memory_space=pltpu.VMEM),
        out_shape=jax.ShapeDtypeStruct((columns + 16, total), bf16),
        scratch_shapes=[pltpu.VMEM((total, total), f32)],
        name="factor",
    )(where, gram)

    pieces = [forecasts[c][d] for d in range(n_cols) for c in range(chunks)]
    field_spec = pl.BlockSpec((1, tile_rows, GROUP, 128), lambda f, g: (f, 0, 0, g))
    updated, mean_out = pl.pallas_call(
        functools.partial(mix_kernel, columns=columns),
        grid=(6, groups),
        in_specs=[
            smem,
            whole_spec((columns + 16, total)),
            pl.BlockSpec((1, tile_rows, cells), lambda f, g: (f, 0, 0)),
        ]
        + [field_spec] * len(pieces),
        out_specs=[
            pl.BlockSpec((columns, 1, tile_rows, 128), lambda f, g: (0, f, 0, g)),
            pl.BlockSpec((1, tile_rows, piece), lambda f, g: (f, 0, 0)),
        ],
        out_shape=[
            jax.ShapeDtypeStruct((columns, 6, tile_rows, cells), f32),
            jax.ShapeDtypeStruct((6, tile_rows, piece), f32),
        ],
        scratch_shapes=[pltpu.VMEM((groups, tile_rows, 128), f32)],
        name="mix",
    )(where, mix, mean_final, *pieces)
    return (mean_out, updated)


def solution(mesh):
    return jax.shard_map(
        local,
        mesh=mesh,
        in_specs=(
            P(None, "space", "cols"),
            P("cols", None, "space", None),
            P(),
            P("space"),
            P("space"),
            P("space"),
        ),
        out_specs=(P(None, "space", "cols"), P("cols", None, "space", None)),
        check_vma=False,
    )
```

time: 526 us -> 225 us (0.43); the launches traced: 519 us -> 224 us
  waiting for transfers between devices: 218 us -> 13.1 us
  Pallas kernels: 0 us -> 154 us
  other arithmetic: 134 us -> 2.67 us
  local copies, waits for them, and re-layouts: 80.2 us -> 6.21 us
  blocking collectives: 45.1 us -> 2.26 us
  starting transfers between devices: 15.3 us -> 44 us
  between operations: 15.2 us -> 1.1 us
  matrix products: 10.6 us -> 0 us
    pallas_call x0 -> x12, Pallas kernels: none -> 154 us  [the longest x4 106 us: local(): pl.pallas_call(functools.partial(window_kernel, tile_rows=tile_rows, grid...]
    ppermute x4 -> x19, waiting for transfers between devices: 121 us -> 13.1 us  [the longest x4 9.78 us: spread_sum(): lax.ppermute(value, axis, [(i, i ^ step) for i in range(count)])]
    psum x2 -> x0, waiting for transfers between devices: 78.6 us -> none  [the longest x1 62.5 us: local(): gram_sum, target = lax.psum((products, target_part), 'space')]
    add x15 -> x4, other arithmetic: 52 us -> 1.56 us  [spread_sum(): value + lax.ppermute(value, axis, [(i, i ^ step) for i in range(count)])]
    psum x1 -> x0, blocking collectives: 41.4 us -> none  [local(): gram_sum, target = lax.psum((products, target_part), 'space')]
    unnamed x209 -> x43, local copies, waits for them, and re-layouts: 41.1 us -> 5.51 us
    ppermute x4 -> x19, starting transfers between devices: 15 us -> 44 us  [the longest x4 18.5 us: local(): lows.append(lax.ppermute(going_up, 'space', up))]
    squeeze x8 -> x0, local copies, waits for them, and re-layouts: 24.7 us -> none  [the longest x4 24.4 us: velocities(): north = inner(field[..., 3 * layer_index + 2, :, :])]
  transfers between devices with their start and end apart: 7 -> 19, of which waited for: 5 -> 6; matrix products, arithmetic and copies ran while one was open for 5% -> 2% of each run, Pallas kernels for 0% -> 62%
where the time goes in v1:
time: 225 us; the launch traced here: 224 us
  Pallas kernels  154 us (68%)
  starting transfers between devices  44 us (20%)
  waiting for transfers between devices  13.1 us (6%)
  local copies, waits for them, and re-layouts  6.21 us (3%)
  other arithmetic  2.67 us (1%)
  blocking collectives  2.26 us (1%)
    pallas_call x4, Pallas kernels, local(): pl.pallas_call(functools.partial(window_kernel, tile_rows=tile_rows, grid...  106 us
    pallas_call x1, Pallas kernels, local(): pl.pallas_call(functools.partial(factor_kernel, columns=columns), in_spec...  18.8 us
    ppermute x4, starting transfers between devices, local(): lows.append(lax.ppermute(going_up, 'space', up))  18.5 us
    ppermute x4, starting transfers between devices, spread_sum(): lax.ppermute(value, axis, [(i, i ^ step) for i in range(count)])  13.5 us
    pallas_call x4, Pallas kernels, local(): pl.pallas_call(functools.partial(pack_kernel, tile_rows=tile_rows), grid=...  12.1 us
    pallas_call x1, Pallas kernels, local(): pl.pallas_call(functools.partial(mix_kernel, columns=columns), grid=(6, g...  11.9 us
    ppermute x4, waiting for transfers between devices, spread_sum(): lax.ppermute(value, axis, [(i, i ^ step) for i in range(count)])  9.78 us
    unnamed x43, local copies, waits for them, and re-layouts  5.51 us
  transfers between devices with their start and end apart: 19, of which 6 were waited for; matrix products, arithmetic and copies ran while one was open for 2% of the time, Pallas kernels for 62%

profile of v1, /device:TPU:0, one launch (start us, length us, event | category | flops | bytes accessed | tf_op | source)
XLA Modules:
  0.0 223.8 jit_solution(7090275872022028469)
XLA Ops:
  0.6 3.0 %pack_1.1 = (bf16[42,16,256]{2,1,0:T(8,128)(2,1)}, bf16[42,16,256]{2,1,0:T(8,128)(2,1)}) custom-call(f32[6144,256]{1,0:T(8,128)} %bitcast.7, f32[6144,256]{1,0:T(8,128)} %bitcast.8), custom_call_target="tpu_custom_call" | custom-call | tf_op jit(solution)/shard_map/pack_1/pallas_call | solution.py:400
  3.6 4.9 %collective-permute-start.4 = (bf16[42,16,256]{2,1,0:T(8,128)(2,1)}, bf16[42,16,256]{2,1,0:T(8,128)(2,1)S(1)}, u32[]{:S(2)}, u32[]{:S(2)}) collective-permute-start(bf16[42,16,256]{2,1,0:T(8,128)(2,1)} %get-tuple-element.30), channel_id=1, source_target_pairs={{0,1},{1,2},{2,3},{3,4},{4,5},{5,6},{6,7},{7,8},{8,9},{9,10},{10,1... | collective-permute-start | bytes 1032200 | tf_op jit(solution)/shard_map/ppermute | solution.py:408
  8.5 1.4 collective-permute-start.5
  10.0 3.0 %pack_0.1 = (bf16[42,16,256]{2,1,0:T(8,128)(2,1)}, bf16[42,16,256]{2,1,0:T(8,128)(2,1)}) custom-call(f32[6144,256]{1,0:T(8,128)} %bitcast.9, f32[6144,256]{1,0:T(8,128)} %bitcast.10), custom_call_target="tpu_custom_call" | custom-call | tf_op jit(solution)/shard_map/pack_0/pallas_call | solution.py:400
  13.0 4.6 %collective-permute-start.2 = (bf16[42,16,256]{2,1,0:T(8,128)(2,1)}, bf16[42,16,256]{2,1,0:T(8,128)(2,1)S(1)}, u32[]{:S(2)}, u32[]{:S(2)}) collective-permute-start(bf16[42,16,256]{2,1,0:T(8,128)(2,1)} %get-tuple-element.25), channel_id=1, source_target_pairs={{0,1},{1,2},{2,3},{3,4},{4,5},{5,6},{6,7},{7,8},{8,9},{9,10},{10,1... | collective-permute-start | bytes 1032200 | tf_op jit(solution)/shard_map/ppermute | solution.py:408
  17.6 4.3 %collective-permute-start = (f32[6,8,128]{2,1,0:T(8,128)S(1)}, f32[6,8,128]{2,1,0:T(8,128)S(1)}, u32[]{:S(2)}, u32[]{:S(2)}) collective-permute-start(f32[6,8,128]{2,1,0:T(8,128)S(1)} %get-tuple-element.46), channel_id=1, source_target_pairs={{0,1},{1,2},{2,3},{3,4},{4,5},{5,6},{6,7},{7,8},{8,9},{9,10},{10,1... | collective-permute-start | bytes 73736 | tf_op jit(solution)/shard_map/ppermute | solution.py:385
  21.8 1.3 collective-permute-start.1
  23.1 0.6 pad_add_fusion.where_ref
  23.8 3.0 %pack_3.1 = (bf16[42,16,256]{2,1,0:T(8,128)(2,1)}, bf16[42,16,256]{2,1,0:T(8,128)(2,1)}) custom-call(f32[6144,256]{1,0:T(8,128)} %bitcast.11, f32[6144,256]{1,0:T(8,128)} %bitcast.12), custom_call_target="tpu_custom_call" | custom-call | tf_op jit(solution)/shard_map/pack_3/pallas_call | solution.py:400
  26.8 3.1 %pack_2.1 = (bf16[42,16,256]{2,1,0:T(8,128)(2,1)}, bf16[42,16,256]{2,1,0:T(8,128)(2,1)}) custom-call(f32[6144,256]{1,0:T(8,128)} %bitcast.13, f32[6144,256]{1,0:T(8,128)} %bitcast.14), custom_call_target="tpu_custom_call" | custom-call | tf_op jit(solution)/shard_map/pack_2/pallas_call | solution.py:400
  29.8 2.0 collective-permute-done
  31.8 4.4 %collective-permute-start.8 = (bf16[42,16,256]{2,1,0:T(8,128)(2,1)}, bf16[42,16,256]{2,1,0:T(8,128)(2,1)S(1)}, u32[]{:S(2)}, u32[]{:S(2)}) collective-permute-start(bf16[42,16,256]{2,1,0:T(8,128)(2,1)} %get-tuple-element.36), channel_id=1, source_target_pairs={{0,1},{1,2},{2,3},{3,4},{4,5},{5,6},{6,7},{7,8},{8,9},{9,10},{10,1... | collective-permute-start | bytes 1032200 | tf_op jit(solution)/shard_map/ppermute | solution.py:408
  36.2 1.3 collective-permute-start.9
  37.6 4.7 %collective-permute-start.6 = (bf16[42,16,256]{2,1,0:T(8,128)(2,1)}, bf16[42,16,256]{2,1,0:T(8,128)(2,1)S(1)}, u32[]{:S(2)}, u32[]{:S(2)}) collective-permute-start(bf16[42,16,256]{2,1,0:T(8,128)(2,1)} %get-tuple-element.33), channel_id=1, source_target_pairs={{0,1},{1,2},{2,3},{3,4},{4,5},{5,6},{6,7},{7,8},{8,9},{9,10},{10,1... | collective-permute-start | bytes 1032200 | tf_op jit(solution)/shard_map/ppermute | solution.py:408
  42.2 1.3 collective-permute-start.7
  43.6 1.3 collective-permute-start.3
  44.9 0.5 subtract_bitcast_fusion.stations_ref
  45.4 2.3 %all_gather.3.mean_ref = f32[6,32,256]{2,1,0:T(8,128)} all-gather(f32[6,32,128]{2,1,0:T(8,128)S(1)} %pad_maximum_fusion), channel_id=1, replica_groups=mesh['cols'=2,'space'=16] {'cols'}, dimensions={2}, use_global_device_ids=true | all-gather | bytes 294912 | tf_op jit(solution)/shard_map/all_gather | solution.py:388
  47.6 3.5 %mean_window.1 = (f32[192,128]{1,0:T(8,128)}, f32[1536,128]{1,0:T(8,128)}, f32[6,16,256]{2,1,0:T(8,128)}, f32[8,128]{1,0:T(8,128)}) custom-call(s32[2]{0:T(128)} %pad_add_fusion.where_ref, f32[6,32,256]{2,1,0:T(8,128)} %all_gather.3.mean_ref, s32[256,256]{1,0:T(8,128)} %mask_ref.1, s32[1,128]{1,0:T(1,128)} %subtract_bitcast_fusion.stations_ref, ...), custom_call_target="tpu_custom_call" | custom-call | tf_op jit(solution)/shard_map/mean_window/pallas_call | solution.py:413
  51.1 26.6 %window_1.1 = (bf16[6,16,16,256]{3,2,1,0:T(8,128)(2,1)}, f32[16,128]{1,0:T(8,128)}) custom-call(s32[2]{0:T(128)} %pad_add_fusion.where_ref, bf16[42,16,256]{2,1,0:T(8,128)(2,1)} %copy-done.5, bf16[42,16,256]{2,1,0:T(8,128)(2,1)} %copy-done.6, f32[192,128]{1,0:T(8,128)} %get-tuple-element.27.wet_ref, f32[1536,128]{1,0:T(8,128)} %get-tuple-element.28.coef_ref, ...), custom_call_target="tpu_custom_call" | custom-call | tf_op jit(solution)/shard_map/window_1/pallas_call | solution.py:428
  78.0 0.5 copy-done.11
  78.5 26.6 %window_0.1 = (bf16[6,16,16,256]{3,2,1,0:T(8,128)(2,1)}, f32[16,128]{1,0:T(8,128)}) custom-call(s32[2]{0:T(128)} %pad_add_fusion.where_ref, bf16[42,16,256]{2,1,0:T(8,128)(2,1)} %copy-done.4, bf16[42,16,256]{2,1,0:T(8,128)(2,1)} %copy-done.11, f32[192,128]{1,0:T(8,128)} %get-tuple-element.27.wet_ref, f32[1536,128]{1,0:T(8,128)} %get-tuple-element.28.coef_ref, ...), custom_call_target="tpu_custom_call" | custom-call | tf_op jit(solution)/shard_map/window_0/pallas_call | solution.py:428
  105.4 0.5 copy-done.9
  105.9 0.7 copy-done.10
  106.6 26.6 %window_2.1 = (bf16[6,16,16,256]{3,2,1,0:T(8,128)(2,1)}, f32[16,128]{1,0:T(8,128)}) custom-call(s32[2]{0:T(128)} %pad_add_fusion.where_ref, bf16[42,16,256]{2,1,0:T(8,128)(2,1)} %copy-done.9, bf16[42,16,256]{2,1,0:T(8,128)(2,1)} %copy-done.10, f32[192,128]{1,0:T(8,128)} %get-tuple-element.27.wet_ref, f32[1536,128]{1,0:T(8,128)} %get-tuple-element.28.coef_ref, ...), custom_call_target="tpu_custom_call" | custom-call | tf_op jit(solution)/shard_map/window_2/pallas_call | solution.py:428
  133.5 0.7 copy-done.7
  134.2 0.7 copy-done.8
  135.0 26.6 %window_3.1 = (bf16[6,16,16,256]{3,2,1,0:T(8,128)(2,1)}, f32[16,128]{1,0:T(8,128)}) custom-call(s32[2]{0:T(128)} %pad_add_fusion.where_ref, bf16[42,16,256]{2,1,0:T(8,128)(2,1)} %copy-done.7, bf16[42,16,256]{2,1,0:T(8,128)(2,1)} %copy-done.8, f32[192,128]{1,0:T(8,128)} %get-tuple-element.27.wet_ref, f32[1536,128]{1,0:T(8,128)} %get-tuple-element.28.coef_ref, ...), custom_call_target="tpu_custom_call" | custom-call | tf_op jit(solution)/shard_map/window_3/pallas_call | solution.py:428
  161.6 0.4 collective-permute-start.18
  162.0 0.7 constant_dynamic-update-slice_fusion.refs_0_
  162.8 1.3 collective-permute-done.10.refs_1_
  164.1 0.6 copy-done.14
  164.7 1.7 gram.1
  166.4 4.2 %collective-permute-start.11 = (f32[136,128]{1,0:T(8,128)}, f32[136,128]{1,0:T(8,128)S(1)}, u32[]{:S(2)}, u32[]{:S(2)}) collective-permute-start(f32[136,128]{1,0:T(8,128)} %gram.1), channel_id=1, source_target_pairs={{0,1},{1,0},{2,3},{3,2},{4,5},{5,4},{6,7},{7,6},{8,9},{9,8},{10,11... | collective-permute-start | bytes 208904 | tf_op jit(solution)/shard_map/ppermute | solution.py:348
  170.6 2.9 %collective-permute-done.11 = f32[136,128]{1,0:T(8,128)S(1)} collective-permute-done((f32[136,128]{1,0:T(8,128)}, f32[136,128]{1,0:T(8,128)S(1)}, u32[]{:S(2)}, u32[]{:S(2)}) %collective-permute-start.11) | collective-permute-done | bytes 69664 | tf_op jit(solution)/shard_map/ppermute | solution.py:348
  173.5 0.9 add.12
  174.4 3.5 %collective-permute-start.12 = (f32[136,128]{1,0:T(8,128)S(1)}, f32[136,128]{1,0:T(8,128)S(1)}, u32[]{:S(2)}, u32[]{:S(2)}) collective-permute-start(f32[136,128]{1,0:T(8,128)S(1)} %add.12), channel_id=1, source_target_pairs={{0,2},{1,3},{2,0},{3,1},{4,6},{5,7},{6,4},{7,5},{8,10},{9,11},{10,... | collective-permute-start | bytes 208904 | tf_op jit(solution)/shard_map/ppermute | solution.py:348
  177.9 2.3 %collective-permute-done.12 = f32[136,128]{1,0:T(8,128)S(1)} collective-permute-done((f32[136,128]{1,0:T(8,128)S(1)}, f32[136,128]{1,0:T(8,128)S(1)}, u32[]{:S(2)}, u32[]{:S(2)}) %collective-permute-start.12) | collective-permute-done | bytes 69664 | tf_op jit(solution)/shard_map/ppermute | solution.py:348
  180.2 2.7 %collective-permute-start.13 = (f32[136,128]{1,0:T(8,128)S(1)}, f32[136,128]{1,0:T(8,128)S(1)}, u32[]{:S(2)}, u32[]{:S(2)}) collective-permute-start(f32[136,128]{1,0:T(8,128)S(1)} %add.13), channel_id=1, source_target_pairs={{0,4},{1,5},{2,6},{3,7},{4,0},{5,1},{6,2},{7,3},{8,12},{9,13},{10,... | collective-permute-start | bytes 208904 | tf_op jit(solution)/shard_map/ppermute | solution.py:348
  182.9 2.3 %collective-permute-done.13 = f32[136,128]{1,0:T(8,128)S(1)} collective-permute-done((f32[136,128]{1,0:T(8,128)S(1)}, f32[136,128]{1,0:T(8,128)S(1)}, u32[]{:S(2)}, u32[]{:S(2)}) %collective-permute-start.13) | collective-permute-done | bytes 69664 | tf_op jit(solution)/shard_map/ppermute | solution.py:348
  185.2 3.1 %collective-permute-start.14 = (f32[136,128]{1,0:T(8,128)S(1)}, f32[136,128]{1,0:T(8,128)S(1)}, u32[]{:S(2)}, u32[]{:S(2)}) collective-permute-start(f32[136,128]{1,0:T(8,128)S(1)} %add.14), channel_id=1, source_target_pairs={{0,8},{1,9},{2,10},{3,11},{4,12},{5,13},{6,14},{7,15},{8,0},{9,1},... | collective-permute-start | bytes 208904 | tf_op jit(solution)/shard_map/ppermute | solution.py:348
  188.3 2.3 %collective-permute-done.14 = f32[136,128]{1,0:T(8,128)S(1)} collective-permute-done((f32[136,128]{1,0:T(8,128)S(1)}, f32[136,128]{1,0:T(8,128)S(1)}, u32[]{:S(2)}, u32[]{:S(2)}) %collective-permute-start.14) | collective-permute-done | bytes 69664 | tf_op jit(solution)/shard_map/ppermute | solution.py:348
  190.6 0.6 add.15.gram_ref
  191.3 18.8 %factor.1.mix_ref = bf16[80,128]{1,0:T(8,128)(2,1)} custom-call(s32[2]{0:T(128)} %pad_add_fusion.where_ref, f32[136,128]{1,0:T(8,128)} %add.15.gram_ref), custom_call_target="tpu_custom_call" | custom-call | tf_op jit(solution)/shard_map/factor/pallas_call | solution.py:464
  210.1 0.8 copy-done
  211.0 0.3 copy-done.1
  211.2 0.3 copy-done.2
  211.7 11.9 %mix.1 = (f32[64,6,16,256]{3,2,1,0:T(8,128)}, f32[6,16,128]{2,1,0:T(8,128)}) custom-call(s32[2]{0:T(128)} %pad_add_fusion.where_ref, bf16[80,128]{1,0:T(8,128)(2,1)} %factor.1.mix_ref, f32[6,16,256]{2,1,0:T(8,128)} %get-tuple-element.39.mean_ref, bf16[6,16,16,256]{3,2,1,0:T(8,128)(2,1)} %get-tuple-element.40.refs_0_, ...), custom_call_target="tpu_custom_call" | custom-call | tf_op jit(solution)/shard_map/mix/pallas_call | solution.py:475
  (55 shorter events, 1.2 us)
Async XLA Ops:
  3.6 33.9 %collective-permute-start.4 = (bf16[42,16,256]{2,1,0:T(8,128)(2,1)}, bf16[42,16,256]{2,1,0:T(8,128)(2,1)S(1)}, u32[]{:S(2)}, u32[]{:S(2)}) collective-permute-start(bf16[42,16,256]{2,1,0:T(8,128)(2,1)} %get-tuple-element.30), channel_id=1, source_target_pairs={{0,1},{1,2},{2,3},{3,4},{4,5},{5,6},{6,7},{7,8},{8,9},{9,10},{10,1... | collective-permute-start | bytes 1032200 | tf_op jit(solution)/shard_map/ppermute | solution.py:408
  8.5 9.0 %copy-start.12 = (f32[6,16,128]{2,1,0:T(8,128)S(1)}, f32[6,16,128]{2,1,0:T(8,128)}, u32[]{:S(2)}) copy-start(f32[6,16,128]{2,1,0:T(8,128)} %param.6) | copy-start | bytes 147460
  8.5 33.7 %collective-permute-start.5 = (bf16[42,16,256]{2,1,0:T(8,128)(2,1)}, bf16[42,16,256]{2,1,0:T(8,128)(2,1)S(1)}, u32[]{:S(2)}, u32[]{:S(2)}) collective-permute-start(bf16[42,16,256]{2,1,0:T(8,128)(2,1)} %get-tuple-element.31), channel_id=1, source_target_pairs={{1,0},{2,1},{3,2},{4,3},{5,4},{6,5},{7,6},{8,7},{9,8},{10,9},{11,1... | collective-permute-start | bytes 1032200 | tf_op jit(solution)/shard_map/ppermute | solution.py:409
  13.0 30.6 %collective-permute-start.2 = (bf16[42,16,256]{2,1,0:T(8,128)(2,1)}, bf16[42,16,256]{2,1,0:T(8,128)(2,1)S(1)}, u32[]{:S(2)}, u32[]{:S(2)}) collective-permute-start(bf16[42,16,256]{2,1,0:T(8,128)(2,1)} %get-tuple-element.25), channel_id=1, source_target_pairs={{0,1},{1,2},{2,3},{3,4},{4,5},{5,6},{6,7},{7,8},{8,9},{9,10},{10,1... | collective-permute-start | bytes 1032200 | tf_op jit(solution)/shard_map/ppermute | solution.py:408
  17.6 14.3 %collective-permute-start = (f32[6,8,128]{2,1,0:T(8,128)S(1)}, f32[6,8,128]{2,1,0:T(8,128)S(1)}, u32[]{:S(2)}, u32[]{:S(2)}) collective-permute-start(f32[6,8,128]{2,1,0:T(8,128)S(1)} %get-tuple-element.46), channel_id=1, source_target_pairs={{0,1},{1,2},{2,3},{3,4},{4,5},{5,6},{6,7},{7,8},{8,9},{9,10},{10,1... | collective-permute-start | bytes 73736 | tf_op jit(solution)/shard_map/ppermute | solution.py:385
  21.8 14.4 %collective-permute-start.1 = (f32[6,8,128]{2,1,0:T(8,128)S(1)}, f32[6,8,128]{2,1,0:T(8,128)S(1)}, u32[]{:S(2)}, u32[]{:S(2)}) collective-permute-start(f32[6,8,128]{2,1,0:T(8,128)S(1)} %get-tuple-element.47), channel_id=1, source_target_pairs={{1,0},{2,1},{3,2},{4,3},{5,4},{6,5},{7,6},{8,7},{9,8},{10,9},{11,1... | collective-permute-start | bytes 73736 | tf_op jit(solution)/shard_map/ppermute | solution.py:386
  26.8 9.5 %copy-start.18 = (bf16[42,16,256]{2,1,0:T(8,128)(2,1)S(1)}, bf16[42,16,256]{2,1,0:T(8,128)(2,1)}, u32[]{:S(2)}) copy-start(bf16[42,16,256]{2,1,0:T(8,128)(2,1)} %get-tuple-element.37) | copy-start | bytes 1032196
  26.8 18.1 %copy-start.19 = (s32[128]{0:T(128)S(1)}, s32[128]{0:T(128)}, u32[]{:S(2)}) copy-start(s32[128]{0:T(128)} %param.9) | copy-start | bytes 1540
  31.8 101.7 %collective-permute-start.8 = (bf16[42,16,256]{2,1,0:T(8,128)(2,1)}, bf16[42,16,256]{2,1,0:T(8,128)(2,1)S(1)}, u32[]{:S(2)}, u32[]{:S(2)}) collective-permute-start(bf16[42,16,256]{2,1,0:T(8,128)(2,1)} %get-tuple-element.36), channel_id=1, source_target_pairs={{0,1},{1,2},{2,3},{3,4},{4,5},{5,6},{6,7},{7,8},{8,9},{9,10},{10,1... | collective-permute-start | bytes 1032200 | tf_op jit(solution)/shard_map/ppermute | solution.py:408
  36.2 97.3 %collective-permute-start.9 = (bf16[42,16,256]{2,1,0:T(8,128)(2,1)S(1)}, bf16[42,16,256]{2,1,0:T(8,128)(2,1)S(1)}, u32[]{:S(2)}, u32[]{:S(2)}) collective-permute-start(bf16[42,16,256]{2,1,0:T(8,128)(2,1)S(1)} %copy-done.18), channel_id=1, source_target_pairs={{1,0},{2,1},{3,2},{4,3},{5,4},{6,5},{7,6},{8,7},{9,8},{10,9},{11,1... | collective-permute-start | bytes 1032200 | tf_op jit(solution)/shard_map/ppermute | solution.py:409
  37.5 13.6 %copy-start.5 = (bf16[42,16,256]{2,1,0:T(8,128)(2,1)}, bf16[42,16,256]{2,1,0:T(8,128)(2,1)S(1)}, u32[]{:S(2)}) copy-start(bf16[42,16,256]{2,1,0:T(8,128)(2,1)S(1)} %collective-permute-done.4.low_ref) | copy-start | bytes 1032196
  37.6 67.6 %collective-permute-start.6 = (bf16[42,16,256]{2,1,0:T(8,128)(2,1)}, bf16[42,16,256]{2,1,0:T(8,128)(2,1)S(1)}, u32[]{:S(2)}, u32[]{:S(2)}) collective-permute-start(bf16[42,16,256]{2,1,0:T(8,128)(2,1)} %get-tuple-element.33), channel_id=1, source_target_pairs={{0,1},{1,2},{2,3},{3,4},{4,5},{5,6},{6,7},{7,8},{8,9},{9,10},{10,1... | collective-permute-start | bytes 1032200 | tf_op jit(solution)/shard_map/ppermute | solution.py:408
  42.2 8.9 %copy-start.6 = (bf16[42,16,256]{2,1,0:T(8,128)(2,1)}, bf16[42,16,256]{2,1,0:T(8,128)(2,1)S(1)}, u32[]{:S(2)}) copy-start(bf16[42,16,256]{2,1,0:T(8,128)(2,1)S(1)} %collective-permute-done.5.high_ref) | copy-start | bytes 1032196
  42.2 63.1 %collective-permute-start.7 = (bf16[42,16,256]{2,1,0:T(8,128)(2,1)}, bf16[42,16,256]{2,1,0:T(8,128)(2,1)S(1)}, u32[]{:S(2)}, u32[]{:S(2)}) collective-permute-start(bf16[42,16,256]{2,1,0:T(8,128)(2,1)} %get-tuple-element.34), channel_id=1, source_target_pairs={{1,0},{2,1},{3,2},{4,3},{5,4},{6,5},{7,6},{8,7},{9,8},{10,9},{11,1... | collective-permute-start | bytes 1032200 | tf_op jit(solution)/shard_map/ppermute | solution.py:409
  43.6 34.2 %copy-start.4 = (bf16[42,16,256]{2,1,0:T(8,128)(2,1)}, bf16[42,16,256]{2,1,0:T(8,128)(2,1)S(1)}, u32[]{:S(2)}) copy-start(bf16[42,16,256]{2,1,0:T(8,128)(2,1)S(1)} %collective-permute-done.2.low_ref) | copy-start | bytes 1032196
  43.6 34.2 %collective-permute-start.3 = (bf16[42,16,256]{2,1,0:T(8,128)(2,1)}, bf16[42,16,256]{2,1,0:T(8,128)(2,1)S(1)}, u32[]{:S(2)}, u32[]{:S(2)}) collective-permute-start(bf16[42,16,256]{2,1,0:T(8,128)(2,1)} %get-tuple-element.26), channel_id=1, source_target_pairs={{1,0},{2,1},{3,2},{4,3},{5,4},{6,5},{7,6},{8,7},{9,8},{10,9},{11,1... | collective-permute-start | bytes 1032200 | tf_op jit(solution)/shard_map/ppermute | solution.py:409
  77.8 0.7 copy-start.11
  77.8 132.3 %collective-permute-start.16 = (bf16[6,16,16,256]{3,2,1,0:T(8,128)(2,1)}, bf16[6,16,16,256]{3,2,1,0:T(8,128)(2,1)S(1)}, u32[]{:S(2)}, u32[]{:S(2)}) collective-permute-start(bf16[6,16,16,256]{3,2,1,0:T(8,128)(2,1)} %get-tuple-element.41.refs_1_), channel_id=1, source_target_pairs={{16,0},{0,16},{17,1},{1,17},{18,2},{2,18},{19,3},{3,19},{20,4},{4,... | collective-permute-start | bytes 2359304 | tf_op jit(solution)/shard_map/ppermute | solution.py:356
  105.1 0.8 copy-start.9
  105.1 104.9 %collective-permute-start.15 = (bf16[6,16,16,256]{3,2,1,0:T(8,128)(2,1)}, bf16[6,16,16,256]{3,2,1,0:T(8,128)(2,1)S(1)}, u32[]{:S(2)}, u32[]{:S(2)}) collective-permute-start(bf16[6,16,16,256]{3,2,1,0:T(8,128)(2,1)} %get-tuple-element.40.refs_0_), channel_id=1, source_target_pairs={{16,0},{0,16},{17,1},{1,17},{18,2},{2,18},{19,3},{3,19},{20,4},{4,... | collective-permute-start | bytes 2359304 | tf_op jit(solution)/shard_map/ppermute | solution.py:356
  105.9 0.7 copy-start.10
  133.3 28.7 %copy-start.16 = (f32[16,128]{1,0:T(8,128)S(1)}, f32[16,128]{1,0:T(8,128)}, u32[]{:S(2)}) copy-start(f32[16,128]{1,0:T(8,128)} %get-tuple-element.29) | copy-start | bytes 24580
  133.3 28.7 %copy-start.15 = (f32[16,128]{1,0:T(8,128)S(1)}, f32[16,128]{1,0:T(8,128)}, u32[]{:S(2)}) copy-start(f32[16,128]{1,0:T(8,128)} %get-tuple-element.32) | copy-start | bytes 24580
  133.3 28.7 %copy-start.17 = (f32[16,128]{1,0:T(8,128)S(1)}, f32[16,128]{1,0:T(8,128)}, u32[]{:S(2)}) copy-start(f32[16,128]{1,0:T(8,128)} %get-tuple-element.35) | copy-start | bytes 24580
  133.3 76.8 %collective-permute-start.17 = (bf16[6,16,16,256]{3,2,1,0:T(8,128)(2,1)}, bf16[6,16,16,256]{3,2,1,0:T(8,128)(2,1)S(1)}, u32[]{:S(2)}, u32[]{:S(2)}) collective-permute-start(bf16[6,16,16,256]{3,2,1,0:T(8,128)(2,1)} %get-tuple-element.42.refs_2_), channel_id=1, source_target_pairs={{16,0},{0,16},{17,1},{1,17},{18,2},{2,18},{19,3},{3,19},{20,4},{4,... | collective-permute-start | bytes 2359304 | tf_op jit(solution)/shard_map/ppermute | solution.py:356
  133.5 0.7 copy-start.7
  134.2 0.7 copy-start.8
  161.6 48.6 %collective-permute-start.18 = (bf16[6,16,16,256]{3,2,1,0:T(8,128)(2,1)}, bf16[6,16,16,256]{3,2,1,0:T(8,128)(2,1)S(1)}, u32[]{:S(2)}, u32[]{:S(2)}) collective-permute-start(bf16[6,16,16,256]{3,2,1,0:T(8,128)(2,1)} %get-tuple-element.43.refs_3_), channel_id=1, source_target_pairs={{16,0},{0,16},{17,1},{1,17},{18,2},{2,18},{19,3},{3,19},{20,4},{4,... | collective-permute-start | bytes 2359304 | tf_op jit(solution)/shard_map/ppermute | solution.py:356
  162.7 1.5 copy-start.13
  162.7 1.4 collective-permute-start.10
  164.1 0.6 copy-start.14
  166.4 7.1 %collective-permute-start.11 = (f32[136,128]{1,0:T(8,128)}, f32[136,128]{1,0:T(8,128)S(1)}, u32[]{:S(2)}, u32[]{:S(2)}) collective-permute-start(f32[136,128]{1,0:T(8,128)} %gram.1), channel_id=1, source_target_pairs={{0,1},{1,0},{2,3},{3,2},{4,5},{5,4},{6,7},{7,6},{8,9},{9,8},{10,11... | collective-permute-start | bytes 208904 | tf_op jit(solution)/shard_map/ppermute | solution.py:348
  174.4 5.8 %collective-permute-start.12 = (f32[136,128]{1,0:T(8,128)S(1)}, f32[136,128]{1,0:T(8,128)S(1)}, u32[]{:S(2)}, u32[]{:S(2)}) collective-permute-start(f32[136,128]{1,0:T(8,128)S(1)} %add.12), channel_id=1, source_target_pairs={{0,2},{1,3},{2,0},{3,1},{4,6},{5,7},{6,4},{7,5},{8,10},{9,11},{10,... | collective-permute-start | bytes 208904 | tf_op jit(solution)/shard_map/ppermute | solution.py:348
  180.2 5.0 %collective-permute-start.13 = (f32[136,128]{1,0:T(8,128)S(1)}, f32[136,128]{1,0:T(8,128)S(1)}, u32[]{:S(2)}, u32[]{:S(2)}) collective-permute-start(f32[136,128]{1,0:T(8,128)S(1)} %add.13), channel_id=1, source_target_pairs={{0,4},{1,5},{2,6},{3,7},{4,0},{5,1},{6,2},{7,3},{8,12},{9,13},{10,... | collective-permute-start | bytes 208904 | tf_op jit(solution)/shard_map/ppermute | solution.py:348
  185.2 5.4 %collective-permute-start.14 = (f32[136,128]{1,0:T(8,128)S(1)}, f32[136,128]{1,0:T(8,128)S(1)}, u32[]{:S(2)}, u32[]{:S(2)}) collective-permute-start(f32[136,128]{1,0:T(8,128)S(1)} %add.14), channel_id=1, source_target_pairs={{0,8},{1,9},{2,10},{3,11},{4,12},{5,13},{6,14},{7,15},{8,0},{9,1},... | collective-permute-start | bytes 208904 | tf_op jit(solution)/shard_map/ppermute | solution.py:348
  210.1 0.9 copy-start
  210.1 1.1 copy-start.1
  210.1 1.4 copy-start.2
  210.1 1.6 copy-start.3

commit v2 on v1

--- a/solution.py
+++ b/solution.py
@@ -141,112 +141,132 @@
     where_ref, low_ref, high_ref, wet_ref, coef_ref, stations_ref, *refs,
     tile_rows, grid_rows,
 ):
-    cov_refs, (pf_out, sensed_out, st) = refs[:-3], refs[-3:]
+    cov_refs, (pf_out, sensed_out, state_a, state_b, press, flux) = refs[:-6], refs[-6:]
     first_row = where_ref[0]
     ext = tile_rows + 2 * DEPTH
     groups = len(cov_refs)
     cells = 128 * groups
     stride = 6 * tile_rows
+    halves = range(GROUP // 8)
+
+    def at(ref, field, r, kg):
+        return [ref[field, r, pl.ds(8 * kg, 8), pl.ds(128 * c, 128)] for c in range(groups)]
+
+    def put(ref, field, r, kg, parts):
+        for c in range(groups):
+            ref[field, r, pl.ds(8 * kg, 8), pl.ds(128 * c, 128)] = parts[c]
+
+    def spread(ref, index, r):
+        rows = ref.shape[0] // groups
+        return [ref[pl.ds(c * rows + index * ext + r, 8, stride=0), :] for c in range(groups)]
 
     def fill(r, carry):
         for f in range(6):
             for c in range(groups):
-                st[f, DEPTH + r, :, pl.ds(128 * c, 128)] = cov_refs[c][
+                state_a[f, DEPTH + r, :, pl.ds(128 * c, 128)] = cov_refs[c][
                     pl.ds(f * tile_rows + r, GROUP, stride=stride), :
                 ]
         return carry
 
     lax.fori_loop(0, tile_rows, fill, 0)
     for i, (field, d) in enumerate(halo_rows()):
-        st[field, DEPTH - d] = low_ref[i].astype(f32)
-        st[field, DEPTH + tile_rows + d - 1] = high_ref[i].astype(f32)
+        state_a[field, DEPTH - d] = low_ref[i].astype(f32)
+        state_a[field, DEPTH + tile_rows + d - 1] = high_ref[i].astype(f32)
     for layer in range(2):
         for r in (1, ext - 2):
-            st[3 * layer + 2, r] = jnp.zeros((GROUP, cells), f32)
+            state_a[3 * layer + 2, r] = jnp.zeros((GROUP, cells), f32)
+
+    def press_of(top, bottom):
+        p_top = gravity * (top + bottom)
+        return p_top, p_top - reduced_gravity * top
+
+    def first_press(r, carry):
+        press[0, r], press[1, r] = press_of(state_a[0, r], state_a[3, r])
+        return carry
+
+    lax.fori_loop(0, ext, first_press, 0, unroll=2)
     lane = lax.broadcasted_iota(jnp.int32, (8, 128), 1)
 
-    for t in range(ITERS):
-        shrink = 2 * t
-        for kg in range(GROUP // 8):
-
-            def load(field, r, kg=kg):
-                return [
-                    st[field, r, pl.ds(8 * kg, 8), pl.ds(128 * c, 128)] for c in range(groups)
-                ]
-
-            def store(field, r, parts, kg=kg):
-                for c in range(groups):
-                    st[field, r, pl.ds(8 * kg, 8), pl.ds(128 * c, 128)] = parts[c]
-
-            def spread(ref, index, r):
-                rows = ref.shape[0] // groups
-                return [
-                    ref[pl.ds(c * rows + index * ext + r, 8, stride=0), :] for c in range(groups)
-                ]
-
-            def pressures(h):
-                top = [a + b for a, b in zip(h[0], h[1])]
-                return [top, [p - reduced_gravity * a for p, a in zip(top, h[0])]]
-
-            def body(r, carry, t=t, load=load, store=store):
-                p_prev, p_here, h_here, flux_2, flux_1, part_1 = carry
-                h_next = [load(0, r + 1), load(3, r + 1)]
-                p_next = pressures(h_next)
-                wet_a, wet_b, wet_c = (spread(wet_ref, q, r) for q in range(3))
-                g = first_row - DEPTH + r - 1
-                keep = jnp.where(jnp.logical_and(g >= 0, g < grid_rows), 1.0, 0.0).astype(f32)
-                flux_0, part_0 = [], []
-                for layer in range(2):
-                    u, v = load(3 * layer + 1, r), load(3 * layer + 2, r)
-                    depth, mu, mv = (
-                        spread(coef_ref, t * 6 + 3 * layer + q, r) for q in range(3)
-                    )
-                    slope = lane_steps(p_here[layer], lane)
-                    u_new, v_new, flux, cross = [], [], [], []
+    def move(t, src, dst, r_first, count):
+        stores = []
+        for r in [r_first + k for k in range(count)]:
+            wet_a, wet_b, wet_c = (spread(wet_ref, q, r) for q in range(3))
+            for layer in range(2):
+                depth, mu, mv = (spread(coef_ref, t * 6 + 3 * layer + q, r) for q in range(3))
+                for kg in halves:
+                    h = at(src, 3 * layer, r, kg)
+                    u = at(src, 3 * layer + 1, r, kg)
+                    v = at(src, 3 * layer + 2, r, kg)
+                    before = at(press, layer, r - 1, kg)
+                    after = at(press, layer, r + 1, kg)
+                    slope = lane_steps(at(press, layer, r, kg), lane)
+                    u_new, v_new, along, cross = [], [], [], []
                     for c in range(groups):
-                        u_c = (
-                            wet_a[c] * u[c]
-                            + wet_b[c] * v[c]
-                            - wet_c[c] * (p_next[layer][c] - p_prev[layer][c])
-                        )
+                        u_c = wet_a[c] * u[c] + wet_b[c] * v[c] - wet_c[c] * (after[c] - before[c])
                         v_c = wet_a[c] * v[c] - wet_b[c] * u[c] - wet_c[c] * slope[c]
-                        h = h_here[layer][c]
                         u_new.append(u_c)
                         v_new.append(v_c)
-                        flux.append(depth[c] * u_c + h * mu[c])
-                        cross.append(depth[c] * v_c + h * mv[c])
-                    store(3 * layer + 1, r, u_new)
-                    store(3 * layer + 2, r, v_new)
+                        along.append(depth[c] * u_c + h[c] * mu[c])
+                        cross.append(depth[c] * v_c + h[c] * mv[c])
                     cross = lane_steps(cross, lane)
-                    part_0.append([h_here[layer][c] - cross[c] for c in range(groups)])
-                    flux_0.append(flux)
-                    store(
-                        3 * layer,
-                        r - 1,
-                        [
-                            keep * (part_1[layer][c] - (flux[c] - flux_2[layer][c]))
-                            for c in range(groups)
-                        ],
+                    part = [h[c] - cross[c] for c in range(groups)]
+                    stores += [
+                        (dst, 3 * layer, r, kg, part),
+                        (dst, 3 * layer + 1, r, kg, u_new),
+                        (dst, 3 * layer + 2, r, kg, v_new),
+                        (flux, layer, r, kg, along),
+                    ]
+        for store in stores:
+            put(*store)
+
+    def rise(t, dst, r_first, count):
+        stores = []
+        for r in [r_first + k for k in range(count)]:
+            g = first_row - DEPTH + r
+            keep = jnp.where(jnp.logical_and(g >= 0, g < grid_rows), 1.0, 0.0).astype(f32)
+            for kg in halves:
+                fresh = []
+                for layer in range(2):
+                    part = at(dst, 3 * layer, r, kg)
+                    before, after = at(flux, layer, r - 1, kg), at(flux, layer, r + 1, kg)
+                    fresh.append(
+                        [keep * (part[c] - (after[c] - before[c])) for c in range(groups)]
                     )
-                return (p_here, p_next, h_next, flux_1, flux_0, part_0)
-
-            h_a = [load(0, shrink), load(3, shrink)]
-            h_b = [load(0, shrink + 1), load(3, shrink + 1)]
-            nothing = [[a - a for a in h] for h in h_a]
-            lax.fori_loop(
-                shrink + 1,
-                ext - shrink - 1,
-                body,
-                (pressures(h_a), pressures(h_b), h_b, nothing, nothing, nothing),
-                unroll=2,
-            )
+                    stores.append((dst, 3 * layer, r, kg, fresh[-1]))
+                if t < ITERS - 1:
+                    both = [press_of(fresh[0][c], fresh[1][c]) for c in range(groups)]
+                    for layer in range(2):
+                        stores.append((press, layer, r, kg, [p[layer] for p in both]))
+        for store in stores:
+            put(*store)
+
+    src, dst = state_a, state_b
+    for t in range(ITERS):
+        first = 2 * t + 1
+        n_move = ext - 4 * t - 2
+        pace = 2 if n_move % 2 == 0 else 1
+
+        def move_body(i, carry, t=t, src=src, dst=dst, first=first, pace=pace):
+            move(t, src, dst, first + pace * i, pace)
+            return carry
+
+        lax.fori_loop(0, n_move // pace, move_body, 0)
+        n_rise = n_move - 2
+        pace_rise = 4 if n_rise % 4 == 0 else (2 if n_rise % 2 == 0 else 1)
+
+        def rise_body(i, carry, t=t, dst=dst, first=first, pace=pace_rise):
+            rise(t, dst, first + 1 + pace * i, pace)
+            return carry
+
+        lax.fori_loop(0, n_rise // pace_rise, rise_body, 0)
+        src, dst = dst, src
 
     n_stations = stations_ref.shape[1]
     total = jnp.zeros((3 * GROUP, n_stations), f32)
     for r in range(tile_rows):
         for f in range(6):
-            pf_out[f, r] = st[f, DEPTH + r].astype(bf16)
-        surface = st[0, DEPTH + r] + st[3, DEPTH + r]
+            pf_out[f, r] = src[f, DEPTH + r].astype(bf16)
+        surface = src[0, DEPTH + r] + src[3, DEPTH + r]
         high = surface.astype(bf16)
         rest = surface - high.astype(f32)
         middle = rest.astype(bf16)
@@ -286,26 +306,46 @@
     eye = [(lane == sub + 8 * b).astype(f32) for b in range(blocks)]
     m = [gram_ref[pl.ds(8 * b, 8), :] + eye[b] for b in range(blocks)]
     w = list(eye)
-    pivots = [jnp.ones((8, total), f32) for _ in range(blocks)]
-    for j in range(total):
-        b, i = j // 8, j % 8
-        heads = {q: jnp.broadcast_to(m[q][:, j : j + 1], (8, total)) for q in range(b, blocks)}
-        pivot = jnp.broadcast_to(heads[b][i : i + 1, :], (8, total))
-        pivots[b] = jnp.where(sub == i, pivot, pivots[b])
-        inverse = 1.0 / pivot
-        row_m = jnp.broadcast_to(m[b][i : i + 1, :], (8, total)) * inverse
-        row_w = jnp.broadcast_to(w[b][i : i + 1, :], (8, total)) * inverse
-        for q in range(b, blocks):
-            head = jnp.where(sub > i, heads[q], 0.0) if q == b else heads[q]
-            m[q] = m[q] - head * row_m
-            w[q] = w[q] - head * row_w
+
+    def column(x, j):
+        return jnp.broadcast_to(x[:, j : j + 1], (8, total))
+
+    def row(x, i):
+        return jnp.broadcast_to(x[i : i + 1, :], (8, total))
+
+    scaled = []
+    for b in range(blocks):
+        heads = [column(m[b], 8 * b + i) for i in range(8)]
+        z_m, z_w, low = m[b], w[b], w[b]
+        pivots = jnp.ones((8, total), f32)
+        for i in range(8):
+            pivot = row(heads[i], i)
+            pivots = jnp.where(sub == i, pivot, pivots)
+            inverse = 1.0 / pivot
+            here = sub == i
+            head = heads[i]
+            for k in range(i + 1, 8):
+                factor = row(heads[k], i) * inverse
+                heads[k] = jnp.where(here, factor, heads[k] - head * factor)
+            row_m = row(z_m, i) * inverse
+            row_w = row(z_w, i) * inverse
+            z_m = jnp.where(here, row_m, z_m - head * row_m)
+            z_w = jnp.where(here, row_w, z_w - head * row_w)
+            low = jnp.where(sub > i, low - head * row_w, low)
+        scaled.append(low / jnp.sqrt(pivots))
+        rows_m = [row(z_m, i) for i in range(8)]
+        rows_w = [row(z_w, i) for i in range(8)]
+        for q in range(b + 1, blocks):
+            tails = [column(m[q], 8 * b + i) for i in range(8)]
+            m[q] = m[q] - tree_sum([tails[i] * rows_m[i] for i in range(8)])
+            w[q] = w[q] - tree_sum([tails[i] * rows_w[i] for i in range(8)])
     target = gram_ref[pl.ds(total, 1), :]
-    weights = jnp.zeros((1, total), f32)
+    weights = jnp.zeros((8, total), f32)
     for b in range(blocks):
-        inv = w[b] / jnp.sqrt(pivots[b])
-        scr[pl.ds(8 * b, 8), :] = inv
-        half = jnp.sum(inv * target, axis=1, keepdims=True)
-        weights = weights + jnp.sum(inv * half, axis=0, keepdims=True)
+        scr[pl.ds(8 * b, 8), :] = scaled[b]
+        half = jnp.sum(scaled[b] * target, axis=1, keepdims=True)
+        weights = weights + scaled[b] * half
+    weights = jnp.sum(weights, axis=0, keepdims=True)
     shift = lax.rem(total - index * columns, total)
     mine = scr[pl.ds(pl.multiple_of(index * columns, 8), columns), :]
     mix_out[pl.ds(0, columns), :] = pltpu.roll(mine, shift, 1).astype(bf16)
@@ -317,16 +357,23 @@
     mix_out[pl.ds(columns, 16), :] = jnp.concatenate([rows, pad], axis=0).astype(bf16)
 
 
+def tree_sum(values):
+    while len(values) > 1:
+        values = [values[i] + values[i + 1] for i in range(0, len(values), 2)]
+    return values[0]
+
+
 def mix_kernel(where_ref, mix_ref, mean_ref, *refs, columns):
     piece_refs, cov_out, mean_out, scr = refs[:-3], refs[-3], refs[-2], refs[-1]
     tile_rows, cells = mean_ref.shape[1:]
     piece = mean_out.shape[2]
     group = pl.program_id(1)
     mix = mix_ref[...]
+    cov_flat = cov_out.reshape(columns * tile_rows, 128)
     for r in range(tile_rows):
         stack = jnp.concatenate([ref[0, r] for ref in piece_refs], axis=0)
         result = jnp.dot(mix, stack, preferred_element_type=f32)
-        cov_out[:, 0, r, :] = result[:columns]
+        cov_flat[pl.ds(r, columns, stride=tile_rows), :] = result[:columns]
         scr[group, pl.ds(r, 1), :] = (
             result[columns : columns + 1] + result[columns + 1 : columns + 2]
         )
@@ -445,7 +492,7 @@
                 jax.ShapeDtypeStruct((6, tile_rows, GROUP, cells), bf16),
                 jax.ShapeDtypeStruct((GROUP, n_stations), f32),
             ],
-            scratch_shapes=[pltpu.VMEM((6, ext, GROUP, cells), f32)],
+            scratch_shapes=[pltpu.VMEM((n, ext, GROUP, cells), f32) for n in (6, 6, 2, 2)],
             name=f"window_{c}",
         )(where, lows[c], highs[c], wet, coef, station_row, *[flat] * groups)
         forecasts.append(shifted(pf, "cols"))

time: 225 us -> 166 us (0.74)
  Pallas kernels: 154 us -> 89.7 us
  waiting for transfers between devices: 13.1 us -> 26.7 us
  starting transfers between devices: 44 us -> 35.2 us
    pallas_call x4, Pallas kernels: 106 us -> 54.9 us  [local(): pl.pallas_call(functools.partial(window_kernel, tile_rows=tile_rows, grid...]
    pallas_call x1, Pallas kernels: 18.8 us -> 6.26 us  [local(): pl.pallas_call(functools.partial(factor_kernel, columns=columns), in_spec...]
    ppermute x4, waiting for transfers between devices: 0.01 us -> 9.82 us  [local(): highs.append(lax.ppermute(going_down, 'space', down))]
    ppermute x4, starting transfers between devices: 13.5 us -> 5.18 us  [spread_sum(): lax.ppermute(value, axis, [(i, i ^ step) for i in range(count)])]
    ppermute x4, waiting for transfers between devices: 9.78 us -> 13.5 us  [spread_sum(): lax.ppermute(value, axis, [(i, i ^ step) for i in range(count)])]
  transfers between devices with their start and end apart: 19 -> 19, of which waited for: 6 -> 7; matrix products, arithmetic and copies ran while one was open for 2% -> 2% of each run, Pallas kernels for 62% -> 46%
where the time goes in v2:
time: 166 us; the launch traced here: 164 us
  Pallas kernels  89.7 us (54%)
  starting transfers between devices  35.2 us (21%)
  waiting for transfers between devices  26.7 us (16%)
  local copies, waits for them, and re-layouts  6.55 us (4%)
  other arithmetic  2.67 us (2%)
  blocking collectives  2.26 us (1%)
    pallas_call x4, Pallas kernels, local(): pl.pallas_call(functools.partial(window_kernel, tile_rows=tile_rows, grid...  54.9 us
    ppermute x4, starting transfers between devices, local(): lows.append(lax.ppermute(going_up, 'space', up))  18.5 us
    ppermute x4, waiting for transfers between devices, spread_sum(): lax.ppermute(value, axis, [(i, i ^ step) for i in range(count)])  13.5 us
    pallas_call x4, Pallas kernels, local(): pl.pallas_call(functools.partial(pack_kernel, tile_rows=tile_rows), grid=...  12.1 us
    pallas_call x1, Pallas kernels, local(): pl.pallas_call(functools.partial(mix_kernel, columns=columns), grid=(6, g...  11.2 us
    ppermute x4, waiting for transfers between devices, local(): highs.append(lax.ppermute(going_down, 'space', down))  9.82 us
    pallas_call x1, Pallas kernels, local(): pl.pallas_call(functools.partial(factor_kernel, columns=columns), in_spec...  6.26 us
    unnamed x43, local copies, waits for them, and re-layouts  5.85 us
  transfers between devices with their start and end apart: 19, of which 7 were waited for; matrix products, arithmetic and copies ran while one was open for 2% of the time, Pallas kernels for 46%

profile of v2, /device:TPU:0, one launch (start us, length us, event | category | flops | bytes accessed | tf_op | source)
XLA Modules:
  0.0 164.2 jit_solution(12023746290419494091)
XLA Ops:
  0.6 3.0 %pack_1.1 = (bf16[42,16,256]{2,1,0:T(8,128)(2,1)}, bf16[42,16,256]{2,1,0:T(8,128)(2,1)}) custom-call(f32[6144,256]{1,0:T(8,128)} %bitcast.7, f32[6144,256]{1,0:T(8,128)} %bitcast.8), custom_call_target="tpu_custom_call" | custom-call | tf_op jit(solution)/shard_map/pack_1/pallas_call | solution.py:447
  3.6 4.9 %collective-permute-start.4 = (bf16[42,16,256]{2,1,0:T(8,128)(2,1)}, bf16[42,16,256]{2,1,0:T(8,128)(2,1)S(1)}, u32[]{:S(2)}, u32[]{:S(2)}) collective-permute-start(bf16[42,16,256]{2,1,0:T(8,128)(2,1)} %get-tuple-element.30), channel_id=1, source_target_pairs={{0,1},{1,2},{2,3},{3,4},{4,5},{5,6},{6,7},{7,8},{8,9},{9,10},{10,1... | collective-permute-start | bytes 1032200 | tf_op jit(solution)/shard_map/ppermute | solution.py:455
  8.5 1.4 collective-permute-start.5
  10.0 3.0 %pack_0.1 = (bf16[42,16,256]{2,1,0:T(8,128)(2,1)}, bf16[42,16,256]{2,1,0:T(8,128)(2,1)}) custom-call(f32[6144,256]{1,0:T(8,128)} %bitcast.9, f32[6144,256]{1,0:T(8,128)} %bitcast.10), custom_call_target="tpu_custom_call" | custom-call | tf_op jit(solution)/shard_map/pack_0/pallas_call | solution.py:447
  13.0 4.6 %collective-permute-start.2 = (bf16[42,16,256]{2,1,0:T(8,128)(2,1)}, bf16[42,16,256]{2,1,0:T(8,128)(2,1)S(1)}, u32[]{:S(2)}, u32[]{:S(2)}) collective-permute-start(bf16[42,16,256]{2,1,0:T(8,128)(2,1)} %get-tuple-element.25), channel_id=1, source_target_pairs={{0,1},{1,2},{2,3},{3,4},{4,5},{5,6},{6,7},{7,8},{8,9},{9,10},{10,1... | collective-permute-start | bytes 1032200 | tf_op jit(solution)/shard_map/ppermute | solution.py:455
  17.6 4.3 %collective-permute-start = (f32[6,8,128]{2,1,0:T(8,128)S(1)}, f32[6,8,128]{2,1,0:T(8,128)S(1)}, u32[]{:S(2)}, u32[]{:S(2)}) collective-permute-start(f32[6,8,128]{2,1,0:T(8,128)S(1)} %get-tuple-element.46), channel_id=1, source_target_pairs={{0,1},{1,2},{2,3},{3,4},{4,5},{5,6},{6,7},{7,8},{8,9},{9,10},{10,1... | collective-permute-start | bytes 73736 | tf_op jit(solution)/shard_map/ppermute | solution.py:432
  21.8 1.3 collective-permute-start.1
  23.1 0.6 pad_add_fusion.where_ref
  23.8 3.0 %pack_3.1 = (bf16[42,16,256]{2,1,0:T(8,128)(2,1)}, bf16[42,16,256]{2,1,0:T(8,128)(2,1)}) custom-call(f32[6144,256]{1,0:T(8,128)} %bitcast.11, f32[6144,256]{1,0:T(8,128)} %bitcast.12), custom_call_target="tpu_custom_call" | custom-call | tf_op jit(solution)/shard_map/pack_3/pallas_call | solution.py:447
  26.8 3.1 %pack_2.1 = (bf16[42,16,256]{2,1,0:T(8,128)(2,1)}, bf16[42,16,256]{2,1,0:T(8,128)(2,1)}) custom-call(f32[6144,256]{1,0:T(8,128)} %bitcast.13, f32[6144,256]{1,0:T(8,128)} %bitcast.14), custom_call_target="tpu_custom_call" | custom-call | tf_op jit(solution)/shard_map/pack_2/pallas_call | solution.py:447
  29.8 2.0 %collective-permute-done = f32[6,8,128]{2,1,0:T(8,128)S(1)} collective-permute-done((f32[6,8,128]{2,1,0:T(8,128)S(1)}, f32[6,8,128]{2,1,0:T(8,128)S(1)}, u32[]{:S(2)}, u32[]{:S(2)}) %collective-permute-start) | collective-permute-done | bytes 24608 | tf_op jit(solution)/shard_map/ppermute | solution.py:432
  31.8 4.4 %collective-permute-start.8 = (bf16[42,16,256]{2,1,0:T(8,128)(2,1)}, bf16[42,16,256]{2,1,0:T(8,128)(2,1)S(1)}, u32[]{:S(2)}, u32[]{:S(2)}) collective-permute-start(bf16[42,16,256]{2,1,0:T(8,128)(2,1)} %get-tuple-element.36), channel_id=1, source_target_pairs={{0,1},{1,2},{2,3},{3,4},{4,5},{5,6},{6,7},{7,8},{8,9},{9,10},{10,1... | collective-permute-start | bytes 1032200 | tf_op jit(solution)/shard_map/ppermute | solution.py:455
  36.2 1.3 collective-permute-start.9
  37.6 4.7 %collective-permute-start.6 = (bf16[42,16,256]{2,1,0:T(8,128)(2,1)}, bf16[42,16,256]{2,1,0:T(8,128)(2,1)S(1)}, u32[]{:S(2)}, u32[]{:S(2)}) collective-permute-start(bf16[42,16,256]{2,1,0:T(8,128)(2,1)} %get-tuple-element.33), channel_id=1, source_target_pairs={{0,1},{1,2},{2,3},{3,4},{4,5},{5,6},{6,7},{7,8},{8,9},{9,10},{10,1... | collective-permute-start | bytes 1032200 | tf_op jit(solution)/shard_map/ppermute | solution.py:455
  42.2 1.3 collective-permute-start.7
  43.6 1.3 collective-permute-start.3
  44.9 0.5 subtract_bitcast_fusion.stations_ref
  45.4 2.3 %all_gather.3.mean_ref = f32[6,32,256]{2,1,0:T(8,128)} all-gather(f32[6,32,128]{2,1,0:T(8,128)S(1)} %pad_maximum_fusion), channel_id=1, replica_groups=mesh['cols'=2,'space'=16] {'cols'}, dimensions={2}, use_global_device_ids=true | all-gather | bytes 294912 | tf_op jit(solution)/shard_map/all_gather | solution.py:435
  47.6 3.5 %mean_window.1 = (f32[192,128]{1,0:T(8,128)}, f32[1536,128]{1,0:T(8,128)}, f32[6,16,256]{2,1,0:T(8,128)}, f32[8,128]{1,0:T(8,128)}) custom-call(s32[2]{0:T(128)} %pad_add_fusion.where_ref, f32[6,32,256]{2,1,0:T(8,128)} %all_gather.3.mean_ref, s32[256,256]{1,0:T(8,128)} %mask_ref.1, s32[1,128]{1,0:T(1,128)} %subtract_bitcast_fusion.stations_ref, ...), custom_call_target="tpu_custom_call" | custom-call | tf_op jit(solution)/shard_map/mean_window/pallas_call | solution.py:460
  51.1 13.7 %window_1.1 = (bf16[6,16,16,256]{3,2,1,0:T(8,128)(2,1)}, f32[16,128]{1,0:T(8,128)}) custom-call(s32[2]{0:T(128)} %pad_add_fusion.where_ref, bf16[42,16,256]{2,1,0:T(8,128)(2,1)} %copy-done.5, bf16[42,16,256]{2,1,0:T(8,128)(2,1)} %copy-done.6, f32[192,128]{1,0:T(8,128)} %get-tuple-element.27.wet_ref, f32[1536,128]{1,0:T(8,128)} %get-tuple-element.28.coef_ref, ...), custom_call_target="tpu_custom_call" | custom-call | tf_op jit(solution)/shard_map/window_1/pallas_call | solution.py:475
  64.9 9.8 %collective-permute-done.3.high_ref = bf16[42,16,256]{2,1,0:T(8,128)(2,1)S(1)} collective-permute-done((bf16[42,16,256]{2,1,0:T(8,128)(2,1)}, bf16[42,16,256]{2,1,0:T(8,128)(2,1)S(1)}, u32[]{:S(2)}, u32[]{:S(2)}) %collective-permute-start.3) | collective-permute-done | bytes 344096 | tf_op jit(solution)/shard_map/ppermute | solution.py:456
  74.7 0.7 copy-done.11
  75.4 13.7 %window_0.1 = (bf16[6,16,16,256]{3,2,1,0:T(8,128)(2,1)}, f32[16,128]{1,0:T(8,128)}) custom-call(s32[2]{0:T(128)} %pad_add_fusion.where_ref, bf16[42,16,256]{2,1,0:T(8,128)(2,1)} %copy-done.4, bf16[42,16,256]{2,1,0:T(8,128)(2,1)} %copy-done.11, f32[192,128]{1,0:T(8,128)} %get-tuple-element.27.wet_ref, f32[1536,128]{1,0:T(8,128)} %get-tuple-element.28.coef_ref, ...), custom_call_target="tpu_custom_call" | custom-call | tf_op jit(solution)/shard_map/window_0/pallas_call | solution.py:475
  89.2 0.7 copy-done.9
  89.9 0.7 copy-done.10
  90.7 13.7 %window_2.1 = (bf16[6,16,16,256]{3,2,1,0:T(8,128)(2,1)}, f32[16,128]{1,0:T(8,128)}) custom-call(s32[2]{0:T(128)} %pad_add_fusion.where_ref, bf16[42,16,256]{2,1,0:T(8,128)(2,1)} %copy-done.9, bf16[42,16,256]{2,1,0:T(8,128)(2,1)} %copy-done.10, f32[192,128]{1,0:T(8,128)} %get-tuple-element.27.wet_ref, f32[1536,128]{1,0:T(8,128)} %get-tuple-element.28.coef_ref, ...), custom_call_target="tpu_custom_call" | custom-call | tf_op jit(solution)/shard_map/window_2/pallas_call | solution.py:475
  104.5 0.7 copy-done.7
  105.2 0.7 copy-done.8
  105.9 13.7 %window_3.1 = (bf16[6,16,16,256]{3,2,1,0:T(8,128)(2,1)}, f32[16,128]{1,0:T(8,128)}) custom-call(s32[2]{0:T(128)} %pad_add_fusion.where_ref, bf16[42,16,256]{2,1,0:T(8,128)(2,1)} %copy-done.7, bf16[42,16,256]{2,1,0:T(8,128)(2,1)} %copy-done.8, f32[192,128]{1,0:T(8,128)} %get-tuple-element.27.wet_ref, f32[1536,128]{1,0:T(8,128)} %get-tuple-element.28.coef_ref, ...), custom_call_target="tpu_custom_call" | custom-call | tf_op jit(solution)/shard_map/window_3/pallas_call | solution.py:475
  119.7 0.5 collective-permute-start.18
  120.2 0.7 constant_dynamic-update-slice_fusion.refs_0_
  120.9 1.4 collective-permute-done.10.refs_1_
  122.3 0.6 copy-done.14
  122.9 1.7 %gram.1 = f32[136,128]{1,0:T(8,128)} custom-call(s32[2]{0:T(128)} %pad_add_fusion.where_ref, f32[1,128]{1,0:T(1,128)} %bitcast.24, f32[8,128]{1,0:T(8,128)} %get-tuple-element.24.innov_ref, f32[64,128]{1,0:T(8,128)} %copy-done.13, f32[64,128]{1,0:T(8,128)} %copy-done.14), custom_call_target="tpu_custom_call" | custom-call | tf_op jit(solution)/shard_map/gram/pallas_call | solution.py:502
  124.6 0.6 collective-permute-start.11
  125.2 4.1 %collective-permute-done.11 = f32[136,128]{1,0:T(8,128)S(1)} collective-permute-done((f32[136,128]{1,0:T(8,128)}, f32[136,128]{1,0:T(8,128)S(1)}, u32[]{:S(2)}, u32[]{:S(2)}) %collective-permute-start.11) | collective-permute-done | bytes 69664 | tf_op jit(solution)/shard_map/ppermute | solution.py:395
  129.3 0.9 add.12
  130.3 4.3 %collective-permute-done.12 = f32[136,128]{1,0:T(8,128)S(1)} collective-permute-done((f32[136,128]{1,0:T(8,128)S(1)}, f32[136,128]{1,0:T(8,128)S(1)}, u32[]{:S(2)}, u32[]{:S(2)}) %collective-permute-start.12) | collective-permute-done | bytes 69664 | tf_op jit(solution)/shard_map/ppermute | solution.py:395
  134.6 1.6 %collective-permute-start.13 = (f32[136,128]{1,0:T(8,128)S(1)}, f32[136,128]{1,0:T(8,128)S(1)}, u32[]{:S(2)}, u32[]{:S(2)}) collective-permute-start(f32[136,128]{1,0:T(8,128)S(1)} %add.13), channel_id=1, source_target_pairs={{0,4},{1,5},{2,6},{3,7},{4,0},{5,1},{6,2},{7,3},{8,12},{9,13},{10,... | collective-permute-start | bytes 208904 | tf_op jit(solution)/shard_map/ppermute | solution.py:395
  136.2 2.7 %collective-permute-done.13 = f32[136,128]{1,0:T(8,128)S(1)} collective-permute-done((f32[136,128]{1,0:T(8,128)S(1)}, f32[136,128]{1,0:T(8,128)S(1)}, u32[]{:S(2)}, u32[]{:S(2)}) %collective-permute-start.13) | collective-permute-done | bytes 69664 | tf_op jit(solution)/shard_map/ppermute | solution.py:395
  139.0 2.9 %collective-permute-start.14 = (f32[136,128]{1,0:T(8,128)S(1)}, f32[136,128]{1,0:T(8,128)S(1)}, u32[]{:S(2)}, u32[]{:S(2)}) collective-permute-start(f32[136,128]{1,0:T(8,128)S(1)} %add.14), channel_id=1, source_target_pairs={{0,8},{1,9},{2,10},{3,11},{4,12},{5,13},{6,14},{7,15},{8,0},{9,1},... | collective-permute-start | bytes 208904 | tf_op jit(solution)/shard_map/ppermute | solution.py:395
  141.9 2.4 %collective-permute-done.14 = f32[136,128]{1,0:T(8,128)S(1)} collective-permute-done((f32[136,128]{1,0:T(8,128)S(1)}, f32[136,128]{1,0:T(8,128)S(1)}, u32[]{:S(2)}, u32[]{:S(2)}) %collective-permute-start.14) | collective-permute-done | bytes 69664 | tf_op jit(solution)/shard_map/ppermute | solution.py:395
  144.3 0.6 add.15.gram_ref
  144.9 6.3 %factor.1.mix_ref = bf16[80,128]{1,0:T(8,128)(2,1)} custom-call(s32[2]{0:T(128)} %pad_add_fusion.where_ref, f32[136,128]{1,0:T(8,128)} %add.15.gram_ref), custom_call_target="tpu_custom_call" | custom-call | tf_op jit(solution)/shard_map/factor/pallas_call | solution.py:511
  151.2 0.8 copy-done
  152.1 0.3 copy-done.1
  152.3 0.3 copy-done.2
  152.8 11.2 %mix.1 = (f32[64,6,16,256]{3,2,1,0:T(8,128)}, f32[6,16,128]{2,1,0:T(8,128)}) custom-call(s32[2]{0:T(128)} %pad_add_fusion.where_ref, bf16[80,128]{1,0:T(8,128)(2,1)} %factor.1.mix_ref, f32[6,16,256]{2,1,0:T(8,128)} %get-tuple-element.39.mean_ref, bf16[6,16,16,256]{3,2,1,0:T(8,128)(2,1)} %get-tuple-element.40.refs_0_, ...), custom_call_target="tpu_custom_call" | custom-call | tf_op jit(solution)/shard_map/mix/pallas_call | solution.py:522
  (55 shorter events, 0.6 us)
Async XLA Ops:
  3.6 33.9 %collective-permute-start.4 = (bf16[42,16,256]{2,1,0:T(8,128)(2,1)}, bf16[42,16,256]{2,1,0:T(8,128)(2,1)S(1)}, u32[]{:S(2)}, u32[]{:S(2)}) collective-permute-start(bf16[42,16,256]{2,1,0:T(8,128)(2,1)} %get-tuple-element.30), channel_id=1, source_target_pairs={{0,1},{1,2},{2,3},{3,4},{4,5},{5,6},{6,7},{7,8},{8,9},{9,10},{10,1... | collective-permute-start | bytes 1032200 | tf_op jit(solution)/shard_map/ppermute | solution.py:455
  8.5 9.0 %copy-start.12 = (f32[6,16,128]{2,1,0:T(8,128)S(1)}, f32[6,16,128]{2,1,0:T(8,128)}, u32[]{:S(2)}) copy-start(f32[6,16,128]{2,1,0:T(8,128)} %param.6) | copy-start | bytes 147460
  8.5 33.7 %collective-permute-start.5 = (bf16[42,16,256]{2,1,0:T(8,128)(2,1)}, bf16[42,16,256]{2,1,0:T(8,128)(2,1)S(1)}, u32[]{:S(2)}, u32[]{:S(2)}) collective-permute-start(bf16[42,16,256]{2,1,0:T(8,128)(2,1)} %get-tuple-element.31), channel_id=1, source_target_pairs={{1,0},{2,1},{3,2},{4,3},{5,4},{6,5},{7,6},{8,7},{9,8},{10,9},{11,1... | collective-permute-start | bytes 1032200 | tf_op jit(solution)/shard_map/ppermute | solution.py:456
  13.0 30.6 %collective-permute-start.2 = (bf16[42,16,256]{2,1,0:T(8,128)(2,1)}, bf16[42,16,256]{2,1,0:T(8,128)(2,1)S(1)}, u32[]{:S(2)}, u32[]{:S(2)}) collective-permute-start(bf16[42,16,256]{2,1,0:T(8,128)(2,1)} %get-tuple-element.25), channel_id=1, source_target_pairs={{0,1},{1,2},{2,3},{3,4},{4,5},{5,6},{6,7},{7,8},{8,9},{9,10},{10,1... | collective-permute-start | bytes 1032200 | tf_op jit(solution)/shard_map/ppermute | solution.py:455
  17.6 14.3 %collective-permute-start = (f32[6,8,128]{2,1,0:T(8,128)S(1)}, f32[6,8,128]{2,1,0:T(8,128)S(1)}, u32[]{:S(2)}, u32[]{:S(2)}) collective-permute-start(f32[6,8,128]{2,1,0:T(8,128)S(1)} %get-tuple-element.46), channel_id=1, source_target_pairs={{0,1},{1,2},{2,3},{3,4},{4,5},{5,6},{6,7},{7,8},{8,9},{9,10},{10,1... | collective-permute-start | bytes 73736 | tf_op jit(solution)/shard_map/ppermute | solution.py:432
  21.8 14.4 %collective-permute-start.1 = (f32[6,8,128]{2,1,0:T(8,128)S(1)}, f32[6,8,128]{2,1,0:T(8,128)S(1)}, u32[]{:S(2)}, u32[]{:S(2)}) collective-permute-start(f32[6,8,128]{2,1,0:T(8,128)S(1)} %get-tuple-element.47), channel_id=1, source_target_pairs={{1,0},{2,1},{3,2},{4,3},{5,4},{6,5},{7,6},{8,7},{9,8},{10,9},{11,1... | collective-permute-start | bytes 73736 | tf_op jit(solution)/shard_map/ppermute | solution.py:433
  26.8 9.5 %copy-start.18 = (bf16[42,16,256]{2,1,0:T(8,128)(2,1)S(1)}, bf16[42,16,256]{2,1,0:T(8,128)(2,1)}, u32[]{:S(2)}) copy-start(bf16[42,16,256]{2,1,0:T(8,128)(2,1)} %get-tuple-element.37) | copy-start | bytes 1032196
  26.8 18.1 %copy-start.19 = (s32[128]{0:T(128)S(1)}, s32[128]{0:T(128)}, u32[]{:S(2)}) copy-start(s32[128]{0:T(128)} %param.9) | copy-start | bytes 1540
  31.8 72.7 %collective-permute-start.8 = (bf16[42,16,256]{2,1,0:T(8,128)(2,1)}, bf16[42,16,256]{2,1,0:T(8,128)(2,1)S(1)}, u32[]{:S(2)}, u32[]{:S(2)}) collective-permute-start(bf16[42,16,256]{2,1,0:T(8,128)(2,1)} %get-tuple-element.36), channel_id=1, source_target_pairs={{0,1},{1,2},{2,3},{3,4},{4,5},{5,6},{6,7},{7,8},{8,9},{9,10},{10,1... | collective-permute-start | bytes 1032200 | tf_op jit(solution)/shard_map/ppermute | solution.py:455
  36.2 68.3 %collective-permute-start.9 = (bf16[42,16,256]{2,1,0:T(8,128)(2,1)S(1)}, bf16[42,16,256]{2,1,0:T(8,128)(2,1)S(1)}, u32[]{:S(2)}, u32[]{:S(2)}) collective-permute-start(bf16[42,16,256]{2,1,0:T(8,128)(2,1)S(1)} %copy-done.18), channel_id=1, source_target_pairs={{1,0},{2,1},{3,2},{4,3},{5,4},{6,5},{7,6},{8,7},{9,8},{10,9},{11,1... | collective-permute-start | bytes 1032200 | tf_op jit(solution)/shard_map/ppermute | solution.py:456
  37.5 13.6 %copy-start.5 = (bf16[42,16,256]{2,1,0:T(8,128)(2,1)}, bf16[42,16,256]{2,1,0:T(8,128)(2,1)S(1)}, u32[]{:S(2)}) copy-start(bf16[42,16,256]{2,1,0:T(8,128)(2,1)S(1)} %collective-permute-done.4.low_ref) | copy-start | bytes 1032196
  37.6 51.6 %collective-permute-start.6 = (bf16[42,16,256]{2,1,0:T(8,128)(2,1)}, bf16[42,16,256]{2,1,0:T(8,128)(2,1)S(1)}, u32[]{:S(2)}, u32[]{:S(2)}) collective-permute-start(bf16[42,16,256]{2,1,0:T(8,128)(2,1)} %get-tuple-element.33), channel_id=1, source_target_pairs={{0,1},{1,2},{2,3},{3,4},{4,5},{5,6},{6,7},{7,8},{8,9},{9,10},{10,1... | collective-permute-start | bytes 1032200 | tf_op jit(solution)/shard_map/ppermute | solution.py:455
  42.2 8.9 %copy-start.6 = (bf16[42,16,256]{2,1,0:T(8,128)(2,1)}, bf16[42,16,256]{2,1,0:T(8,128)(2,1)S(1)}, u32[]{:S(2)}) copy-start(bf16[42,16,256]{2,1,0:T(8,128)(2,1)S(1)} %collective-permute-done.5.high_ref) | copy-start | bytes 1032196
  42.2 47.0 %collective-permute-start.7 = (bf16[42,16,256]{2,1,0:T(8,128)(2,1)}, bf16[42,16,256]{2,1,0:T(8,128)(2,1)S(1)}, u32[]{:S(2)}, u32[]{:S(2)}) collective-permute-start(bf16[42,16,256]{2,1,0:T(8,128)(2,1)} %get-tuple-element.34), channel_id=1, source_target_pairs={{1,0},{2,1},{3,2},{4,3},{5,4},{6,5},{7,6},{8,7},{9,8},{10,9},{11,1... | collective-permute-start | bytes 1032200 | tf_op jit(solution)/shard_map/ppermute | solution.py:456
  43.6 21.3 %copy-start.4 = (bf16[42,16,256]{2,1,0:T(8,128)(2,1)}, bf16[42,16,256]{2,1,0:T(8,128)(2,1)S(1)}, u32[]{:S(2)}) copy-start(bf16[42,16,256]{2,1,0:T(8,128)(2,1)S(1)} %collective-permute-done.2.low_ref) | copy-start | bytes 1032196
  43.6 31.1 %collective-permute-start.3 = (bf16[42,16,256]{2,1,0:T(8,128)(2,1)}, bf16[42,16,256]{2,1,0:T(8,128)(2,1)S(1)}, u32[]{:S(2)}, u32[]{:S(2)}) collective-permute-start(bf16[42,16,256]{2,1,0:T(8,128)(2,1)} %get-tuple-element.26), channel_id=1, source_target_pairs={{1,0},{2,1},{3,2},{4,3},{5,4},{6,5},{7,6},{8,7},{9,8},{10,9},{11,1... | collective-permute-start | bytes 1032200 | tf_op jit(solution)/shard_map/ppermute | solution.py:456
  74.7 0.7 copy-start.11
  74.7 76.5 %collective-permute-start.16 = (bf16[6,16,16,256]{3,2,1,0:T(8,128)(2,1)}, bf16[6,16,16,256]{3,2,1,0:T(8,128)(2,1)S(1)}, u32[]{:S(2)}, u32[]{:S(2)}) collective-permute-start(bf16[6,16,16,256]{3,2,1,0:T(8,128)(2,1)} %get-tuple-element.41.refs_1_), channel_id=1, source_target_pairs={{16,0},{0,16},{17,1},{1,17},{18,2},{2,18},{19,3},{3,19},{20,4},{4,... | collective-permute-start | bytes 2359304 | tf_op jit(solution)/shard_map/ppermute | solution.py:403
  89.2 0.8 copy-start.9
  89.2 62.0 %collective-permute-start.15 = (bf16[6,16,16,256]{3,2,1,0:T(8,128)(2,1)}, bf16[6,16,16,256]{3,2,1,0:T(8,128)(2,1)S(1)}, u32[]{:S(2)}, u32[]{:S(2)}) collective-permute-start(bf16[6,16,16,256]{3,2,1,0:T(8,128)(2,1)} %get-tuple-element.40.refs_0_), channel_id=1, source_target_pairs={{16,0},{0,16},{17,1},{1,17},{18,2},{2,18},{19,3},{3,19},{20,4},{4,... | collective-permute-start | bytes 2359304 | tf_op jit(solution)/shard_map/ppermute | solution.py:403
  89.9 0.7 copy-start.10
  104.4 15.8 %copy-start.16 = (f32[16,128]{1,0:T(8,128)S(1)}, f32[16,128]{1,0:T(8,128)}, u32[]{:S(2)}) copy-start(f32[16,128]{1,0:T(8,128)} %get-tuple-element.29) | copy-start | bytes 24580
  104.4 15.8 %copy-start.15 = (f32[16,128]{1,0:T(8,128)S(1)}, f32[16,128]{1,0:T(8,128)}, u32[]{:S(2)}) copy-start(f32[16,128]{1,0:T(8,128)} %get-tuple-element.32) | copy-start | bytes 24580
  104.4 15.8 %copy-start.17 = (f32[16,128]{1,0:T(8,128)S(1)}, f32[16,128]{1,0:T(8,128)}, u32[]{:S(2)}) copy-start(f32[16,128]{1,0:T(8,128)} %get-tuple-element.35) | copy-start | bytes 24580
  104.4 46.8 %collective-permute-start.17 = (bf16[6,16,16,256]{3,2,1,0:T(8,128)(2,1)}, bf16[6,16,16,256]{3,2,1,0:T(8,128)(2,1)S(1)}, u32[]{:S(2)}, u32[]{:S(2)}) collective-permute-start(bf16[6,16,16,256]{3,2,1,0:T(8,128)(2,1)} %get-tuple-element.42.refs_2_), channel_id=1, source_target_pairs={{16,0},{0,16},{17,1},{1,17},{18,2},{2,18},{19,3},{3,19},{20,4},{4,... | collective-permute-start | bytes 2359304 | tf_op jit(solution)/shard_map/ppermute | solution.py:403
  104.5 0.7 copy-start.7
  105.2 0.7 copy-start.8
  119.7 31.5 %collective-permute-start.18 = (bf16[6,16,16,256]{3,2,1,0:T(8,128)(2,1)}, bf16[6,16,16,256]{3,2,1,0:T(8,128)(2,1)S(1)}, u32[]{:S(2)}, u32[]{:S(2)}) collective-permute-start(bf16[6,16,16,256]{3,2,1,0:T(8,128)(2,1)} %get-tuple-element.43.refs_3_), channel_id=1, source_target_pairs={{16,0},{0,16},{17,1},{1,17},{18,2},{2,18},{19,3},{3,19},{20,4},{4,... | collective-permute-start | bytes 2359304 | tf_op jit(solution)/shard_map/ppermute | solution.py:403
  120.9 1.4 copy-start.13
  120.9 1.4 collective-permute-start.10
  122.3 0.6 copy-start.14
  124.6 4.7 %collective-permute-start.11 = (f32[136,128]{1,0:T(8,128)}, f32[136,128]{1,0:T(8,128)S(1)}, u32[]{:S(2)}, u32[]{:S(2)}) collective-permute-start(f32[136,128]{1,0:T(8,128)} %gram.1), channel_id=1, source_target_pairs={{0,1},{1,0},{2,3},{3,2},{4,5},{5,4},{6,7},{7,6},{8,9},{9,8},{10,11... | collective-permute-start | bytes 208904 | tf_op jit(solution)/shard_map/ppermute | solution.py:395
  130.2 4.4 %collective-permute-start.12 = (f32[136,128]{1,0:T(8,128)S(1)}, f32[136,128]{1,0:T(8,128)S(1)}, u32[]{:S(2)}, u32[]{:S(2)}) collective-permute-start(f32[136,128]{1,0:T(8,128)S(1)} %add.12), channel_id=1, source_target_pairs={{0,2},{1,3},{2,0},{3,1},{4,6},{5,7},{6,4},{7,5},{8,10},{9,11},{10,... | collective-permute-start | bytes 208904 | tf_op jit(solution)/shard_map/ppermute | solution.py:395
  134.6 4.4 %collective-permute-start.13 = (f32[136,128]{1,0:T(8,128)S(1)}, f32[136,128]{1,0:T(8,128)S(1)}, u32[]{:S(2)}, u32[]{:S(2)}) collective-permute-start(f32[136,128]{1,0:T(8,128)S(1)} %add.13), channel_id=1, source_target_pairs={{0,4},{1,5},{2,6},{3,7},{4,0},{5,1},{6,2},{7,3},{8,12},{9,13},{10,... | collective-permute-start | bytes 208904 | tf_op jit(solution)/shard_map/ppermute | solution.py:395
  139.0 5.3 %collective-permute-start.14 = (f32[136,128]{1,0:T(8,128)S(1)}, f32[136,128]{1,0:T(8,128)S(1)}, u32[]{:S(2)}, u32[]{:S(2)}) collective-permute-start(f32[136,128]{1,0:T(8,128)S(1)} %add.14), channel_id=1, source_target_pairs={{0,8},{1,9},{2,10},{3,11},{4,12},{5,13},{6,14},{7,15},{8,0},{9,1},... | collective-permute-start | bytes 208904 | tf_op jit(solution)/shard_map/ppermute | solution.py:395
  151.2 0.9 copy-start
  151.2 1.1 copy-start.1
  151.2 1.4 copy-start.2
  151.2 1.6 copy-start.3

commit v3 on v2

--- a/solution.py
+++ b/solution.py
@@ -6,6 +6,7 @@
 from jax.experimental import pallas as pl
 from jax.experimental.pallas import tpu as pltpu
 from jax.sharding import PartitionSpec as P
+
 
 ITERS = 4
 DEPTH = 2 * ITERS
@@ -36,14 +37,39 @@
     return rows
 
 
+def turn(src_ref, src_row, stride, turned, base, tile_rows):
+    pitch = GROUP + 1
+    for k in range(GROUP):
+        for r in range(0, tile_rows, 8):
+            turned[pl.ds(base + r * pitch + k, 8, stride=pitch), :] = src_ref[
+                pl.ds(k * stride + src_row + r, 8), :
+            ]
+
+
+def turned_row(turned, base, r):
+    pitch = GROUP + 1
+    return jnp.concatenate(
+        [turned[pl.ds(base + r * pitch + 8 * kg, 8, stride=1), :] for kg in range(GROUP // 8)],
+        axis=0,
+    )
+
+
+def turned_size(tile_rows):
+    return tile_rows * (GROUP + 1) + 8
+
+
 def pack_kernel(*refs, tile_rows):
-    cov_refs, up_ref, down_ref = refs[:-2], refs[-2], refs[-1]
+    cov_refs, (up_ref, down_ref, turned) = refs[:-3], refs[-3:]
     stride = 6 * tile_rows
+    size = turned_size(tile_rows)
+    groups = len(cov_refs)
+    for f in range(6):
+        for c in range(groups):
+            turn(cov_refs[c], f * tile_rows, stride, turned, (f * groups + c) * size, tile_rows)
 
     def row(field, r):
         return jnp.concatenate(
-            [ref[pl.ds(field * tile_rows + r, GROUP, stride=stride), :] for ref in cov_refs],
-            axis=1,
+            [turned_row(turned, (field * groups + c) * size, r) for c in range(groups)], axis=1
         )
 
     for i, (field, d) in enumerate(halo_rows()):
@@ -141,7 +167,7 @@
     where_ref, low_ref, high_ref, wet_ref, coef_ref, stations_ref, *refs,
     tile_rows, grid_rows,
 ):
-    cov_refs, (pf_out, sensed_out, state_a, state_b, press, flux) = refs[:-6], refs[-6:]
+    cov_refs, (pf_out, sensed_out, state_a, state_b, press, flux, turned) = refs[:-7], refs[-7:]
     first_row = where_ref[0]
     ext = tile_rows + 2 * DEPTH
     groups = len(cov_refs)
@@ -160,15 +186,13 @@
         rows = ref.shape[0] // groups
         return [ref[pl.ds(c * rows + index * ext + r, 8, stride=0), :] for c in range(groups)]
 
-    def fill(r, carry):
-        for f in range(6):
-            for c in range(groups):
-                state_a[f, DEPTH + r, :, pl.ds(128 * c, 128)] = cov_refs[c][
-                    pl.ds(f * tile_rows + r, GROUP, stride=stride), :
-                ]
-        return carry
-
-    lax.fori_loop(0, tile_rows, fill, 0)
+    size = turned_size(tile_rows)
+    for f in range(6):
+        for c in range(groups):
+            base = (f * groups + c) * size
+            turn(cov_refs[c], f * tile_rows, stride, turned, base, tile_rows)
+            for r in range(tile_rows):
+                state_a[f, DEPTH + r, :, pl.ds(128 * c, 128)] = turned_row(turned, base, r)
     for i, (field, d) in enumerate(halo_rows()):
         state_a[field, DEPTH - d] = low_ref[i].astype(f32)
         state_a[field, DEPTH + tile_rows + d - 1] = high_ref[i].astype(f32)
@@ -187,7 +211,7 @@
     lax.fori_loop(0, ext, first_press, 0, unroll=2)
     lane = lax.broadcasted_iota(jnp.int32, (8, 128), 1)
 
-    def move(t, src, dst, r_first, count):
+    def move(t, src, dst, r_first, count, edge=False):
         stores = []
         for r in [r_first + k for k in range(count)]:
             wet_a, wet_b, wet_c = (spread(wet_ref, q, r) for q in range(3))
@@ -199,6 +223,15 @@
                     v = at(src, 3 * layer + 2, r, kg)
                     before = at(press, layer, r - 1, kg)
                     after = at(press, layer, r + 1, kg)
+                    if edge:
+                        u_new, along = [], []
+                        for c in range(groups):
+                            u_c = (
+                                wet_a[c] * u[c] + wet_b[c] * v[c] - wet_c[c] * (after[c] - before[c])
+                            )
+                            along.append(depth[c] * u_c + h[c] * mu[c])
+                        stores.append((flux, layer, r, kg, along))
+                        continue
                     slope = lane_steps(at(press, layer, r, kg), lane)
                     u_new, v_new, along, cross = [], [], [], []
                     for c in range(groups):
@@ -242,23 +275,23 @@
 
     src, dst = state_a, state_b
     for t in range(ITERS):
-        first = 2 * t + 1
-        n_move = ext - 4 * t - 2
-        pace = 2 if n_move % 2 == 0 else 1
+        first = 2 * t + 2
+        rows = ext - 4 * t - 4
+        pace = 4 if rows % 4 == 0 else (2 if rows % 2 == 0 else 1)
+        move(t, src, dst, first - 1, 1, edge=True)
+        move(t, src, dst, first + rows, 1, edge=True)
 
         def move_body(i, carry, t=t, src=src, dst=dst, first=first, pace=pace):
             move(t, src, dst, first + pace * i, pace)
             return carry
 
-        lax.fori_loop(0, n_move // pace, move_body, 0)
-        n_rise = n_move - 2
-        pace_rise = 4 if n_rise % 4 == 0 else (2 if n_rise % 2 == 0 else 1)
-
-        def rise_body(i, carry, t=t, dst=dst, first=first, pace=pace_rise):
-            rise(t, dst, first + 1 + pace * i, pace)
+        lax.fori_loop(0, rows // pace, move_body, 0)
+
+        def rise_body(i, carry, t=t, dst=dst, first=first, pace=pace):
+            rise(t, dst, first + pace * i, pace)
             return carry
 
-        lax.fori_loop(0, n_rise // pace_rise, rise_body, 0)
+        lax.fori_loop(0, rows // pace, rise_body, 0)
         src, dst = dst, src
 
     n_stations = stations_ref.shape[1]
@@ -280,31 +313,40 @@
 
 
 def gram_kernel(where_ref, weight_ref, innov_ref, *refs, columns):
-    sensed_refs, out_ref, both = refs[:-2], refs[-2], refs[-1]
+    sensed_refs, out_ref, both, left = refs[:-3], refs[-3], refs[-2], refs[-1]
     index = where_ref[1]
-    count = len(sensed_refs)
+    count = both.shape[0] // columns
+    each = len(sensed_refs) // count
     for d in range(count):
         start = pl.multiple_of(lax.rem(index + d, count) * columns, 8)
-        both[pl.ds(start, columns), :] = sensed_refs[d][...] * weight_ref[...]
-    total = count * columns
-    both[pl.ds(total, 8), :] = innov_ref[...]
+        for ref in sensed_refs[d * each : (d + 1) * each]:
+            size = ref.shape[0]
+            both[pl.ds(start, size), :] = ref[...] * weight_ref[...]
+            start = pl.multiple_of(start + size, 8)
+    left[pl.ds(0, columns), :] = both[pl.ds(pl.multiple_of(index * columns, 8), columns), :]
+    left[pl.ds(columns, 8), :] = innov_ref[...]
     out_ref[...] = lax.dot_general(
+        left[...],
         both[...],
-        both[pl.ds(0, total), :],
         (((1,), (1,)), ((), ())),
         precision=lax.Precision.HIGHEST,
         preferred_element_type=f32,
     )
 
 
-def factor_kernel(where_ref, gram_ref, mix_out, scr, *, columns):
+def factor_kernel(where_ref, *refs, columns):
+    gram_refs, mix_out, scr = refs[:-2], refs[-2], refs[-1]
     index = where_ref[1]
-    total = gram_ref.shape[1]
+    count = len(gram_refs)
+    total = count * columns
+    for d in range(count):
+        start = pl.multiple_of(lax.rem(index + d, count) * columns, 8)
+        scr[pl.ds(start, columns), :] = gram_refs[d][pl.ds(0, columns), :]
     blocks = total // 8
     lane = lax.broadcasted_iota(jnp.int32, (8, total), 1)
     sub = lax.broadcasted_iota(jnp.int32, (8, total), 0)
     eye = [(lane == sub + 8 * b).astype(f32) for b in range(blocks)]
-    m = [gram_ref[pl.ds(8 * b, 8), :] + eye[b] for b in range(blocks)]
+    m = [scr[pl.ds(8 * b, 8), :] + eye[b] for b in range(blocks)]
     w = list(eye)
 
     def column(x, j):
@@ -339,7 +381,7 @@
             tails = [column(m[q], 8 * b + i) for i in range(8)]
             m[q] = m[q] - tree_sum([tails[i] * rows_m[i] for i in range(8)])
             w[q] = w[q] - tree_sum([tails[i] * rows_w[i] for i in range(8)])
-    target = gram_ref[pl.ds(total, 1), :]
+    target = gram_refs[0][pl.ds(columns, 1), :]
     weights = jnp.zeros((8, total), f32)
     for b in range(blocks):
         scr[pl.ds(8 * b, 8), :] = scaled[b]
@@ -364,26 +406,30 @@
 
 
 def mix_kernel(where_ref, mix_ref, mean_ref, *refs, columns):
-    piece_refs, cov_out, mean_out, scr = refs[:-3], refs[-3], refs[-2], refs[-1]
+    piece_refs, (cov_out, mean_out, scr, turned) = refs[:-4], refs[-4:]
     tile_rows, cells = mean_ref.shape[1:]
+    groups = cells // 128
     piece = mean_out.shape[2]
-    group = pl.program_id(1)
     mix = mix_ref[...]
-    cov_flat = cov_out.reshape(columns * tile_rows, 128)
+    pitch = tile_rows + 1
     for r in range(tile_rows):
         stack = jnp.concatenate([ref[0, r] for ref in piece_refs], axis=0)
         result = jnp.dot(mix, stack, preferred_element_type=f32)
-        cov_flat[pl.ds(r, columns, stride=tile_rows), :] = result[:columns]
-        scr[group, pl.ds(r, 1), :] = (
-            result[columns : columns + 1] + result[columns + 1 : columns + 2]
-        )
-
-    @pl.when(group == pl.num_programs(1) - 1)
-    def _():
-        change = jnp.concatenate([scr[c] for c in range(cells // 128)], axis=1)
-        whole = mean_ref[0] + change
-        shift = lax.rem(cells - where_ref[1] * piece, cells)
-        mean_out[0] = pltpu.roll(whole, shift, 1)[:, :piece]
+        for c in range(groups):
+            for j in range(0, columns, 8):
+                turned[c, pl.ds(j * pitch + r, 8, stride=pitch), :] = result[
+                    j : j + 8, 128 * c : 128 * c + 128
+                ]
+        scr[pl.ds(r, 1), :] = result[columns : columns + 1] + result[columns + 1 : columns + 2]
+    for j in range(columns):
+        for c in range(groups):
+            for r in range(0, tile_rows, 8):
+                cov_out[j, 0, pl.ds(r, 8), pl.ds(128 * c, 128)] = turned[
+                    c, pl.ds(j * pitch + r, 8, stride=1), :
+                ]
+    whole = mean_ref[0] + scr[...]
+    shift = lax.rem(cells - where_ref[1] * piece, cells)
+    mean_out[0] = pltpu.roll(whole, shift, 1)[:, :piece]
 
 
 def spread_sum(value, axis):
@@ -409,6 +455,12 @@
     return pl.BlockSpec(shape, lambda *_: (0,) * len(shape))
 
 
+def chunk_list(count):
+    if count < 3:
+        return [(g, 1) for g in range(count)]
+    return [(0, 1), (1, count - 2), (count - 1, 1)]
+
+
 def local(mean_state, covariance, land_mask, stations, observed, obs_weight):
     columns, _, tile_rows, cells = covariance.shape
     piece = mean_state.shape[2]
@@ -418,7 +470,7 @@
     grid_rows = tile_rows * n_space
     ext = tile_rows + 2 * DEPTH
     n_stations = stations.shape[0]
-    chunks = columns // GROUP
+    chunks = chunk_list(columns // GROUP)
     n_halo = len(halo_rows())
     groups = cells // 128
     space_index = lax.axis_index("space")
@@ -438,26 +490,29 @@
     span = GROUP * 6 * tile_rows
 
 
-    def cov_specs(c):
-        return [pl.BlockSpec((span, 128), lambda i, g=g: (c, g)) for g in range(groups)]
-
+    def cov_specs(start):
+        return [pl.BlockSpec((span, 128), lambda i, g=g: (start + i, g)) for g in range(groups)]
+
+    halo_spec = pl.BlockSpec((n_halo, GROUP, cells), lambda i: (0, i, 0))
     lows, highs = [], []
-    for c in range(chunks):
-        halo_shape = jax.ShapeDtypeStruct((n_halo, GROUP, cells), bf16)
+    source = flat
+    for start, size in chunks:
+        halo_shape = jax.ShapeDtypeStruct((n_halo, size * GROUP, cells), bf16)
         going_up, going_down = pl.pallas_call(
             functools.partial(pack_kernel, tile_rows=tile_rows),
-            grid=(1,),
-            in_specs=cov_specs(c),
-            out_specs=[whole_spec((n_halo, GROUP, cells))] * 2,
+            grid=(size,),
+            in_specs=cov_specs(start),
+            out_specs=[halo_spec] * 2,
             out_shape=[halo_shape, halo_shape],
-            name=f"pack_{c}",
-        )(*[flat] * groups)
+            scratch_shapes=[pltpu.VMEM((6 * groups * turned_size(tile_rows), 128), f32)],
+        )(*[source] * groups)
+        source, going_up, going_down = lax.optimization_barrier((flat, going_up, going_down))
         lows.append(lax.ppermute(going_up, "space", up))
         highs.append(lax.ppermute(going_down, "space", down))
 
     station_row = (stations - first_row * cells).astype(jnp.int32)[None, :]
     weight_row = obs_weight[None, :]
-    wet, coef, mean_final, innovation = pl.pallas_call(
+    mean_run = pl.pallas_call(
         functools.partial(mean_kernel, tile_rows=tile_rows, grid_rows=grid_rows),
         in_specs=[smem] + [pl.BlockSpec(memory_space=pltpu.VMEM)] * 5,
         out_specs=[pl.BlockSpec(memory_space=pltpu.VMEM)] * 4,
@@ -468,75 +523,86 @@
             jax.ShapeDtypeStruct((8, n_stations), f32),
         ],
         name="mean_window",
-    )(where, mean_ext, land_mask, station_row, observed[None, :], weight_row)
+    )
+    wet, coef, mean_final, innovation = mean_run(
+        where, mean_ext, land_mask, station_row, observed[None, :], weight_row
+    )
 
     forecasts, sensed = [], []
-    for c in range(chunks):
-        pf, s = pl.pallas_call(
+    for c, (start, size) in enumerate(chunks):
+        window = pl.pallas_call(
             functools.partial(window_kernel, tile_rows=tile_rows, grid_rows=grid_rows),
-            grid=(1,),
+            grid=(size,),
             in_specs=[
                 smem,
-                whole_spec((n_halo, GROUP, cells)),
-                whole_spec((n_halo, GROUP, cells)),
+                halo_spec,
+                halo_spec,
                 whole_spec((groups * 3 * ext, 128)),
                 whole_spec((groups * ITERS * 6 * ext, 128)),
                 whole_spec((1, n_stations)),
             ]
-            + cov_specs(c),
+            + cov_specs(start),
             out_specs=[
-                whole_spec((6, tile_rows, GROUP, cells)),
-                whole_spec((GROUP, n_stations)),
+                pl.BlockSpec((6, tile_rows, GROUP, cells), lambda i: (0, 0, i, 0)),
+                pl.BlockSpec((GROUP, n_stations), lambda i: (i, 0)),
             ],
             out_shape=[
-                jax.ShapeDtypeStruct((6, tile_rows, GROUP, cells), bf16),
-                jax.ShapeDtypeStruct((GROUP, n_stations), f32),
+                jax.ShapeDtypeStruct((6, tile_rows, size * GROUP, cells), bf16),
+                jax.ShapeDtypeStruct((size * GROUP, n_stations), f32),
             ],
-            scratch_shapes=[pltpu.VMEM((n, ext, GROUP, cells), f32) for n in (6, 6, 2, 2)],
-            name=f"window_{c}",
-        )(where, lows[c], highs[c], wet, coef, station_row, *[flat] * groups)
+            scratch_shapes=[pltpu.VMEM((n, ext, GROUP, cells), f32) for n in (6, 6, 2, 2)]
+            + [pltpu.VMEM((6 * groups * turned_size(tile_rows), 128), f32)],
+        )
+        pf, s = window(where, lows[c], highs[c], wet, coef, station_row, *[flat] * groups)
         forecasts.append(shifted(pf, "cols"))
-        sensed.append(s)
-
-    sensed_all = shifted(jnp.concatenate(sensed, axis=0), "cols")
+        sensed.append(shifted(s, "cols"))
+
+    sensed_all = [sensed[c][d] for d in range(n_cols) for c in range(len(chunks))]
     gram = pl.pallas_call(
         functools.partial(gram_kernel, columns=columns),
-        in_specs=[smem] + [pl.BlockSpec(memory_space=pltpu.VMEM)] * (2 + n_cols),
+        in_specs=[smem] + [pl.BlockSpec(memory_space=pltpu.VMEM)] * (2 + len(sensed_all)),
         out_specs=pl.BlockSpec(memory_space=pltpu.VMEM),
-        out_shape=jax.ShapeDtypeStruct((total + 8, total), f32),
-        scratch_shapes=[pltpu.VMEM((total + 8, n_stations), f32)],
+        out_shape=jax.ShapeDtypeStruct((columns + 8, total), f32),
+        scratch_shapes=[
+            pltpu.VMEM((total, n_stations), f32),
+            pltpu.VMEM((columns + 8, n_stations), f32),
+        ],
         name="gram",
     )(where, weight_row, innovation, *sensed_all)
-    gram = spread_sum(gram, "space")
+    gram_all = shifted(spread_sum(gram, "space"), "cols")
     mix = pl.pallas_call(
         functools.partial(factor_kernel, columns=columns),
-        in_specs=[smem, pl.BlockSpec(memory_space=pltpu.VMEM)],
+        in_specs=[smem] + [pl.BlockSpec(memory_space=pltpu.VMEM)] * n_cols,
         out_specs=pl.BlockSpec(memory_space=pltpu.VMEM),
         out_shape=jax.ShapeDtypeStruct((columns + 16, total), bf16),
         scratch_shapes=[pltpu.VMEM((total, total), f32)],
         name="factor",
-    )(where, gram)
-
-    pieces = [forecasts[c][d] for d in range(n_cols) for c in range(chunks)]
-    field_spec = pl.BlockSpec((1, tile_rows, GROUP, 128), lambda f, g: (f, 0, 0, g))
+    )(where, *gram_all)
+
+    pieces = [forecasts[c][d] for d in range(n_cols) for c in range(len(chunks))]
     updated, mean_out = pl.pallas_call(
         functools.partial(mix_kernel, columns=columns),
-        grid=(6, groups),
+        grid=(6,),
         in_specs=[
             smem,
             whole_spec((columns + 16, total)),
-            pl.BlockSpec((1, tile_rows, cells), lambda f, g: (f, 0, 0)),
+            pl.BlockSpec((1, tile_rows, cells), lambda f: (f, 0, 0)),
         ]
-        + [field_spec] * len(pieces),
+        + [
+            pl.BlockSpec((1, tile_rows, p.shape[2], cells), lambda f: (f, 0, 0, 0)) for p in pieces
+        ],
         out_specs=[
-            pl.BlockSpec((columns, 1, tile_rows, 128), lambda f, g: (0, f, 0, g)),
-            pl.BlockSpec((1, tile_rows, piece), lambda f, g: (f, 0, 0)),
+            pl.BlockSpec((columns, 1, tile_rows, cells), lambda f: (0, f, 0, 0)),
+            pl.BlockSpec((1, tile_rows, piece), lambda f: (f, 0, 0)),
         ],
         out_shape=[
             jax.ShapeDtypeStruct((columns, 6, tile_rows, cells), f32),
             jax.ShapeDtypeStruct((6, tile_rows, piece), f32),
         ],
-        scratch_shapes=[pltpu.VMEM((groups, tile_rows, 128), f32)],
+        scratch_shapes=[
+            pltpu.VMEM((tile_rows, cells), f32),
+            pltpu.VMEM((groups, columns * (tile_rows + 1) + 8, 128), f32),
+        ],
         name="mix",
     )(where, mix, mean_final, *pieces)
     return (mean_out, updated)

time: 166 us -> 163 us (0.982)
  waiting for transfers between devices: 26.7 us -> 52.3 us
  Pallas kernels: 89.7 us -> 66.4 us
  starting transfers between devices: 35.2 us -> 31.1 us
    ppermute x1, waiting for transfers between devices: 1.98 us -> 22.2 us  [local(): mean_low = lax.ppermute(mean_state[:, tile_rows - DEPTH:, :], 'space', up)]
    pallas_call x6 -> x5, Pallas kernels: 69.6 us -> 50.7 us  [the longest x3 39.2 us: local(): window(where, lows[c], highs[c], wet, coef, station_row, *[flat] * groups)]
    ppermute x4 -> x3, waiting for transfers between devices: 0.01 us -> 13.6 us  [local(): lows.append(lax.ppermute(going_up, 'space', up))]
    ppermute x4 -> x3, waiting for transfers between devices: 9.82 us -> 0.01 us  [local(): highs.append(lax.ppermute(going_down, 'space', down))]
    ppermute x4 -> x3, starting transfers between devices: 18.5 us -> 12.9 us  [local(): lows.append(lax.ppermute(going_up, 'space', up))]
    pallas_call x4 -> x3, Pallas kernels: 12.1 us -> 7.79 us  [local(): pl.pallas_call(functools.partial(pack_kernel, tile_rows=tile_rows), grid=...]
    ppermute x4, waiting for transfers between devices: 13.5 us -> 10.8 us  [spread_sum(): lax.ppermute(value, axis, [(i, i ^ step) for i in range(count)])]
    ppermute x5 -> x7, waiting for transfers between devices: 1.42 us -> 3.87 us  [shifted(): lax.ppermute(value, axis, [((i + d) % count, i) for i in range(count)])]
  transfers between devices with their start and end apart: 19 -> 19, of which waited for: 7 -> 10; matrix products, arithmetic and copies ran while one was open for 2% -> 1% of each run, Pallas kernels for 46% -> 21%
where the time goes in v3:
time: 163 us; the launch traced here: 162 us
  Pallas kernels  66.4 us (41%)
  waiting for transfers between devices  52.3 us (32%)
  starting transfers between devices  31.1 us (19%)
  local copies, waits for them, and re-layouts  6.91 us (4%)
  blocking collectives  2.08 us (1%)
  other arithmetic  2.04 us (1%)
    pallas_call x3, Pallas kernels, local(): window(where, lows[c], highs[c], wet, coef, station_row, *[flat] * groups)  39.2 us
    ppermute x1, waiting for transfers between devices, local(): mean_low = lax.ppermute(mean_state[:, tile_rows - DEPTH:, :], 'space', up)  22.2 us
    ppermute x3, waiting for transfers between devices, local(): lows.append(lax.ppermute(going_up, 'space', up))  13.6 us
    ppermute x3, starting transfers between devices, local(): lows.append(lax.ppermute(going_up, 'space', up))  12.9 us
    ppermute x4, waiting for transfers between devices, spread_sum(): lax.ppermute(value, axis, [(i, i ^ step) for i in range(count)])  10.8 us
    pallas_call x1, Pallas kernels, local(): pl.pallas_call(functools.partial(mix_kernel, columns=columns), grid=(6,),...  8.09 us
    pallas_call x3, Pallas kernels, local(): pl.pallas_call(functools.partial(pack_kernel, tile_rows=tile_rows), grid=...  7.79 us
    unnamed x38, local copies, waits for them, and re-layouts  6.9 us
  transfers between devices with their start and end apart: 19, of which 10 were waited for; matrix products, arithmetic and copies ran while one was open for 1% of the time, Pallas kernels for 21%

profile of v3, /device:TPU:0, one launch (start us, length us, event | category | flops | bytes accessed | tf_op | source)
XLA Modules:
  0.0 161.8 jit_solution(16490485672802388608)
XLA Ops:
  0.6 2.4 %shard_map.77 = (bf16[42,16,256]{2,1,0:T(8,128)(2,1)}, bf16[42,16,256]{2,1,0:T(8,128)(2,1)}) custom-call(f32[6144,256]{1,0:T(8,128)} %bitcast.7, f32[6144,256]{1,0:T(8,128)} %bitcast.8), custom_call_target="tpu_custom_call" | custom-call | tf_op jit(solution)/shard_map/pallas_call | solution.py:501
  3.0 3.0 %shard_map.79 = (bf16[42,32,256]{2,1,0:T(8,128)(2,1)}, bf16[42,32,256]{2,1,0:T(8,128)(2,1)}) custom-call(f32[6144,256]{1,0:T(8,128)} %bitcast.9, f32[6144,256]{1,0:T(8,128)} %bitcast.10), custom_call_target="tpu_custom_call" | custom-call | tf_op jit(solution)/shard_map/pallas_call | solution.py:501
  6.0 4.9 %collective-permute-start.4 = (bf16[42,32,256]{2,1,0:T(8,128)(2,1)}, bf16[42,32,256]{2,1,0:T(8,128)(2,1)S(1)}, u32[]{:S(2)}, u32[]{:S(2)}) collective-permute-start(bf16[42,32,256]{2,1,0:T(8,128)(2,1)} %get-tuple-element.39), channel_id=1, source_target_pairs={{0,1},{1,2},{2,3},{3,4},{4,5},{5,6},{6,7},{7,8},{8,9},{9,10},{10,1... | collective-permute-start | bytes 2064392 | tf_op jit(solution)/shard_map/ppermute | solution.py:510
  10.9 1.3 collective-permute-start.5
  12.2 4.5 %collective-permute-start = (f32[6,8,128]{2,1,0:T(8,128)S(1)}, f32[6,8,128]{2,1,0:T(8,128)S(1)}, u32[]{:S(2)}, u32[]{:S(2)}) collective-permute-start(f32[6,8,128]{2,1,0:T(8,128)S(1)} %get-tuple-element.54), channel_id=1, source_target_pairs={{0,1},{1,2},{2,3},{3,4},{4,5},{5,6},{6,7},{7,8},{8,9},{9,10},{10,1... | collective-permute-start | bytes 73736 | tf_op jit(solution)/shard_map/ppermute | solution.py:484
  16.8 1.3 collective-permute-start.1
  18.1 0.6 subtract_bitcast_fusion.stations_ref
  18.7 0.7 pad_add_fusion.where_ref
  19.3 22.2 %collective-permute-done = f32[6,8,128]{2,1,0:T(8,128)S(1)} collective-permute-done((f32[6,8,128]{2,1,0:T(8,128)S(1)}, f32[6,8,128]{2,1,0:T(8,128)S(1)}, u32[]{:S(2)}, u32[]{:S(2)}) %collective-permute-start) | collective-permute-done | bytes 24608 | tf_op jit(solution)/shard_map/ppermute | solution.py:484
  41.5 1.9 %collective-permute-done.1 = f32[6,8,128]{2,1,0:T(8,128)S(1)} collective-permute-done((f32[6,8,128]{2,1,0:T(8,128)S(1)}, f32[6,8,128]{2,1,0:T(8,128)S(1)}, u32[]{:S(2)}, u32[]{:S(2)}) %collective-permute-start.1) | collective-permute-done | bytes 24608 | tf_op jit(solution)/shard_map/ppermute | solution.py:485
  43.5 2.1 %all_gather.3.mean_ref = f32[6,32,256]{2,1,0:T(8,128)} all-gather(f32[6,32,128]{2,1,0:T(8,128)S(1)} %pad_maximum_fusion), channel_id=1, replica_groups=mesh['cols'=2,'space'=16] {'cols'}, dimensions={2}, use_global_device_ids=true | all-gather | bytes 294912 | tf_op jit(solution)/shard_map/all_gather | solution.py:487
  45.6 3.5 %mean_window.1 = (f32[192,128]{1,0:T(8,128)}, f32[1536,128]{1,0:T(8,128)}, f32[6,16,256]{2,1,0:T(8,128)}, f32[8,128]{1,0:T(8,128)}) custom-call(s32[2]{0:T(128)} %pad_add_fusion.where_ref, f32[6,32,256]{2,1,0:T(8,128)} %all_gather.3.mean_ref, s32[256,256]{1,0:T(8,128)} %mask_ref.1, s32[1,128]{1,0:T(1,128)} %subtract_bitcast_fusion.stations_ref, ...), custom_call_target="tpu_custom_call" | custom-call | tf_op jit(solution)/shard_map/mean_window/pallas_call | solution.py:527
  49.1 0.8 copy-done.3
  50.2 18.4 %shard_map.80 = (bf16[6,16,32,256]{3,2,1,0:T(8,128)(2,1)}, f32[32,128]{1,0:T(8,128)}) custom-call(s32[2]{0:T(128)} %pad_add_fusion.where_ref, bf16[42,32,256]{2,1,0:T(8,128)(2,1)} %copy-done.3, bf16[42,32,256]{2,1,0:T(8,128)(2,1)} %copy-done.4, f32[192,128]{1,0:T(8,128)} %get-tuple-element.33.wet_ref, f32[1536,128]{1,0:T(8,128)} %get-tuple-element.34.coef_ref, ...), custom_call_target="tpu_custom_call" | custom-call | tf_op jit(solution)/shard_map/pallas_call | solution.py:556
  68.7 3.4 %collective-permute-start.2 = (bf16[42,16,256]{2,1,0:T(8,128)(2,1)}, bf16[42,16,256]{2,1,0:T(8,128)(2,1)S(1)}, u32[]{:S(2)}, u32[]{:S(2)}) collective-permute-start(bf16[42,16,256]{2,1,0:T(8,128)(2,1)} %get-tuple-element.31), channel_id=1, source_target_pairs={{0,1},{1,2},{2,3},{3,4},{4,5},{5,6},{6,7},{7,8},{8,9},{9,10},{10,1... | collective-permute-start | bytes 1032200 | tf_op jit(solution)/shard_map/ppermute | solution.py:510
  72.1 1.3 collective-permute-start.3
  73.4 2.4 %shard_map.81 = (bf16[42,16,256]{2,1,0:T(8,128)(2,1)}, bf16[42,16,256]{2,1,0:T(8,128)(2,1)}) custom-call(f32[6144,256]{1,0:T(8,128)} %bitcast.13, f32[6144,256]{1,0:T(8,128)} %bitcast.14), custom_call_target="tpu_custom_call" | custom-call | tf_op jit(solution)/shard_map/pallas_call | solution.py:501
  75.8 4.6 %collective-permute-start.6 = (bf16[42,16,256]{2,1,0:T(8,128)(2,1)}, bf16[42,16,256]{2,1,0:T(8,128)(2,1)S(1)}, u32[]{:S(2)}, u32[]{:S(2)}) collective-permute-start(bf16[42,16,256]{2,1,0:T(8,128)(2,1)} %get-tuple-element.45), channel_id=1, source_target_pairs={{0,1},{1,2},{2,3},{3,4},{4,5},{5,6},{6,7},{7,8},{8,9},{9,10},{10,1... | collective-permute-start | bytes 1032200 | tf_op jit(solution)/shard_map/ppermute | solution.py:510
  80.4 1.5 collective-permute-start.7
  81.9 13.6 %collective-permute-done.2.low_ref = bf16[42,16,256]{2,1,0:T(8,128)(2,1)S(1)} collective-permute-done((bf16[42,16,256]{2,1,0:T(8,128)(2,1)}, bf16[42,16,256]{2,1,0:T(8,128)(2,1)S(1)}, u32[]{:S(2)}, u32[]{:S(2)}) %collective-permute-start.2) | collective-permute-done | bytes 344096 | tf_op jit(solution)/shard_map/ppermute | solution.py:510
  95.4 0.7 copy-done.7
  96.2 0.7 copy-done.8
  96.9 10.4 %shard_map.78 = (bf16[6,16,16,256]{3,2,1,0:T(8,128)(2,1)}, f32[16,128]{1,0:T(8,128)}) custom-call(s32[2]{0:T(128)} %pad_add_fusion.where_ref, bf16[42,16,256]{2,1,0:T(8,128)(2,1)} %copy-done.7, bf16[42,16,256]{2,1,0:T(8,128)(2,1)} %copy-done.8, f32[192,128]{1,0:T(8,128)} %get-tuple-element.33.wet_ref, f32[1536,128]{1,0:T(8,128)} %get-tuple-element.34.coef_ref, ...), custom_call_target="tpu_custom_call" | custom-call | tf_op jit(solution)/shard_map/pallas_call | solution.py:556
  107.4 0.7 copy-done.5
  108.2 0.7 copy-done.6
  108.9 10.4 %shard_map.82 = (bf16[6,16,16,256]{3,2,1,0:T(8,128)(2,1)}, f32[16,128]{1,0:T(8,128)}) custom-call(s32[2]{0:T(128)} %pad_add_fusion.where_ref, bf16[42,16,256]{2,1,0:T(8,128)(2,1)} %copy-done.5, bf16[42,16,256]{2,1,0:T(8,128)(2,1)} %copy-done.6, f32[192,128]{1,0:T(8,128)} %get-tuple-element.33.wet_ref, f32[1536,128]{1,0:T(8,128)} %get-tuple-element.34.coef_ref, ...), custom_call_target="tpu_custom_call" | custom-call | tf_op jit(solution)/shard_map/pallas_call | solution.py:556
  119.3 0.5 collective-permute-start.18
  119.8 0.4 collective-permute-start.9
  120.3 1.6 collective-permute-done.8.refs_3_
  121.9 0.4 collective-permute-start.10
  122.3 1.0 collective-permute-done.10.refs_5_
  123.3 0.6 copy-done.16
  123.9 1.7 %gram.1 = f32[72,128]{1,0:T(8,128)} custom-call(s32[2]{0:T(128)} %pad_add_fusion.where_ref, f32[1,128]{1,0:T(1,128)} %bitcast.20, f32[8,128]{1,0:T(8,128)} %get-tuple-element.28.innov_ref, f32[16,128]{1,0:T(8,128)} %get-tuple-element.35.refs_0_, f32[32,128]{1,0:T(8,128)} %get-tuple-element.41.refs_1_, f32[16,128]{1,0:T(8,128)} %get-tuple-element.47.refs_2_, ...), custom_call_target="tpu_custom_call" | custom-call | tf_op jit(solution)/shard_map/gram/pallas_call | solution.py:561
  125.6 2.5 %collective-permute-start.11 = (f32[72,128]{1,0:T(8,128)}, f32[72,128]{1,0:T(8,128)S(1)}, u32[]{:S(2)}, u32[]{:S(2)}) collective-permute-start(f32[72,128]{1,0:T(8,128)} %gram.1), channel_id=1, source_target_pairs={{0,1},{1,0},{2,3},{3,2},{4,5},{5,4},{6,7},{7,6},{8,9},{9,8},{10,11... | collective-permute-start | bytes 110600 | tf_op jit(solution)/shard_map/ppermute | solution.py:441
  128.2 2.2 %collective-permute-done.11 = f32[72,128]{1,0:T(8,128)S(1)} collective-permute-done((f32[72,128]{1,0:T(8,128)}, f32[72,128]{1,0:T(8,128)S(1)}, u32[]{:S(2)}, u32[]{:S(2)}) %collective-permute-start.11) | collective-permute-done | bytes 36896 | tf_op jit(solution)/shard_map/ppermute | solution.py:441
  130.4 0.8 add.12
  131.1 4.0 %collective-permute-done.12 = f32[72,128]{1,0:T(8,128)S(1)} collective-permute-done((f32[72,128]{1,0:T(8,128)S(1)}, f32[72,128]{1,0:T(8,128)S(1)}, u32[]{:S(2)}, u32[]{:S(2)}) %collective-permute-start.12) | collective-permute-done | bytes 36896 | tf_op jit(solution)/shard_map/ppermute | solution.py:441
  135.1 1.6 collective-permute-start.13
  136.7 2.4 %collective-permute-done.13 = f32[72,128]{1,0:T(8,128)S(1)} collective-permute-done((f32[72,128]{1,0:T(8,128)S(1)}, f32[72,128]{1,0:T(8,128)S(1)}, u32[]{:S(2)}, u32[]{:S(2)}) %collective-permute-start.13) | collective-permute-done | bytes 36896 | tf_op jit(solution)/shard_map/ppermute | solution.py:441
  139.1 2.6 %collective-permute-start.14 = (f32[72,128]{1,0:T(8,128)S(1)}, f32[72,128]{1,0:T(8,128)S(1)}, u32[]{:S(2)}, u32[]{:S(2)}) collective-permute-start(f32[72,128]{1,0:T(8,128)S(1)} %add.14), channel_id=1, source_target_pairs={{0,8},{1,9},{2,10},{3,11},{4,12},{5,13},{6,14},{7,15},{8,0},{9,1},... | collective-permute-start | bytes 110600 | tf_op jit(solution)/shard_map/ppermute | solution.py:441
  141.7 2.2 %collective-permute-done.14 = f32[72,128]{1,0:T(8,128)S(1)} collective-permute-done((f32[72,128]{1,0:T(8,128)S(1)}, f32[72,128]{1,0:T(8,128)S(1)}, u32[]{:S(2)}, u32[]{:S(2)}) %collective-permute-start.14) | collective-permute-done | bytes 36896 | tf_op jit(solution)/shard_map/ppermute | solution.py:441
  144.0 1.2 collective-permute-done.15.refs_1_
  145.2 0.6 copy-done.11
  145.8 6.2 %factor.1.mix_ref = bf16[80,128]{1,0:T(8,128)(2,1)} custom-call(s32[2]{0:T(128)} %pad_add_fusion.where_ref, f32[72,128]{1,0:T(8,128)} %copy-done.10, f32[72,128]{1,0:T(8,128)} %copy-done.11), custom_call_target="tpu_custom_call" | custom-call | tf_op jit(solution)/shard_map/factor/pallas_call | solution.py:573
  152.0 0.9 copy-done.1
  152.9 0.3 copy-done.2
  153.2 0.5 copy-done
  153.7 8.1 %mix.1 = (f32[64,6,16,256]{3,2,1,0:T(8,128)}, f32[6,16,128]{2,1,0:T(8,128)}) custom-call(s32[2]{0:T(128)} %pad_add_fusion.where_ref, bf16[80,128]{1,0:T(8,128)(2,1)} %factor.1.mix_ref, f32[6,16,256]{2,1,0:T(8,128)} %get-tuple-element.48.mean_ref, bf16[6,16,16,256]{3,2,1,0:T(8,128)(2,1)} %get-tuple-element.49.refs_0_, ...), custom_call_target="tpu_custom_call" | custom-call | tf_op jit(solution)/shard_map/mix/pallas_call | solution.py:583
  (47 shorter events, 0.7 us)
Async XLA Ops:
  3.0 9.2 %copy-start.9 = (f32[6,16,128]{2,1,0:T(8,128)S(1)}, f32[6,16,128]{2,1,0:T(8,128)}, u32[]{:S(2)}) copy-start(f32[6,16,128]{2,1,0:T(8,128)} %param.6) | copy-start | bytes 147460
  3.0 15.1 %copy-start.18 = (s32[128]{0:T(128)S(1)}, s32[128]{0:T(128)}, u32[]{:S(2)}) copy-start(s32[128]{0:T(128)} %param.9) | copy-start | bytes 1540
  6.0 43.1 %collective-permute-start.4 = (bf16[42,32,256]{2,1,0:T(8,128)(2,1)}, bf16[42,32,256]{2,1,0:T(8,128)(2,1)S(1)}, u32[]{:S(2)}, u32[]{:S(2)}) collective-permute-start(bf16[42,32,256]{2,1,0:T(8,128)(2,1)} %get-tuple-element.39), channel_id=1, source_target_pairs={{0,1},{1,2},{2,3},{3,4},{4,5},{5,6},{6,7},{7,8},{8,9},{9,10},{10,1... | collective-permute-start | bytes 2064392 | tf_op jit(solution)/shard_map/ppermute | solution.py:510
  10.9 38.2 %collective-permute-start.5 = (bf16[42,32,256]{2,1,0:T(8,128)(2,1)}, bf16[42,32,256]{2,1,0:T(8,128)(2,1)S(1)}, u32[]{:S(2)}, u32[]{:S(2)}) collective-permute-start(bf16[42,32,256]{2,1,0:T(8,128)(2,1)} %get-tuple-element.40), channel_id=1, source_target_pairs={{1,0},{2,1},{3,2},{4,3},{5,4},{6,5},{7,6},{8,7},{9,8},{10,9},{11,1... | collective-permute-start | bytes 2064392 | tf_op jit(solution)/shard_map/ppermute | solution.py:511
  12.2 29.3 %collective-permute-start = (f32[6,8,128]{2,1,0:T(8,128)S(1)}, f32[6,8,128]{2,1,0:T(8,128)S(1)}, u32[]{:S(2)}, u32[]{:S(2)}) collective-permute-start(f32[6,8,128]{2,1,0:T(8,128)S(1)} %get-tuple-element.54), channel_id=1, source_target_pairs={{0,1},{1,2},{2,3},{3,4},{4,5},{5,6},{6,7},{7,8},{8,9},{9,10},{10,1... | collective-permute-start | bytes 73736 | tf_op jit(solution)/shard_map/ppermute | solution.py:484
  16.8 26.7 %collective-permute-start.1 = (f32[6,8,128]{2,1,0:T(8,128)S(1)}, f32[6,8,128]{2,1,0:T(8,128)S(1)}, u32[]{:S(2)}, u32[]{:S(2)}) collective-permute-start(f32[6,8,128]{2,1,0:T(8,128)S(1)} %get-tuple-element.55), channel_id=1, source_target_pairs={{1,0},{2,1},{3,2},{4,3},{5,4},{6,5},{7,6},{8,7},{9,8},{10,9},{11,1... | collective-permute-start | bytes 73736 | tf_op jit(solution)/shard_map/ppermute | solution.py:485
  49.1 0.9 copy-start.3
  49.1 1.1 copy-start.4
  50.2 21.9 %copy-start.17 = (bf16[42,16,256]{2,1,0:T(8,128)(2,1)S(1)}, bf16[42,16,256]{2,1,0:T(8,128)(2,1)}, u32[]{:S(2)}) copy-start(bf16[42,16,256]{2,1,0:T(8,128)(2,1)} %get-tuple-element.32) | copy-start | bytes 1032196
  68.5 83.5 %collective-permute-start.17 = (bf16[6,16,32,256]{3,2,1,0:T(8,128)(2,1)}, bf16[6,16,32,256]{3,2,1,0:T(8,128)(2,1)S(1)}, u32[]{:S(2)}, u32[]{:S(2)}) collective-permute-start(bf16[6,16,32,256]{3,2,1,0:T(8,128)(2,1)} %get-tuple-element.50.refs_1_), channel_id=1, source_target_pairs={{16,0},{0,16},{17,1},{1,17},{18,2},{2,18},{19,3},{3,19},{20,4},{4,... | collective-permute-start | bytes 4718600 | tf_op jit(solution)/shard_map/ppermute | solution.py:449
  68.7 26.7 %collective-permute-start.2 = (bf16[42,16,256]{2,1,0:T(8,128)(2,1)}, bf16[42,16,256]{2,1,0:T(8,128)(2,1)S(1)}, u32[]{:S(2)}, u32[]{:S(2)}) collective-permute-start(bf16[42,16,256]{2,1,0:T(8,128)(2,1)} %get-tuple-element.31), channel_id=1, source_target_pairs={{0,1},{1,2},{2,3},{3,4},{4,5},{5,6},{6,7},{7,8},{8,9},{9,10},{10,1... | collective-permute-start | bytes 1032200 | tf_op jit(solution)/shard_map/ppermute | solution.py:510
  72.1 23.3 %collective-permute-start.3 = (bf16[42,16,256]{2,1,0:T(8,128)(2,1)S(1)}, bf16[42,16,256]{2,1,0:T(8,128)(2,1)S(1)}, u32[]{:S(2)}, u32[]{:S(2)}) collective-permute-start(bf16[42,16,256]{2,1,0:T(8,128)(2,1)S(1)} %copy-done.17), channel_id=1, source_target_pairs={{1,0},{2,1},{3,2},{4,3},{5,4},{6,5},{7,6},{8,7},{9,8},{10,9},{11,1... | collective-permute-start | bytes 1032200 | tf_op jit(solution)/shard_map/ppermute | solution.py:511
  75.8 31.6 %collective-permute-start.6 = (bf16[42,16,256]{2,1,0:T(8,128)(2,1)}, bf16[42,16,256]{2,1,0:T(8,128)(2,1)S(1)}, u32[]{:S(2)}, u32[]{:S(2)}) collective-permute-start(bf16[42,16,256]{2,1,0:T(8,128)(2,1)} %get-tuple-element.45), channel_id=1, source_target_pairs={{0,1},{1,2},{2,3},{3,4},{4,5},{5,6},{6,7},{7,8},{8,9},{9,10},{10,1... | collective-permute-start | bytes 1032200 | tf_op jit(solution)/shard_map/ppermute | solution.py:510
  80.4 27.0 %collective-permute-start.7 = (bf16[42,16,256]{2,1,0:T(8,128)(2,1)}, bf16[42,16,256]{2,1,0:T(8,128)(2,1)S(1)}, u32[]{:S(2)}, u32[]{:S(2)}) collective-permute-start(bf16[42,16,256]{2,1,0:T(8,128)(2,1)} %get-tuple-element.46), channel_id=1, source_target_pairs={{1,0},{2,1},{3,2},{4,3},{5,4},{6,5},{7,6},{8,7},{9,8},{10,9},{11,1... | collective-permute-start | bytes 1032200 | tf_op jit(solution)/shard_map/ppermute | solution.py:511
  95.4 0.8 copy-start.7
  96.2 0.7 copy-start.8
  107.3 12.5 %copy-start.14 = (f32[16,128]{1,0:T(8,128)S(1)}, f32[16,128]{1,0:T(8,128)}, u32[]{:S(2)}) copy-start(f32[16,128]{1,0:T(8,128)} %get-tuple-element.35.refs_0_) | copy-start | bytes 24580
  107.3 12.5 %copy-start.12 = (f32[32,128]{1,0:T(8,128)S(1)}, f32[32,128]{1,0:T(8,128)}, u32[]{:S(2)}) copy-start(f32[32,128]{1,0:T(8,128)} %get-tuple-element.41.refs_1_) | copy-start | bytes 49156
  107.3 44.7 %collective-permute-start.16 = (bf16[6,16,16,256]{3,2,1,0:T(8,128)(2,1)}, bf16[6,16,16,256]{3,2,1,0:T(8,128)(2,1)S(1)}, u32[]{:S(2)}, u32[]{:S(2)}) collective-permute-start(bf16[6,16,16,256]{3,2,1,0:T(8,128)(2,1)} %get-tuple-element.49.refs_0_), channel_id=1, source_target_pairs={{16,0},{0,16},{17,1},{1,17},{18,2},{2,18},{19,3},{3,19},{20,4},{4,... | collective-permute-start | bytes 2359304 | tf_op jit(solution)/shard_map/ppermute | solution.py:449
  107.4 0.7 copy-start.5
  108.1 0.7 copy-start.6
  119.3 32.7 %collective-permute-start.18 = (bf16[6,16,16,256]{3,2,1,0:T(8,128)(2,1)}, bf16[6,16,16,256]{3,2,1,0:T(8,128)(2,1)S(1)}, u32[]{:S(2)}, u32[]{:S(2)}) collective-permute-start(bf16[6,16,16,256]{3,2,1,0:T(8,128)(2,1)} %get-tuple-element.51.refs_2_), channel_id=1, source_target_pairs={{16,0},{0,16},{17,1},{1,17},{18,2},{2,18},{19,3},{3,19},{20,4},{4,... | collective-permute-start | bytes 2359304 | tf_op jit(solution)/shard_map/ppermute | solution.py:449
  119.8 2.1 %collective-permute-start.8 = (f32[16,128]{1,0:T(8,128)S(1)}, f32[16,128]{1,0:T(8,128)S(1)}, u32[]{:S(2)}, u32[]{:S(2)}) collective-permute-start(f32[16,128]{1,0:T(8,128)S(1)} %copy-done.14), channel_id=1, source_target_pairs={{16,0},{0,16},{17,1},{1,17},{18,2},{2,18},{19,3},{3,19},{20,4},{4,... | collective-permute-start | bytes 24584 | tf_op jit(solution)/shard_map/ppermute | solution.py:449
  119.8 3.5 %collective-permute-start.9 = (f32[32,128]{1,0:T(8,128)S(1)}, f32[32,128]{1,0:T(8,128)S(1)}, u32[]{:S(2)}, u32[]{:S(2)}) collective-permute-start(f32[32,128]{1,0:T(8,128)S(1)} %copy-done.12), channel_id=1, source_target_pairs={{16,0},{0,16},{17,1},{1,17},{18,2},{2,18},{19,3},{3,19},{20,4},{4,... | collective-permute-start | bytes 49160 | tf_op jit(solution)/shard_map/ppermute | solution.py:449
  121.9 1.4 copy-start.15
  121.9 1.4 collective-permute-start.10
  123.3 0.6 copy-start.16
  123.3 0.6 copy-start.13
  125.6 4.7 %collective-permute-start.11 = (f32[72,128]{1,0:T(8,128)}, f32[72,128]{1,0:T(8,128)S(1)}, u32[]{:S(2)}, u32[]{:S(2)}) collective-permute-start(f32[72,128]{1,0:T(8,128)} %gram.1), channel_id=1, source_target_pairs={{0,1},{1,0},{2,3},{3,2},{4,5},{5,4},{6,7},{7,6},{8,9},{9,8},{10,11... | collective-permute-start | bytes 110600 | tf_op jit(solution)/shard_map/ppermute | solution.py:441
  131.1 4.0 %collective-permute-start.12 = (f32[72,128]{1,0:T(8,128)S(1)}, f32[72,128]{1,0:T(8,128)S(1)}, u32[]{:S(2)}, u32[]{:S(2)}) collective-permute-start(f32[72,128]{1,0:T(8,128)S(1)} %add.12), channel_id=1, source_target_pairs={{0,2},{1,3},{2,0},{3,1},{4,6},{5,7},{6,4},{7,5},{8,10},{9,11},{10,... | collective-permute-start | bytes 110600 | tf_op jit(solution)/shard_map/ppermute | solution.py:441
  135.1 4.0 %collective-permute-start.13 = (f32[72,128]{1,0:T(8,128)S(1)}, f32[72,128]{1,0:T(8,128)S(1)}, u32[]{:S(2)}, u32[]{:S(2)}) collective-permute-start(f32[72,128]{1,0:T(8,128)S(1)} %add.13), channel_id=1, source_target_pairs={{0,4},{1,5},{2,6},{3,7},{4,0},{5,1},{6,2},{7,3},{8,12},{9,13},{10,... | collective-permute-start | bytes 110600 | tf_op jit(solution)/shard_map/ppermute | solution.py:441
  139.1 4.9 %collective-permute-start.14 = (f32[72,128]{1,0:T(8,128)S(1)}, f32[72,128]{1,0:T(8,128)S(1)}, u32[]{:S(2)}, u32[]{:S(2)}) collective-permute-start(f32[72,128]{1,0:T(8,128)S(1)} %add.14), channel_id=1, source_target_pairs={{0,8},{1,9},{2,10},{3,11},{4,12},{5,13},{6,14},{7,15},{8,0},{9,1},... | collective-permute-start | bytes 110600 | tf_op jit(solution)/shard_map/ppermute | solution.py:441
  143.9 1.3 copy-start.10
  143.9 1.3 collective-permute-start.15
  145.2 0.6 copy-start.11
  152.0 0.9 copy-start.1
  152.0 1.2 copy-start.2
  152.0 1.7 %copy-start = (bf16[6,16,32,256]{3,2,1,0:T(8,128)(2,1)}, bf16[6,16,32,256]{3,2,1,0:T(8,128)(2,1)S(1)}, u32[]{:S(2)}) copy-start(bf16[6,16,32,256]{3,2,1,0:T(8,128)(2,1)S(1)} %collective-permute-done.17.refs_4_) | copy-start | bytes 4718596

commit v4 on v3

--- a/solution.py
+++ b/solution.py
@@ -58,8 +58,20 @@
     return tile_rows * (GROUP + 1) + 8
 
 
-def pack_kernel(*refs, tile_rows):
+def pack_kernel(*refs, tile_rows, with_mean):
     cov_refs, (up_ref, down_ref, turned) = refs[:-3], refs[-3:]
+    if with_mean:
+        mean_ref, cov_refs = cov_refs[0], cov_refs[1:]
+        piece = mean_ref.shape[2]
+        for i in range(3):
+            for ref, r in ((up_ref, tile_rows - DEPTH), (down_ref, 0)):
+                value = jnp.concatenate(
+                    [mean_ref[f, pl.ds(r, DEPTH), :] for f in (2 * i, 2 * i + 1)], axis=0
+                )
+                high = value.astype(bf16)
+                low = (value - high.astype(f32)).astype(bf16)
+                ref[len(halo_rows()) + i, :, pl.ds(0, piece)] = high
+                ref[len(halo_rows()) + i, :, pl.ds(128, piece)] = low
     stride = 6 * tile_rows
     size = turned_size(tile_rows)
     groups = len(cov_refs)
@@ -451,6 +463,14 @@
     ]
 
 
+def grant(mib):
+    return pltpu.CompilerParams(vmem_limit_bytes=mib << 20)
+
+
+def in_hbm(value):
+    return pltpu.with_memory_space_constraint(value, pltpu.HBM)
+
+
 def whole_spec(shape):
     return pl.BlockSpec(shape, lambda *_: (0,) * len(shape))
 
@@ -481,11 +501,6 @@
     down = [(i + 1, i) for i in range(n_space - 1)]
     smem = pl.BlockSpec(memory_space=pltpu.SMEM)
 
-    mean_low = lax.ppermute(mean_state[:, tile_rows - DEPTH :, :], "space", up)
-    mean_high = lax.ppermute(mean_state[:, :DEPTH, :], "space", down)
-    mean_ext = jnp.concatenate([mean_low, mean_state, mean_high], axis=1)
-    mean_ext = lax.all_gather(mean_ext, "cols", axis=2, tiled=True)
-
     flat = covariance.reshape(columns * 6 * tile_rows, cells)
     span = GROUP * 6 * tile_rows
 
@@ -496,20 +511,31 @@
     halo_spec = pl.BlockSpec((n_halo, GROUP, cells), lambda i: (0, i, 0))
     lows, highs = [], []
     source = flat
-    for start, size in chunks:
-        halo_shape = jax.ShapeDtypeStruct((n_halo, size * GROUP, cells), bf16)
+    for c, (start, size) in enumerate(chunks):
+        rows = n_halo + 3 if c == 0 else n_halo
+        halo_shape = jax.ShapeDtypeStruct((rows, size * GROUP, cells), bf16)
+        halo_out = pl.BlockSpec((rows, GROUP, cells), lambda i: (0, i, 0))
         going_up, going_down = pl.pallas_call(
-            functools.partial(pack_kernel, tile_rows=tile_rows),
+            functools.partial(pack_kernel, tile_rows=tile_rows, with_mean=c == 0),
             grid=(size,),
-            in_specs=cov_specs(start),
-            out_specs=[halo_spec] * 2,
+            in_specs=[whole_spec(mean_state.shape)] * (c == 0) + cov_specs(start),
+            out_specs=[halo_out] * 2,
             out_shape=[halo_shape, halo_shape],
             scratch_shapes=[pltpu.VMEM((6 * groups * turned_size(tile_rows), 128), f32)],
-        )(*[source] * groups)
+            compiler_params=grant(9),
+        )(*[in_hbm(mean_state)] * (c == 0), *[in_hbm(source)] * groups)
         source, going_up, going_down = lax.optimization_barrier((flat, going_up, going_down))
         lows.append(lax.ppermute(going_up, "space", up))
         highs.append(lax.ppermute(going_down, "space", down))
 
+
+    def mean_halo(payload):
+        parts = payload[n_halo:].astype(f32)
+        value = parts[:, :, :piece] + parts[:, :, 128 : 128 + piece]
+        return value.reshape(6, DEPTH, piece)
+
+    mean_ext = jnp.concatenate([mean_halo(lows[0]), mean_state, mean_halo(highs[0])], axis=1)
+    mean_ext = lax.all_gather(mean_ext, "cols", axis=2, tiled=True)
     station_row = (stations - first_row * cells).astype(jnp.int32)[None, :]
     weight_row = obs_weight[None, :]
     mean_run = pl.pallas_call(
@@ -523,6 +549,7 @@
             jax.ShapeDtypeStruct((8, n_stations), f32),
         ],
         name="mean_window",
+        compiler_params=grant(4),
     )
     wet, coef, mean_final, innovation = mean_run(
         where, mean_ext, land_mask, station_row, observed[None, :], weight_row
@@ -552,6 +579,7 @@
             ],
             scratch_shapes=[pltpu.VMEM((n, ext, GROUP, cells), f32) for n in (6, 6, 2, 2)]
             + [pltpu.VMEM((6 * groups * turned_size(tile_rows), 128), f32)],
+            compiler_params=grant(22),
         )
         pf, s = window(where, lows[c], highs[c], wet, coef, station_row, *[flat] * groups)
         forecasts.append(shifted(pf, "cols"))
@@ -568,6 +596,7 @@
             pltpu.VMEM((columns + 8, n_stations), f32),
         ],
         name="gram",
+        compiler_params=grant(2),
     )(where, weight_row, innovation, *sensed_all)
     gram_all = shifted(spread_sum(gram, "space"), "cols")
     mix = pl.pallas_call(
@@ -577,6 +606,7 @@
         out_shape=jax.ShapeDtypeStruct((columns + 16, total), bf16),
         scratch_shapes=[pltpu.VMEM((total, total), f32)],
         name="factor",
+        compiler_params=grant(2),
     )(where, *gram_all)
 
     pieces = [forecasts[c][d] for d in range(n_cols) for c in range(len(chunks))]
@@ -604,6 +634,7 @@
             pltpu.VMEM((groups, columns * (tile_rows + 1) + 8, 128), f32),
         ],
         name="mix",
+        compiler_params=grant(10),
     )(where, mix, mean_final, *pieces)
     return (mean_out, updated)
 

time: 163 us -> 138 us (0.85)
  Pallas kernels: 66.4 us -> 53.2 us
  starting transfers between devices: 31.1 us -> 25.8 us
  local copies, waits for them, and re-layouts: 6.91 us -> 2.82 us
  other arithmetic: 2.04 us -> 0.14 us
    ppermute x2 -> x0, waiting for transfers between devices: 24.2 us -> none  [the longest x1 22.2 us: local(): mean_low = lax.ppermute(mean_state[:, tile_rows - DEPTH:, :], 'space', up)]
    ppermute x3, waiting for transfers between devices: 13.6 us -> 36.4 us  [local(): lows.append(lax.ppermute(going_up, 'space', up))]
    pallas_call x3, Pallas kernels: 39.2 us -> 32.7 us  [local(): window(where, lows[c], highs[c], wet, coef, station_row, *[flat] * groups)]
    ppermute x2 -> x0, starting transfers between devices: 5.84 us -> none  [the longest x1 4.55 us: local(): mean_low = lax.ppermute(mean_state[:, tile_rows - DEPTH:, :], 'space', up)]
    unnamed x38 -> x16, local copies, waits for them, and re-layouts: 6.9 us -> 2.82 us
    pallas_call x1, Pallas kernels: 8.09 us -> 5.34 us  [local(): pl.pallas_call(functools.partial(mix_kernel, columns=columns), grid=(6,),...]
    ppermute x3, waiting for transfers between devices: 0.01 us -> 2.59 us  [local(): highs.append(lax.ppermute(going_down, 'space', down))]
  transfers between devices with their start and end apart: 19 -> 17, of which waited for: 10 -> 12; matrix products, arithmetic and copies ran while one was open for 1% -> 0% of each run, Pallas kernels for 21% -> 21%
where the time goes in v4:
time: 138 us
  Pallas kernels  53.2 us (39%)
  waiting for transfers between devices  53 us (38%)
  starting transfers between devices  25.8 us (19%)
  local copies, waits for them, and re-layouts  2.82 us (2%)
  blocking collectives  1.95 us (1%)
    ppermute x3, waiting for transfers between devices, local(): lows.append(lax.ppermute(going_up, 'space', up))  36.4 us
    pallas_call x3, Pallas kernels, local(): window(where, lows[c], highs[c], wet, coef, station_row, *[flat] * groups)  32.7 us
    ppermute x3, starting transfers between devices, local(): lows.append(lax.ppermute(going_up, 'space', up))  13.1 us
    ppermute x4, waiting for transfers between devices, spread_sum(): lax.ppermute(value, axis, [(i, i ^ step) for i in range(count)])  10 us
    ppermute x4, starting transfers between devices, spread_sum(): lax.ppermute(value, axis, [(i, i ^ step) for i in range(count)])  7.53 us
    pallas_call x3, Pallas kernels, local(): pl.pallas_call(functools.partial(pack_kernel, tile_rows=tile_rows, with_m...  6.78 us
    pallas_call x1, Pallas kernels, local(): pl.pallas_call(functools.partial(mix_kernel, columns=columns), grid=(6,),...  5.34 us
    pallas_call x1, Pallas kernels, local(): pl.pallas_call(functools.partial(factor_kernel, columns=columns), in_spec...  5.3 us
  transfers between devices with their start and end apart: 17, of which 12 were waited for; matrix products, arithmetic and copies ran while one was open for 0% of the time, Pallas kernels for 21%

profile of v4, /device:TPU:0, one launch (start us, length us, event | category | flops | bytes accessed | tf_op | source)
XLA Modules:
  0.0 137.9 jit_solution(12322451406199744276)
XLA Ops:
  0.6 2.3 %shard_map.77 = (bf16[45,16,256]{2,1,0:T(8,128)(2,1)}, bf16[45,16,256]{2,1,0:T(8,128)(2,1)S(1)}) custom-call(f32[6,16,128]{2,1,0:T(8,128)} %refs_0_.1, f32[6144,256]{1,0:T(8,128)} %bitcast.9, f32[6144,256]{1,0:T(8,128)} %bitcast.10), custom_call_target="tpu_custom_call" | custom-call | tf_op jit(solution)/shard_map/pallas_call | solution.py:518
  3.0 0.0 copy-start.3
  3.0 5.0 %collective-permute-start = (bf16[45,16,256]{2,1,0:T(8,128)(2,1)}, bf16[45,16,256]{2,1,0:T(8,128)(2,1)S(1)}, u32[]{:S(2)}, u32[]{:S(2)}) collective-permute-start(bf16[45,16,256]{2,1,0:T(8,128)(2,1)} %get-tuple-element.30), channel_id=1, source_target_pairs={{0,1},{1,2},{2,3},{3,4},{4,5},{5,6},{6,7},{7,8},{8,9},{9,10},{10,1... | collective-permute-start | bytes 1105928 | tf_op jit(solution)/shard_map/ppermute | solution.py:528
  8.0 1.3 collective-permute-start.1
  9.3 2.8 %shard_map.79 = (bf16[42,32,256]{2,1,0:T(8,128)(2,1)}, bf16[42,32,256]{2,1,0:T(8,128)(2,1)S(1)}) custom-call(f32[6144,256]{1,0:T(8,128)} %bitcast.11, f32[6144,256]{1,0:T(8,128)} %bitcast.12), custom_call_target="tpu_custom_call" | custom-call | tf_op jit(solution)/shard_map/pallas_call | solution.py:518
  12.1 4.6 %collective-permute-start.2 = (bf16[42,32,256]{2,1,0:T(8,128)(2,1)}, bf16[42,32,256]{2,1,0:T(8,128)(2,1)S(1)}, u32[]{:S(2)}, u32[]{:S(2)}) collective-permute-start(bf16[42,32,256]{2,1,0:T(8,128)(2,1)} %get-tuple-element.39), channel_id=1, source_target_pairs={{0,1},{1,2},{2,3},{3,4},{4,5},{5,6},{6,7},{7,8},{8,9},{9,10},{10,1... | collective-permute-start | bytes 2064392 | tf_op jit(solution)/shard_map/ppermute | solution.py:528
  16.7 1.3 collective-permute-start.3
  18.0 0.1 pad_add_fusion.where_ref
  18.0 21.8 %collective-permute-done.low_ref = bf16[45,16,256]{2,1,0:T(8,128)(2,1)S(1)} collective-permute-done((bf16[45,16,256]{2,1,0:T(8,128)(2,1)}, bf16[45,16,256]{2,1,0:T(8,128)(2,1)S(1)}, u32[]{:S(2)}, u32[]{:S(2)}) %collective-permute-start) | collective-permute-done | bytes 368672 | tf_op jit(solution)/shard_map/ppermute | solution.py:528
  39.9 0.0 collective-permute-done.1.high_ref
  40.0 1.9 %all_gather.3.mean_ref = f32[6,32,256]{2,1,0:T(8,128)S(1)} all-gather(f32[6,32,128]{2,1,0:T(8,128)S(1)} %pad_maximum_fusion), channel_id=1, replica_groups=mesh['cols'=2,'space'=16] {'cols'}, dimensions={2}, use_global_device_ids=true | all-gather | bytes 294912 | tf_op jit(solution)/shard_map/all_gather | solution.py:538
  41.9 2.4 %mean_window.1 = (f32[192,128]{1,0:T(8,128)S(1)}, f32[1536,128]{1,0:T(8,128)S(1)}, f32[6,16,256]{2,1,0:T(8,128)S(1)}, f32[8,128]{1,0:T(8,128)S(1)}) custom-call(s32[2]{0:T(128)S(1)} %pad_add_fusion.where_ref, f32[6,32,256]{2,1,0:T(8,128)S(1)} %all_gather.3.mean_ref, s32[256,256]{1,0:T(8,128)S(1)} %copy-done.1, ...), custom_call_target="tpu_custom_call" | custom-call | tf_op jit(solution)/shard_map/mean_window/pallas_call | solution.py:554
  44.3 9.2 %collective-permute-done.2.low_ref = bf16[42,32,256]{2,1,0:T(8,128)(2,1)S(1)} collective-permute-done((bf16[42,32,256]{2,1,0:T(8,128)(2,1)}, bf16[42,32,256]{2,1,0:T(8,128)(2,1)S(1)}, u32[]{:S(2)}, u32[]{:S(2)}) %collective-permute-start.2) | collective-permute-done | bytes 688160 | tf_op jit(solution)/shard_map/ppermute | solution.py:528
  53.5 1.8 %collective-permute-done.3.high_ref = bf16[42,32,256]{2,1,0:T(8,128)(2,1)S(1)} collective-permute-done((bf16[42,32,256]{2,1,0:T(8,128)(2,1)S(1)}, bf16[42,32,256]{2,1,0:T(8,128)(2,1)S(1)}, u32[]{:S(2)}, u32[]{:S(2)}) %collective-permute-start.3) | collective-permute-done | bytes 688160 | tf_op jit(solution)/shard_map/ppermute | solution.py:529
  55.4 2.8 %copy-done = f32[64,6,16,256]{3,2,1,0:T(8,128)S(1)} copy-done((f32[64,6,16,256]{3,2,1,0:T(8,128)S(1)}, f32[64,6,16,256]{3,2,1,0:T(8,128)}, u32[]{:S(2)}) %copy-start) | copy-done | bytes 6291480
  58.1 16.3 %shard_map.80 = (bf16[6,16,32,256]{3,2,1,0:T(8,128)(2,1)S(1)}, f32[32,128]{1,0:T(8,128)S(1)}) custom-call(s32[2]{0:T(128)S(1)} %pad_add_fusion.where_ref, bf16[42,32,256]{2,1,0:T(8,128)(2,1)S(1)} %collective-permute-done.2.low_ref, bf16[42,32,256]{2,1,0:T(8,128)(2,1)S(1)} %collective-permute-done.3.high_ref, f32[192,128]{1,0:T(8,128)S(1)} %get-tuple-element.33.wet_ref, ...), custom_call_target="tpu_custom_call" | custom-call | tf_op jit(solution)/shard_map/pallas_call | solution.py:584
  74.5 0.0 slice-start
  74.5 0.0 slice-start.1
  74.5 0.1 collective-permute-start.15
  74.6 1.7 %shard_map.81 = (bf16[42,16,256]{2,1,0:T(8,128)(2,1)S(1)}, bf16[42,16,256]{2,1,0:T(8,128)(2,1)S(1)}) custom-call(f32[6144,256]{1,0:T(8,128)} %bitcast.13, f32[6144,256]{1,0:T(8,128)} %bitcast.14), custom_call_target="tpu_custom_call" | custom-call | tf_op jit(solution)/shard_map/pallas_call | solution.py:518
  76.3 3.5 %collective-permute-start.4 = (bf16[42,16,256]{2,1,0:T(8,128)(2,1)S(1)}, bf16[42,16,256]{2,1,0:T(8,128)(2,1)S(1)}, u32[]{:S(2)}, u32[]{:S(2)}) collective-permute-start(bf16[42,16,256]{2,1,0:T(8,128)(2,1)S(1)} %get-tuple-element.45), channel_id=1, source_target_pairs={{0,1},{1,2},{2,3},{3,4},{4,5},{5,6},{6,7},{7,8},{8,9},{9,10},{10,1... | collective-permute-start | bytes 1032200 | tf_op jit(solution)/shard_map/ppermute | solution.py:528
  79.8 1.5 %collective-permute-start.5 = (bf16[42,16,256]{2,1,0:T(8,128)(2,1)S(1)}, bf16[42,16,256]{2,1,0:T(8,128)(2,1)S(1)}, u32[]{:S(2)}, u32[]{:S(2)}) collective-permute-start(bf16[42,16,256]{2,1,0:T(8,128)(2,1)S(1)} %get-tuple-element.46), channel_id=1, source_target_pairs={{1,0},{2,1},{3,2},{4,3},{5,4},{6,5},{7,6},{8,7},{9,8},{10,9},{11,1... | collective-permute-start | bytes 1032200 | tf_op jit(solution)/shard_map/ppermute | solution.py:529
  81.3 8.2 %shard_map.78 = (bf16[6,16,16,256]{3,2,1,0:T(8,128)(2,1)S(1)}, f32[16,128]{1,0:T(8,128)S(1)}) custom-call(s32[2]{0:T(128)S(1)} %pad_add_fusion.where_ref, bf16[45,16,256]{2,1,0:T(8,128)(2,1)S(1)} %collective-permute-done.low_ref, bf16[45,16,256]{2,1,0:T(8,128)(2,1)S(1)} %collective-permute-done.1.high_ref, f32[192,128]{1,0:T(8,128)S(1)} %get-tuple-element.33.wet_ref, ...), custom_call_target="tpu_custom_call" | custom-call | tf_op jit(solution)/shard_map/pallas_call | solution.py:584
  89.5 0.2 collective-permute-start.14
  89.7 5.3 %collective-permute-done.4.low_ref = bf16[42,16,256]{2,1,0:T(8,128)(2,1)S(1)} collective-permute-done((bf16[42,16,256]{2,1,0:T(8,128)(2,1)S(1)}, bf16[42,16,256]{2,1,0:T(8,128)(2,1)S(1)}, u32[]{:S(2)}, u32[]{:S(2)}) %collective-permute-start.4) | collective-permute-done | bytes 344096 | tf_op jit(solution)/shard_map/ppermute | solution.py:528
  95.1 0.7 collective-permute-done.5.high_ref
  95.8 8.2 %shard_map.82 = (bf16[6,16,16,256]{3,2,1,0:T(8,128)(2,1)S(1)}, f32[16,128]{1,0:T(8,128)S(1)}) custom-call(s32[2]{0:T(128)S(1)} %pad_add_fusion.where_ref, bf16[42,16,256]{2,1,0:T(8,128)(2,1)S(1)} %collective-permute-done.4.low_ref, bf16[42,16,256]{2,1,0:T(8,128)(2,1)S(1)} %collective-permute-done.5.high_ref, f32[192,128]{1,0:T(8,128)S(1)} %get-tuple-element.33.wet_ref, ...), custom_call_target="tpu_custom_call" | custom-call | tf_op jit(solution)/shard_map/pallas_call | solution.py:584
  104.0 0.1 collective-permute-start.16
  104.1 0.5 collective-permute-start.6
  104.6 0.1 collective-permute-start.7
  104.7 1.7 %collective-permute-done.6.refs_3_ = f32[16,128]{1,0:T(8,128)S(1)} collective-permute-done((f32[16,128]{1,0:T(8,128)S(1)}, f32[16,128]{1,0:T(8,128)S(1)}, u32[]{:S(2)}, u32[]{:S(2)}) %collective-permute-start.6) | collective-permute-done | bytes 8224 | tf_op jit(solution)/shard_map/ppermute | solution.py:461
  106.4 0.1 collective-permute-start.8
  106.5 1.0 collective-permute-done.8.refs_5_
  107.6 0.0 collective-permute-done.7.refs_4_
  107.6 0.8 gram.1
  108.4 1.8 %collective-permute-start.9 = (f32[72,128]{1,0:T(8,128)S(1)}, f32[72,128]{1,0:T(8,128)S(1)}, u32[]{:S(2)}, u32[]{:S(2)}) collective-permute-start(f32[72,128]{1,0:T(8,128)S(1)} %gram.1), channel_id=1, source_target_pairs={{0,1},{1,0},{2,3},{3,2},{4,5},{5,4},{6,7},{7,6},{8,9},{9,8},{10,11... | collective-permute-start | bytes 110600 | tf_op jit(solution)/shard_map/ppermute | solution.py:453
  110.2 2.2 %collective-permute-done.9 = f32[72,128]{1,0:T(8,128)S(1)} collective-permute-done((f32[72,128]{1,0:T(8,128)S(1)}, f32[72,128]{1,0:T(8,128)S(1)}, u32[]{:S(2)}, u32[]{:S(2)}) %collective-permute-start.9) | collective-permute-done | bytes 36896 | tf_op jit(solution)/shard_map/ppermute | solution.py:453
  112.4 0.0 collective-permute-start.10
  112.4 3.9 %collective-permute-done.10 = f32[72,128]{1,0:T(8,128)S(1)} collective-permute-done((f32[72,128]{1,0:T(8,128)S(1)}, f32[72,128]{1,0:T(8,128)S(1)}, u32[]{:S(2)}, u32[]{:S(2)}) %collective-permute-start.10) | collective-permute-done | bytes 36896 | tf_op jit(solution)/shard_map/ppermute | solution.py:453
  116.4 2.7 %collective-permute-start.11 = (f32[72,128]{1,0:T(8,128)S(1)}, f32[72,128]{1,0:T(8,128)S(1)}, u32[]{:S(2)}, u32[]{:S(2)}) collective-permute-start(f32[72,128]{1,0:T(8,128)S(1)} %add.21), channel_id=1, source_target_pairs={{0,4},{1,5},{2,6},{3,7},{4,0},{5,1},{6,2},{7,3},{8,12},{9,13},{10,... | collective-permute-start | bytes 110600 | tf_op jit(solution)/shard_map/ppermute | solution.py:453
  119.1 1.9 %collective-permute-done.11 = f32[72,128]{1,0:T(8,128)S(1)} collective-permute-done((f32[72,128]{1,0:T(8,128)S(1)}, f32[72,128]{1,0:T(8,128)S(1)}, u32[]{:S(2)}, u32[]{:S(2)}) %collective-permute-start.11) | collective-permute-done | bytes 36896 | tf_op jit(solution)/shard_map/ppermute | solution.py:453
  121.0 3.0 %collective-permute-start.12 = (f32[72,128]{1,0:T(8,128)S(1)}, f32[72,128]{1,0:T(8,128)S(1)}, u32[]{:S(2)}, u32[]{:S(2)}) collective-permute-start(f32[72,128]{1,0:T(8,128)S(1)} %add.22), channel_id=1, source_target_pairs={{0,8},{1,9},{2,10},{3,11},{4,12},{5,13},{6,14},{7,15},{8,0},{9,1},... | collective-permute-start | bytes 110600 | tf_op jit(solution)/shard_map/ppermute | solution.py:453
  124.0 1.9 %collective-permute-done.12 = f32[72,128]{1,0:T(8,128)S(1)} collective-permute-done((f32[72,128]{1,0:T(8,128)S(1)}, f32[72,128]{1,0:T(8,128)S(1)}, u32[]{:S(2)}, u32[]{:S(2)}) %collective-permute-start.12) | collective-permute-done | bytes 36896 | tf_op jit(solution)/shard_map/ppermute | solution.py:453
  126.0 1.2 collective-permute-done.13.refs_1_
  127.2 5.3 %factor.1.mix_ref = bf16[80,128]{1,0:T(8,128)(2,1)S(1)} custom-call(s32[2]{0:T(128)S(1)} %pad_add_fusion.where_ref, f32[72,128]{1,0:T(8,128)S(1)} %add.23.refs_0_, f32[72,128]{1,0:T(8,128)S(1)} %collective-permute-done.13.refs_1_), custom_call_target="tpu_custom_call" | custom-call | tf_op jit(solution)/shard_map/factor/pallas_call | solution.py:602
  132.5 0.0 collective-permute-done.14.refs_3_
  132.5 0.0 collective-permute-done.16.refs_5_
  132.5 5.3 %mix.1 = (f32[64,6,16,256]{3,2,1,0:T(8,128)}, f32[6,16,128]{2,1,0:T(8,128)}) custom-call(s32[2]{0:T(128)S(1)} %pad_add_fusion.where_ref, bf16[80,128]{1,0:T(8,128)(2,1)S(1)} %factor.1.mix_ref, f32[6,16,256]{2,1,0:T(8,128)S(1)} %get-tuple-element.48.mean_ref, bf16[6,16,16,256]{3,2,1,0:T(8,128)(2,1)S(1)} %get-tuple-element.49.refs_0_, ...), custom_call_target="tpu_custom_call" | custom-call | tf_op jit(solution)/shard_map/mix/pallas_call | solution.py:613
  (25 shorter events, 0.1 us)
Async XLA Ops:
  2.9 15.1 %copy-start.5 = (s32[128]{0:T(128)S(1)}, s32[128]{0:T(128)}, u32[]{:S(2)}) copy-start(s32[128]{0:T(128)} %param.9) | copy-start | bytes 1540
  2.9 37.0 %copy-start.4 = (f32[6,16,128]{2,1,0:T(8,128)S(1)}, f32[6,16,128]{2,1,0:T(8,128)}, u32[]{:S(2)}) copy-start(f32[6,16,128]{2,1,0:T(8,128)} %refs_0_.1) | copy-start | bytes 147460
  2.9 39.0 %copy-start.1 = (s32[256,256]{1,0:T(8,128)S(1)}, s32[256,256]{1,0:T(8,128)}, u32[]{:S(2)}) copy-start(s32[256,256]{1,0:T(8,128)} %mask_ref.1) | copy-start | bytes 786436
  2.9 39.0 %copy-start.2 = (f32[128]{0:T(128)S(1)}, f32[128]{0:T(128)}, u32[]{:S(2)}) copy-start(f32[128]{0:T(128)} %param.11) | copy-start | bytes 1540
  3.0 39.0 %copy-start.3 = (f32[128]{0:T(128)S(1)}, f32[128]{0:T(128)}, u32[]{:S(2)}) copy-start(f32[128]{0:T(128)} %param.10) | copy-start | bytes 1540
  3.0 36.9 %collective-permute-start = (bf16[45,16,256]{2,1,0:T(8,128)(2,1)}, bf16[45,16,256]{2,1,0:T(8,128)(2,1)S(1)}, u32[]{:S(2)}, u32[]{:S(2)}) collective-permute-start(bf16[45,16,256]{2,1,0:T(8,128)(2,1)} %get-tuple-element.30), channel_id=1, source_target_pairs={{0,1},{1,2},{2,3},{3,4},{4,5},{5,6},{6,7},{7,8},{8,9},{9,10},{10,1... | collective-permute-start | bytes 1105928 | tf_op jit(solution)/shard_map/ppermute | solution.py:528
  8.0 31.9 %collective-permute-start.1 = (bf16[45,16,256]{2,1,0:T(8,128)(2,1)S(1)}, bf16[45,16,256]{2,1,0:T(8,128)(2,1)S(1)}, u32[]{:S(2)}, u32[]{:S(2)}) collective-permute-start(bf16[45,16,256]{2,1,0:T(8,128)(2,1)S(1)} %get-tuple-element.31), channel_id=1, source_target_pairs={{1,0},{2,1},{3,2},{4,3},{5,4},{6,5},{7,6},{8,7},{9,8},{10,9},{11,1... | collective-permute-start | bytes 1105928 | tf_op jit(solution)/shard_map/ppermute | solution.py:529
  12.1 41.4 %collective-permute-start.2 = (bf16[42,32,256]{2,1,0:T(8,128)(2,1)}, bf16[42,32,256]{2,1,0:T(8,128)(2,1)S(1)}, u32[]{:S(2)}, u32[]{:S(2)}) collective-permute-start(bf16[42,32,256]{2,1,0:T(8,128)(2,1)} %get-tuple-element.39), channel_id=1, source_target_pairs={{0,1},{1,2},{2,3},{3,4},{4,5},{5,6},{6,7},{7,8},{8,9},{9,10},{10,1... | collective-permute-start | bytes 2064392 | tf_op jit(solution)/shard_map/ppermute | solution.py:528
  16.7 38.7 %collective-permute-start.3 = (bf16[42,32,256]{2,1,0:T(8,128)(2,1)S(1)}, bf16[42,32,256]{2,1,0:T(8,128)(2,1)S(1)}, u32[]{:S(2)}, u32[]{:S(2)}) collective-permute-start(bf16[42,32,256]{2,1,0:T(8,128)(2,1)S(1)} %get-tuple-element.40), channel_id=1, source_target_pairs={{1,0},{2,1},{3,2},{4,3},{5,4},{6,5},{7,6},{8,7},{9,8},{10,9},{11,1... | collective-permute-start | bytes 2064392 | tf_op jit(solution)/shard_map/ppermute | solution.py:529
  55.4 2.8 %copy-start = (f32[64,6,16,256]{3,2,1,0:T(8,128)S(1)}, f32[64,6,16,256]{3,2,1,0:T(8,128)}, u32[]{:S(2)}) copy-start(f32[64,6,16,256]{3,2,1,0:T(8,128)} %param.7) | copy-start | bytes 18874372
  74.5 6.8 %slice-start = ((s8[6291456]{0:T(1024)(128)(4,1)}), s8[4194304]{0:T(1024)(128)(4,1)S(1)}, s32[]{:S(2)}) async-start(s8[6291456]{0:T(1024)(128)(4,1)} %bitcast.17), calls=%async_computation | async-start | bytes 8388608
  74.5 6.8 %slice-start.1 = ((s8[6291456]{0:T(1024)(128)(4,1)}), s8[2097152]{0:T(1024)(128)(4,1)S(1)}, s32[]{:S(2)}) async-start(s8[6291456]{0:T(1024)(128)(4,1)} %bitcast.17), calls=%async_computation.1 | async-start | bytes 4194304
  74.5 58.1 %collective-permute-start.15 = (bf16[6,16,32,256]{3,2,1,0:T(8,128)(2,1)S(1)}, bf16[6,16,32,256]{3,2,1,0:T(8,128)(2,1)S(1)}, u32[]{:S(2)}, u32[]{:S(2)}) collective-permute-start(bf16[6,16,32,256]{3,2,1,0:T(8,128)(2,1)S(1)} %get-tuple-element.50.refs_1_), channel_id=1, source_target_pairs={{16,0},{0,16},{17,1},{1,17},{18,2},{2,18},{19,3},{3,19},{20,4},{4,... | collective-permute-start | bytes 4718600 | tf_op jit(solution)/shard_map/ppermute | solution.py:461
  76.3 18.8 %collective-permute-start.4 = (bf16[42,16,256]{2,1,0:T(8,128)(2,1)S(1)}, bf16[42,16,256]{2,1,0:T(8,128)(2,1)S(1)}, u32[]{:S(2)}, u32[]{:S(2)}) collective-permute-start(bf16[42,16,256]{2,1,0:T(8,128)(2,1)S(1)} %get-tuple-element.45), channel_id=1, source_target_pairs={{0,1},{1,2},{2,3},{3,4},{4,5},{5,6},{6,7},{7,8},{8,9},{9,10},{10,1... | collective-permute-start | bytes 1032200 | tf_op jit(solution)/shard_map/ppermute | solution.py:528
  79.8 16.0 %collective-permute-start.5 = (bf16[42,16,256]{2,1,0:T(8,128)(2,1)S(1)}, bf16[42,16,256]{2,1,0:T(8,128)(2,1)S(1)}, u32[]{:S(2)}, u32[]{:S(2)}) collective-permute-start(bf16[42,16,256]{2,1,0:T(8,128)(2,1)S(1)} %get-tuple-element.46), channel_id=1, source_target_pairs={{1,0},{2,1},{3,2},{4,3},{5,4},{6,5},{7,6},{8,7},{9,8},{10,9},{11,1... | collective-permute-start | bytes 1032200 | tf_op jit(solution)/shard_map/ppermute | solution.py:529
  89.5 43.0 %collective-permute-start.14 = (bf16[6,16,16,256]{3,2,1,0:T(8,128)(2,1)S(1)}, bf16[6,16,16,256]{3,2,1,0:T(8,128)(2,1)S(1)}, u32[]{:S(2)}, u32[]{:S(2)}) collective-permute-start(bf16[6,16,16,256]{3,2,1,0:T(8,128)(2,1)S(1)} %get-tuple-element.49.refs_0_), channel_id=1, source_target_pairs={{16,0},{0,16},{17,1},{1,17},{18,2},{2,18},{19,3},{3,19},{20,4},{4,... | collective-permute-start | bytes 2359304 | tf_op jit(solution)/shard_map/ppermute | solution.py:461
  104.0 28.5 %collective-permute-start.16 = (bf16[6,16,16,256]{3,2,1,0:T(8,128)(2,1)S(1)}, bf16[6,16,16,256]{3,2,1,0:T(8,128)(2,1)S(1)}, u32[]{:S(2)}, u32[]{:S(2)}) collective-permute-start(bf16[6,16,16,256]{3,2,1,0:T(8,128)(2,1)S(1)} %get-tuple-element.51.refs_2_), channel_id=1, source_target_pairs={{16,0},{0,16},{17,1},{1,17},{18,2},{2,18},{19,3},{3,19},{20,4},{4,... | collective-permute-start | bytes 2359304 | tf_op jit(solution)/shard_map/ppermute | solution.py:461
  104.1 2.3 %collective-permute-start.6 = (f32[16,128]{1,0:T(8,128)S(1)}, f32[16,128]{1,0:T(8,128)S(1)}, u32[]{:S(2)}, u32[]{:S(2)}) collective-permute-start(f32[16,128]{1,0:T(8,128)S(1)} %get-tuple-element.35.refs_0_), channel_id=1, source_target_pairs={{16,0},{0,16},{17,1},{1,17},{18,2},{2,18},{19,3},{3,19},{20,4},{4,... | collective-permute-start | bytes 24584 | tf_op jit(solution)/shard_map/ppermute | solution.py:461
  104.6 3.0 %collective-permute-start.7 = (f32[32,128]{1,0:T(8,128)S(1)}, f32[32,128]{1,0:T(8,128)S(1)}, u32[]{:S(2)}, u32[]{:S(2)}) collective-permute-start(f32[32,128]{1,0:T(8,128)S(1)} %get-tuple-element.41.refs_1_), channel_id=1, source_target_pairs={{16,0},{0,16},{17,1},{1,17},{18,2},{2,18},{19,3},{3,19},{20,4},{4,... | collective-permute-start | bytes 49160 | tf_op jit(solution)/shard_map/ppermute | solution.py:461
  106.4 1.2 collective-permute-start.8
  108.4 4.0 %collective-permute-start.9 = (f32[72,128]{1,0:T(8,128)S(1)}, f32[72,128]{1,0:T(8,128)S(1)}, u32[]{:S(2)}, u32[]{:S(2)}) collective-permute-start(f32[72,128]{1,0:T(8,128)S(1)} %gram.1), channel_id=1, source_target_pairs={{0,1},{1,0},{2,3},{3,2},{4,5},{5,4},{6,7},{7,6},{8,9},{9,8},{10,11... | collective-permute-start | bytes 110600 | tf_op jit(solution)/shard_map/ppermute | solution.py:453
  112.4 4.0 %collective-permute-start.10 = (f32[72,128]{1,0:T(8,128)S(1)}, f32[72,128]{1,0:T(8,128)S(1)}, u32[]{:S(2)}, u32[]{:S(2)}) collective-permute-start(f32[72,128]{1,0:T(8,128)S(1)} %add.20), channel_id=1, source_target_pairs={{0,2},{1,3},{2,0},{3,1},{4,6},{5,7},{6,4},{7,5},{8,10},{9,11},{10,... | collective-permute-start | bytes 110600 | tf_op jit(solution)/shard_map/ppermute | solution.py:453
  116.4 4.6 %collective-permute-start.11 = (f32[72,128]{1,0:T(8,128)S(1)}, f32[72,128]{1,0:T(8,128)S(1)}, u32[]{:S(2)}, u32[]{:S(2)}) collective-permute-start(f32[72,128]{1,0:T(8,128)S(1)} %add.21), channel_id=1, source_target_pairs={{0,4},{1,5},{2,6},{3,7},{4,0},{5,1},{6,2},{7,3},{8,12},{9,13},{10,... | collective-permute-start | bytes 110600 | tf_op jit(solution)/shard_map/ppermute | solution.py:453
  121.0 5.0 %collective-permute-start.12 = (f32[72,128]{1,0:T(8,128)S(1)}, f32[72,128]{1,0:T(8,128)S(1)}, u32[]{:S(2)}, u32[]{:S(2)}) collective-permute-start(f32[72,128]{1,0:T(8,128)S(1)} %add.22), channel_id=1, source_target_pairs={{0,8},{1,9},{2,10},{3,11},{4,12},{5,13},{6,14},{7,15},{8,0},{9,1},... | collective-permute-start | bytes 110600 | tf_op jit(solution)/shard_map/ppermute | solution.py:453
  126.0 1.2 collective-permute-start.13

commit v5 on v4

--- a/solution.py
+++ b/solution.py
@@ -30,7 +30,7 @@
 def halo_rows():
     rows = []
     for layer in range(2):
-        rows += [(3 * layer, d) for d in range(DEPTH, 0, -1)]
+        rows += [(3 * layer, d) for d in range(DEPTH - 1, 0, -1)]
     for layer in range(2):
         rows += [(3 * layer + 1, d) for d in range(DEPTH - 1, 0, -1)]
         rows += [(3 * layer + 2, d) for d in range(DEPTH - 2, 0, -1)]
@@ -85,10 +85,15 @@
         )
 
     for i, (field, d) in enumerate(halo_rows()):
-        for ref, r in ((up_ref, tile_rows - d), (down_ref, d - 1)):
+        for ref, r, side in ((up_ref, tile_rows - d, -1), (down_ref, d - 1, 1)):
             value = row(field, r)
             if d == DEPTH - 1 and field % 3 == 1:
+                top = row(0, r + side)
+                beyond = gravity * (top + row(3, r + side))
+                if field > 3:
+                    beyond = beyond - reduced_gravity * top
                 value = value + (turn_part / keep_part) * row(field + 1, r)
+                value = value - (side * slope_part / keep_part) * beyond
             ref[i] = value.astype(bf16)
 
 
@@ -211,6 +216,8 @@
     for layer in range(2):
         for r in (1, ext - 2):
             state_a[3 * layer + 2, r] = jnp.zeros((GROUP, cells), f32)
+        for r in (0, ext - 1):
+            state_a[3 * layer, r] = jnp.zeros((GROUP, cells), f32)
 
     def press_of(top, bottom):
         p_top = gravity * (top + bottom)

time: 138 us -> 135 us (0.978)
  waiting for transfers between devices: 53 us -> 50.2 us
    ppermute x3, waiting for transfers between devices: 36.4 us -> 33.6 us  [local(): lows.append(lax.ppermute(going_up, 'space', up))]
  transfers between devices with their start and end apart: 17 -> 17, of which waited for: 12 -> 12; matrix products, arithmetic and copies ran while one was open for 0% -> 0% of each run, Pallas kernels for 21% -> 22%
where the time goes in v5:
time: 135 us
  Pallas kernels  53.2 us (39%)
  waiting for transfers between devices  50.2 us (37%)
  starting transfers between devices  25.8 us (19%)
  local copies, waits for them, and re-layouts  2.82 us (2%)
  blocking collectives  1.95 us (1%)
    ppermute x3, waiting for transfers between devices, local(): lows.append(lax.ppermute(going_up, 'space', up))  33.6 us
    pallas_call x3, Pallas kernels, local(): window(where, lows[c], highs[c], wet, coef, station_row, *[flat] * groups)  32.6 us
    ppermute x3, starting transfers between devices, local(): lows.append(lax.ppermute(going_up, 'space', up))  13.1 us
    ppermute x4, waiting for transfers between devices, spread_sum(): lax.ppermute(value, axis, [(i, i ^ step) for i in range(count)])  10 us
    ppermute x4, starting transfers between devices, spread_sum(): lax.ppermute(value, axis, [(i, i ^ step) for i in range(count)])  7.53 us
    pallas_call x3, Pallas kernels, local(): pl.pallas_call(functools.partial(pack_kernel, tile_rows=tile_rows, with_m...  6.77 us
    pallas_call x1, Pallas kernels, local(): pl.pallas_call(functools.partial(mix_kernel, columns=columns), grid=(6,),...  5.36 us
    pallas_call x1, Pallas kernels, local(): pl.pallas_call(functools.partial(factor_kernel, columns=columns), in_spec...  5.3 us
  transfers between devices with their start and end apart: 17, of which 12 were waited for; matrix products, arithmetic and copies ran while one was open for 0% of the time, Pallas kernels for 22%

profile of v5, /device:TPU:0, one launch (start us, length us, event | category | flops | bytes accessed | tf_op | source)
XLA Modules:
  0.0 135.1 jit_solution(17361017401255771517)
XLA Ops:
  0.6 2.3 %shard_map.77 = (bf16[43,16,256]{2,1,0:T(8,128)(2,1)}, bf16[43,16,256]{2,1,0:T(8,128)(2,1)S(1)}) custom-call(f32[6,16,128]{2,1,0:T(8,128)} %refs_0_.1, f32[6144,256]{1,0:T(8,128)} %bitcast.9, f32[6144,256]{1,0:T(8,128)} %bitcast.10), custom_call_target="tpu_custom_call" | custom-call | tf_op jit(solution)/shard_map/pallas_call | solution.py:525
  2.9 0.0 copy-start.3
  3.0 5.0 %collective-permute-start = (bf16[43,16,256]{2,1,0:T(8,128)(2,1)}, bf16[43,16,256]{2,1,0:T(8,128)(2,1)S(1)}, u32[]{:S(2)}, u32[]{:S(2)}) collective-permute-start(bf16[43,16,256]{2,1,0:T(8,128)(2,1)} %get-tuple-element.30), channel_id=1, source_target_pairs={{0,1},{1,2},{2,3},{3,4},{4,5},{5,6},{6,7},{7,8},{8,9},{9,10},{10,1... | collective-permute-start | bytes 1056776 | tf_op jit(solution)/shard_map/ppermute | solution.py:535
  8.0 1.3 collective-permute-start.1
  9.3 2.8 %shard_map.79 = (bf16[40,32,256]{2,1,0:T(8,128)(2,1)}, bf16[40,32,256]{2,1,0:T(8,128)(2,1)S(1)}) custom-call(f32[6144,256]{1,0:T(8,128)} %bitcast.11, f32[6144,256]{1,0:T(8,128)} %bitcast.12), custom_call_target="tpu_custom_call" | custom-call | tf_op jit(solution)/shard_map/pallas_call | solution.py:525
  12.1 4.6 %collective-permute-start.2 = (bf16[40,32,256]{2,1,0:T(8,128)(2,1)}, bf16[40,32,256]{2,1,0:T(8,128)(2,1)S(1)}, u32[]{:S(2)}, u32[]{:S(2)}) collective-permute-start(bf16[40,32,256]{2,1,0:T(8,128)(2,1)} %get-tuple-element.39), channel_id=1, source_target_pairs={{0,1},{1,2},{2,3},{3,4},{4,5},{5,6},{6,7},{7,8},{8,9},{9,10},{10,1... | collective-permute-start | bytes 1966088 | tf_op jit(solution)/shard_map/ppermute | solution.py:535
  16.6 1.3 collective-permute-start.3
  18.0 0.1 pad_add_fusion.where_ref
  18.0 20.5 %collective-permute-done.low_ref = bf16[43,16,256]{2,1,0:T(8,128)(2,1)S(1)} collective-permute-done((bf16[43,16,256]{2,1,0:T(8,128)(2,1)}, bf16[43,16,256]{2,1,0:T(8,128)(2,1)S(1)}, u32[]{:S(2)}, u32[]{:S(2)}) %collective-permute-start) | collective-permute-done | bytes 352288 | tf_op jit(solution)/shard_map/ppermute | solution.py:535
  38.5 0.0 collective-permute-done.1.high_ref
  38.6 1.9 %all_gather.3.mean_ref = f32[6,32,256]{2,1,0:T(8,128)S(1)} all-gather(f32[6,32,128]{2,1,0:T(8,128)S(1)} %pad_maximum_fusion), channel_id=1, replica_groups=mesh['cols'=2,'space'=16] {'cols'}, dimensions={2}, use_global_device_ids=true | all-gather | bytes 294912 | tf_op jit(solution)/shard_map/all_gather | solution.py:545
  40.5 2.4 %mean_window.1 = (f32[192,128]{1,0:T(8,128)S(1)}, f32[1536,128]{1,0:T(8,128)S(1)}, f32[6,16,256]{2,1,0:T(8,128)S(1)}, f32[8,128]{1,0:T(8,128)S(1)}) custom-call(s32[2]{0:T(128)S(1)} %pad_add_fusion.where_ref, f32[6,32,256]{2,1,0:T(8,128)S(1)} %all_gather.3.mean_ref, s32[256,256]{1,0:T(8,128)S(1)} %copy-done.1, ...), custom_call_target="tpu_custom_call" | custom-call | tf_op jit(solution)/shard_map/mean_window/pallas_call | solution.py:561
  42.9 8.5 %collective-permute-done.2.low_ref = bf16[40,32,256]{2,1,0:T(8,128)(2,1)S(1)} collective-permute-done((bf16[40,32,256]{2,1,0:T(8,128)(2,1)}, bf16[40,32,256]{2,1,0:T(8,128)(2,1)S(1)}, u32[]{:S(2)}, u32[]{:S(2)}) %collective-permute-start.2) | collective-permute-done | bytes 655392 | tf_op jit(solution)/shard_map/ppermute | solution.py:535
  51.4 1.8 %collective-permute-done.3.high_ref = bf16[40,32,256]{2,1,0:T(8,128)(2,1)S(1)} collective-permute-done((bf16[40,32,256]{2,1,0:T(8,128)(2,1)S(1)}, bf16[40,32,256]{2,1,0:T(8,128)(2,1)S(1)}, u32[]{:S(2)}, u32[]{:S(2)}) %collective-permute-start.3) | collective-permute-done | bytes 655392 | tf_op jit(solution)/shard_map/ppermute | solution.py:536
  53.2 2.8 %copy-done = f32[64,6,16,256]{3,2,1,0:T(8,128)S(1)} copy-done((f32[64,6,16,256]{3,2,1,0:T(8,128)S(1)}, f32[64,6,16,256]{3,2,1,0:T(8,128)}, u32[]{:S(2)}) %copy-start) | copy-done | bytes 6291480
  56.0 16.3 %shard_map.80 = (bf16[6,16,32,256]{3,2,1,0:T(8,128)(2,1)S(1)}, f32[32,128]{1,0:T(8,128)S(1)}) custom-call(s32[2]{0:T(128)S(1)} %pad_add_fusion.where_ref, bf16[40,32,256]{2,1,0:T(8,128)(2,1)S(1)} %collective-permute-done.2.low_ref, bf16[40,32,256]{2,1,0:T(8,128)(2,1)S(1)} %collective-permute-done.3.high_ref, f32[192,128]{1,0:T(8,128)S(1)} %get-tuple-element.33.wet_ref, ...), custom_call_target="tpu_custom_call" | custom-call | tf_op jit(solution)/shard_map/pallas_call | solution.py:591
  72.3 0.0 slice-start
  72.4 0.0 slice-start.1
  72.4 0.1 collective-permute-start.15
  72.4 1.7 %shard_map.81 = (bf16[40,16,256]{2,1,0:T(8,128)(2,1)S(1)}, bf16[40,16,256]{2,1,0:T(8,128)(2,1)S(1)}) custom-call(f32[6144,256]{1,0:T(8,128)} %bitcast.13, f32[6144,256]{1,0:T(8,128)} %bitcast.14), custom_call_target="tpu_custom_call" | custom-call | tf_op jit(solution)/shard_map/pallas_call | solution.py:525
  74.1 3.5 %collective-permute-start.4 = (bf16[40,16,256]{2,1,0:T(8,128)(2,1)S(1)}, bf16[40,16,256]{2,1,0:T(8,128)(2,1)S(1)}, u32[]{:S(2)}, u32[]{:S(2)}) collective-permute-start(bf16[40,16,256]{2,1,0:T(8,128)(2,1)S(1)} %get-tuple-element.45), channel_id=1, source_target_pairs={{0,1},{1,2},{2,3},{3,4},{4,5},{5,6},{6,7},{7,8},{8,9},{9,10},{10,1... | collective-permute-start | bytes 983048 | tf_op jit(solution)/shard_map/ppermute | solution.py:535
  77.7 1.5 %collective-permute-start.5 = (bf16[40,16,256]{2,1,0:T(8,128)(2,1)S(1)}, bf16[40,16,256]{2,1,0:T(8,128)(2,1)S(1)}, u32[]{:S(2)}, u32[]{:S(2)}) collective-permute-start(bf16[40,16,256]{2,1,0:T(8,128)(2,1)S(1)} %get-tuple-element.46), channel_id=1, source_target_pairs={{1,0},{2,1},{3,2},{4,3},{5,4},{6,5},{7,6},{8,7},{9,8},{10,9},{11,1... | collective-permute-start | bytes 983048 | tf_op jit(solution)/shard_map/ppermute | solution.py:536
  79.2 8.2 %shard_map.78 = (bf16[6,16,16,256]{3,2,1,0:T(8,128)(2,1)S(1)}, f32[16,128]{1,0:T(8,128)S(1)}) custom-call(s32[2]{0:T(128)S(1)} %pad_add_fusion.where_ref, bf16[43,16,256]{2,1,0:T(8,128)(2,1)S(1)} %collective-permute-done.low_ref, bf16[43,16,256]{2,1,0:T(8,128)(2,1)S(1)} %collective-permute-done.1.high_ref, f32[192,128]{1,0:T(8,128)S(1)} %get-tuple-element.33.wet_ref, ...), custom_call_target="tpu_custom_call" | custom-call | tf_op jit(solution)/shard_map/pallas_call | solution.py:591
  87.4 0.2 collective-permute-start.14
  87.6 4.6 %collective-permute-done.4.low_ref = bf16[40,16,256]{2,1,0:T(8,128)(2,1)S(1)} collective-permute-done((bf16[40,16,256]{2,1,0:T(8,128)(2,1)S(1)}, bf16[40,16,256]{2,1,0:T(8,128)(2,1)S(1)}, u32[]{:S(2)}, u32[]{:S(2)}) %collective-permute-start.4) | collective-permute-done | bytes 327712 | tf_op jit(solution)/shard_map/ppermute | solution.py:535
  92.3 0.7 collective-permute-done.5.high_ref
  93.0 8.2 %shard_map.82 = (bf16[6,16,16,256]{3,2,1,0:T(8,128)(2,1)S(1)}, f32[16,128]{1,0:T(8,128)S(1)}) custom-call(s32[2]{0:T(128)S(1)} %pad_add_fusion.where_ref, bf16[40,16,256]{2,1,0:T(8,128)(2,1)S(1)} %collective-permute-done.4.low_ref, bf16[40,16,256]{2,1,0:T(8,128)(2,1)S(1)} %collective-permute-done.5.high_ref, f32[192,128]{1,0:T(8,128)S(1)} %get-tuple-element.33.wet_ref, ...), custom_call_target="tpu_custom_call" | custom-call | tf_op jit(solution)/shard_map/pallas_call | solution.py:591
  101.2 0.1 collective-permute-start.16
  101.3 0.5 collective-permute-start.6
  101.8 0.1 collective-permute-start.7
  101.9 1.7 %collective-permute-done.6.refs_3_ = f32[16,128]{1,0:T(8,128)S(1)} collective-permute-done((f32[16,128]{1,0:T(8,128)S(1)}, f32[16,128]{1,0:T(8,128)S(1)}, u32[]{:S(2)}, u32[]{:S(2)}) %collective-permute-start.6) | collective-permute-done | bytes 8224 | tf_op jit(solution)/shard_map/ppermute | solution.py:468
  103.6 0.1 collective-permute-start.8
  103.7 1.0 collective-permute-done.8.refs_5_
  104.7 0.0 collective-permute-done.7.refs_4_
  104.7 0.8 gram.1
  105.6 1.8 %collective-permute-start.9 = (f32[72,128]{1,0:T(8,128)S(1)}, f32[72,128]{1,0:T(8,128)S(1)}, u32[]{:S(2)}, u32[]{:S(2)}) collective-permute-start(f32[72,128]{1,0:T(8,128)S(1)} %gram.1), channel_id=1, source_target_pairs={{0,1},{1,0},{2,3},{3,2},{4,5},{5,4},{6,7},{7,6},{8,9},{9,8},{10,11... | collective-permute-start | bytes 110600 | tf_op jit(solution)/shard_map/ppermute | solution.py:460
  107.4 2.2 %collective-permute-done.9 = f32[72,128]{1,0:T(8,128)S(1)} collective-permute-done((f32[72,128]{1,0:T(8,128)S(1)}, f32[72,128]{1,0:T(8,128)S(1)}, u32[]{:S(2)}, u32[]{:S(2)}) %collective-permute-start.9) | collective-permute-done | bytes 36896 | tf_op jit(solution)/shard_map/ppermute | solution.py:460
  109.6 0.0 collective-permute-start.10
  109.6 3.9 %collective-permute-done.10 = f32[72,128]{1,0:T(8,128)S(1)} collective-permute-done((f32[72,128]{1,0:T(8,128)S(1)}, f32[72,128]{1,0:T(8,128)S(1)}, u32[]{:S(2)}, u32[]{:S(2)}) %collective-permute-start.10) | collective-permute-done | bytes 36896 | tf_op jit(solution)/shard_map/ppermute | solution.py:460
  113.5 2.7 %collective-permute-start.11 = (f32[72,128]{1,0:T(8,128)S(1)}, f32[72,128]{1,0:T(8,128)S(1)}, u32[]{:S(2)}, u32[]{:S(2)}) collective-permute-start(f32[72,128]{1,0:T(8,128)S(1)} %add.21), channel_id=1, source_target_pairs={{0,4},{1,5},{2,6},{3,7},{4,0},{5,1},{6,2},{7,3},{8,12},{9,13},{10,... | collective-permute-start | bytes 110600 | tf_op jit(solution)/shard_map/ppermute | solution.py:460
  116.2 1.9 %collective-permute-done.11 = f32[72,128]{1,0:T(8,128)S(1)} collective-permute-done((f32[72,128]{1,0:T(8,128)S(1)}, f32[72,128]{1,0:T(8,128)S(1)}, u32[]{:S(2)}, u32[]{:S(2)}) %collective-permute-start.11) | collective-permute-done | bytes 36896 | tf_op jit(solution)/shard_map/ppermute | solution.py:460
  118.2 3.0 %collective-permute-start.12 = (f32[72,128]{1,0:T(8,128)S(1)}, f32[72,128]{1,0:T(8,128)S(1)}, u32[]{:S(2)}, u32[]{:S(2)}) collective-permute-start(f32[72,128]{1,0:T(8,128)S(1)} %add.22), channel_id=1, source_target_pairs={{0,8},{1,9},{2,10},{3,11},{4,12},{5,13},{6,14},{7,15},{8,0},{9,1},... | collective-permute-start | bytes 110600 | tf_op jit(solution)/shard_map/ppermute | solution.py:460
  121.2 1.9 %collective-permute-done.12 = f32[72,128]{1,0:T(8,128)S(1)} collective-permute-done((f32[72,128]{1,0:T(8,128)S(1)}, f32[72,128]{1,0:T(8,128)S(1)}, u32[]{:S(2)}, u32[]{:S(2)}) %collective-permute-start.12) | collective-permute-done | bytes 36896 | tf_op jit(solution)/shard_map/ppermute | solution.py:460
  123.2 1.2 collective-permute-done.13.refs_1_
  124.4 5.3 %factor.1.mix_ref = bf16[80,128]{1,0:T(8,128)(2,1)S(1)} custom-call(s32[2]{0:T(128)S(1)} %pad_add_fusion.where_ref, f32[72,128]{1,0:T(8,128)S(1)} %add.23.refs_0_, f32[72,128]{1,0:T(8,128)S(1)} %collective-permute-done.13.refs_1_), custom_call_target="tpu_custom_call" | custom-call | tf_op jit(solution)/shard_map/factor/pallas_call | solution.py:609
  129.7 0.0 collective-permute-done.14.refs_3_
  129.7 0.0 collective-permute-done.16.refs_5_
  129.7 5.4 %mix.1 = (f32[64,6,16,256]{3,2,1,0:T(8,128)}, f32[6,16,128]{2,1,0:T(8,128)}) custom-call(s32[2]{0:T(128)S(1)} %pad_add_fusion.where_ref, bf16[80,128]{1,0:T(8,128)(2,1)S(1)} %factor.1.mix_ref, f32[6,16,256]{2,1,0:T(8,128)S(1)} %get-tuple-element.48.mean_ref, bf16[6,16,16,256]{3,2,1,0:T(8,128)(2,1)S(1)} %get-tuple-element.49.refs_0_, ...), custom_call_target="tpu_custom_call" | custom-call | tf_op jit(solution)/shard_map/mix/pallas_call | solution.py:620
  (25 shorter events, 0.1 us)
Async XLA Ops:
  2.9 15.1 %copy-start.5 = (s32[128]{0:T(128)S(1)}, s32[128]{0:T(128)}, u32[]{:S(2)}) copy-start(s32[128]{0:T(128)} %param.9) | copy-start | bytes 1540
  2.9 35.6 %copy-start.4 = (f32[6,16,128]{2,1,0:T(8,128)S(1)}, f32[6,16,128]{2,1,0:T(8,128)}, u32[]{:S(2)}) copy-start(f32[6,16,128]{2,1,0:T(8,128)} %refs_0_.1) | copy-start | bytes 147460
  2.9 37.6 %copy-start.1 = (s32[256,256]{1,0:T(8,128)S(1)}, s32[256,256]{1,0:T(8,128)}, u32[]{:S(2)}) copy-start(s32[256,256]{1,0:T(8,128)} %mask_ref.1) | copy-start | bytes 786436
  2.9 37.6 %copy-start.2 = (f32[128]{0:T(128)S(1)}, f32[128]{0:T(128)}, u32[]{:S(2)}) copy-start(f32[128]{0:T(128)} %param.11) | copy-start | bytes 1540
  2.9 37.6 %copy-start.3 = (f32[128]{0:T(128)S(1)}, f32[128]{0:T(128)}, u32[]{:S(2)}) copy-start(f32[128]{0:T(128)} %param.10) | copy-start | bytes 1540
  3.0 35.5 %collective-permute-start = (bf16[43,16,256]{2,1,0:T(8,128)(2,1)}, bf16[43,16,256]{2,1,0:T(8,128)(2,1)S(1)}, u32[]{:S(2)}, u32[]{:S(2)}) collective-permute-start(bf16[43,16,256]{2,1,0:T(8,128)(2,1)} %get-tuple-element.30), channel_id=1, source_target_pairs={{0,1},{1,2},{2,3},{3,4},{4,5},{5,6},{6,7},{7,8},{8,9},{9,10},{10,1... | collective-permute-start | bytes 1056776 | tf_op jit(solution)/shard_map/ppermute | solution.py:535
  8.0 30.5 %collective-permute-start.1 = (bf16[43,16,256]{2,1,0:T(8,128)(2,1)S(1)}, bf16[43,16,256]{2,1,0:T(8,128)(2,1)S(1)}, u32[]{:S(2)}, u32[]{:S(2)}) collective-permute-start(bf16[43,16,256]{2,1,0:T(8,128)(2,1)S(1)} %get-tuple-element.31), channel_id=1, source_target_pairs={{1,0},{2,1},{3,2},{4,3},{5,4},{6,5},{7,6},{8,7},{9,8},{10,9},{11,1... | collective-permute-start | bytes 1056776 | tf_op jit(solution)/shard_map/ppermute | solution.py:536
  12.1 39.3 %collective-permute-start.2 = (bf16[40,32,256]{2,1,0:T(8,128)(2,1)}, bf16[40,32,256]{2,1,0:T(8,128)(2,1)S(1)}, u32[]{:S(2)}, u32[]{:S(2)}) collective-permute-start(bf16[40,32,256]{2,1,0:T(8,128)(2,1)} %get-tuple-element.39), channel_id=1, source_target_pairs={{0,1},{1,2},{2,3},{3,4},{4,5},{5,6},{6,7},{7,8},{8,9},{9,10},{10,1... | collective-permute-start | bytes 1966088 | tf_op jit(solution)/shard_map/ppermute | solution.py:535
  16.6 36.6 %collective-permute-start.3 = (bf16[40,32,256]{2,1,0:T(8,128)(2,1)S(1)}, bf16[40,32,256]{2,1,0:T(8,128)(2,1)S(1)}, u32[]{:S(2)}, u32[]{:S(2)}) collective-permute-start(bf16[40,32,256]{2,1,0:T(8,128)(2,1)S(1)} %get-tuple-element.40), channel_id=1, source_target_pairs={{1,0},{2,1},{3,2},{4,3},{5,4},{6,5},{7,6},{8,7},{9,8},{10,9},{11,1... | collective-permute-start | bytes 1966088 | tf_op jit(solution)/shard_map/ppermute | solution.py:536
  53.2 2.8 %copy-start = (f32[64,6,16,256]{3,2,1,0:T(8,128)S(1)}, f32[64,6,16,256]{3,2,1,0:T(8,128)}, u32[]{:S(2)}) copy-start(f32[64,6,16,256]{3,2,1,0:T(8,128)} %param.7) | copy-start | bytes 18874372
  72.3 6.8 %slice-start = ((s8[6291456]{0:T(1024)(128)(4,1)}), s8[4194304]{0:T(1024)(128)(4,1)S(1)}, s32[]{:S(2)}) async-start(s8[6291456]{0:T(1024)(128)(4,1)} %bitcast.17), calls=%async_computation | async-start | bytes 8388608
  72.4 6.8 %slice-start.1 = ((s8[6291456]{0:T(1024)(128)(4,1)}), s8[2097152]{0:T(1024)(128)(4,1)S(1)}, s32[]{:S(2)}) async-start(s8[6291456]{0:T(1024)(128)(4,1)} %bitcast.17), calls=%async_computation.1 | async-start | bytes 4194304
  72.4 57.4 %collective-permute-start.15 = (bf16[6,16,32,256]{3,2,1,0:T(8,128)(2,1)S(1)}, bf16[6,16,32,256]{3,2,1,0:T(8,128)(2,1)S(1)}, u32[]{:S(2)}, u32[]{:S(2)}) collective-permute-start(bf16[6,16,32,256]{3,2,1,0:T(8,128)(2,1)S(1)} %get-tuple-element.50.refs_1_), channel_id=1, source_target_pairs={{16,0},{0,16},{17,1},{1,17},{18,2},{2,18},{19,3},{3,19},{20,4},{4,... | collective-permute-start | bytes 4718600 | tf_op jit(solution)/shard_map/ppermute | solution.py:468
  74.1 18.1 %collective-permute-start.4 = (bf16[40,16,256]{2,1,0:T(8,128)(2,1)S(1)}, bf16[40,16,256]{2,1,0:T(8,128)(2,1)S(1)}, u32[]{:S(2)}, u32[]{:S(2)}) collective-permute-start(bf16[40,16,256]{2,1,0:T(8,128)(2,1)S(1)} %get-tuple-element.45), channel_id=1, source_target_pairs={{0,1},{1,2},{2,3},{3,4},{4,5},{5,6},{6,7},{7,8},{8,9},{9,10},{10,1... | collective-permute-start | bytes 983048 | tf_op jit(solution)/shard_map/ppermute | solution.py:535
  77.7 15.3 %collective-permute-start.5 = (bf16[40,16,256]{2,1,0:T(8,128)(2,1)S(1)}, bf16[40,16,256]{2,1,0:T(8,128)(2,1)S(1)}, u32[]{:S(2)}, u32[]{:S(2)}) collective-permute-start(bf16[40,16,256]{2,1,0:T(8,128)(2,1)S(1)} %get-tuple-element.46), channel_id=1, source_target_pairs={{1,0},{2,1},{3,2},{4,3},{5,4},{6,5},{7,6},{8,7},{9,8},{10,9},{11,1... | collective-permute-start | bytes 983048 | tf_op jit(solution)/shard_map/ppermute | solution.py:536
  87.4 42.3 %collective-permute-start.14 = (bf16[6,16,16,256]{3,2,1,0:T(8,128)(2,1)S(1)}, bf16[6,16,16,256]{3,2,1,0:T(8,128)(2,1)S(1)}, u32[]{:S(2)}, u32[]{:S(2)}) collective-permute-start(bf16[6,16,16,256]{3,2,1,0:T(8,128)(2,1)S(1)} %get-tuple-element.49.refs_0_), channel_id=1, source_target_pairs={{16,0},{0,16},{17,1},{1,17},{18,2},{2,18},{19,3},{3,19},{20,4},{4,... | collective-permute-start | bytes 2359304 | tf_op jit(solution)/shard_map/ppermute | solution.py:468
  101.2 28.5 %collective-permute-start.16 = (bf16[6,16,16,256]{3,2,1,0:T(8,128)(2,1)S(1)}, bf16[6,16,16,256]{3,2,1,0:T(8,128)(2,1)S(1)}, u32[]{:S(2)}, u32[]{:S(2)}) collective-permute-start(bf16[6,16,16,256]{3,2,1,0:T(8,128)(2,1)S(1)} %get-tuple-element.51.refs_2_), channel_id=1, source_target_pairs={{16,0},{0,16},{17,1},{1,17},{18,2},{2,18},{19,3},{3,19},{20,4},{4,... | collective-permute-start | bytes 2359304 | tf_op jit(solution)/shard_map/ppermute | solution.py:468
  101.3 2.3 %collective-permute-start.6 = (f32[16,128]{1,0:T(8,128)S(1)}, f32[16,128]{1,0:T(8,128)S(1)}, u32[]{:S(2)}, u32[]{:S(2)}) collective-permute-start(f32[16,128]{1,0:T(8,128)S(1)} %get-tuple-element.35.refs_0_), channel_id=1, source_target_pairs={{16,0},{0,16},{17,1},{1,17},{18,2},{2,18},{19,3},{3,19},{20,4},{4,... | collective-permute-start | bytes 24584 | tf_op jit(solution)/shard_map/ppermute | solution.py:468
  101.8 3.0 %collective-permute-start.7 = (f32[32,128]{1,0:T(8,128)S(1)}, f32[32,128]{1,0:T(8,128)S(1)}, u32[]{:S(2)}, u32[]{:S(2)}) collective-permute-start(f32[32,128]{1,0:T(8,128)S(1)} %get-tuple-element.41.refs_1_), channel_id=1, source_target_pairs={{16,0},{0,16},{17,1},{1,17},{18,2},{2,18},{19,3},{3,19},{20,4},{4,... | collective-permute-start | bytes 49160 | tf_op jit(solution)/shard_map/ppermute | solution.py:468
  103.6 1.2 collective-permute-start.8
  105.6 4.0 %collective-permute-start.9 = (f32[72,128]{1,0:T(8,128)S(1)}, f32[72,128]{1,0:T(8,128)S(1)}, u32[]{:S(2)}, u32[]{:S(2)}) collective-permute-start(f32[72,128]{1,0:T(8,128)S(1)} %gram.1), channel_id=1, source_target_pairs={{0,1},{1,0},{2,3},{3,2},{4,5},{5,4},{6,7},{7,6},{8,9},{9,8},{10,11... | collective-permute-start | bytes 110600 | tf_op jit(solution)/shard_map/ppermute | solution.py:460
  109.6 4.0 %collective-permute-start.10 = (f32[72,128]{1,0:T(8,128)S(1)}, f32[72,128]{1,0:T(8,128)S(1)}, u32[]{:S(2)}, u32[]{:S(2)}) collective-permute-start(f32[72,128]{1,0:T(8,128)S(1)} %add.20), channel_id=1, source_target_pairs={{0,2},{1,3},{2,0},{3,1},{4,6},{5,7},{6,4},{7,5},{8,10},{9,11},{10,... | collective-permute-start | bytes 110600 | tf_op jit(solution)/shard_map/ppermute | solution.py:460
  113.5 4.6 %collective-permute-start.11 = (f32[72,128]{1,0:T(8,128)S(1)}, f32[72,128]{1,0:T(8,128)S(1)}, u32[]{:S(2)}, u32[]{:S(2)}) collective-permute-start(f32[72,128]{1,0:T(8,128)S(1)} %add.21), channel_id=1, source_target_pairs={{0,4},{1,5},{2,6},{3,7},{4,0},{5,1},{6,2},{7,3},{8,12},{9,13},{10,... | collective-permute-start | bytes 110600 | tf_op jit(solution)/shard_map/ppermute | solution.py:460
  118.2 5.0 %collective-permute-start.12 = (f32[72,128]{1,0:T(8,128)S(1)}, f32[72,128]{1,0:T(8,128)S(1)}, u32[]{:S(2)}, u32[]{:S(2)}) collective-permute-start(f32[72,128]{1,0:T(8,128)S(1)} %add.22), channel_id=1, source_target_pairs={{0,8},{1,9},{2,10},{3,11},{4,12},{5,13},{6,14},{7,15},{8,0},{9,1},... | collective-permute-start | bytes 110600 | tf_op jit(solution)/shard_map/ppermute | solution.py:460
  123.2 1.2 collective-permute-start.13

commit v6 on v5

--- a/solution.py
+++ b/solution.py
@@ -536,12 +536,10 @@
         highs.append(lax.ppermute(going_down, "space", down))
 
 
-    def mean_halo(payload):
-        parts = payload[n_halo:].astype(f32)
-        value = parts[:, :, :piece] + parts[:, :, 128 : 128 + piece]
-        return value.reshape(6, DEPTH, piece)
-
-    mean_ext = jnp.concatenate([mean_halo(lows[0]), mean_state, mean_halo(highs[0])], axis=1)
+    parts = jnp.concatenate([lows[0][n_halo:], highs[0][n_halo:]], axis=0)
+    parts = lax.optimization_barrier(parts).astype(f32)
+    halo = (parts[:, :, :piece] + parts[:, :, 128 : 128 + piece]).reshape(12, DEPTH, piece)
+    mean_ext = jnp.concatenate([halo[:6], mean_state, halo[6:]], axis=1)
     mean_ext = lax.all_gather(mean_ext, "cols", axis=2, tiled=True)
     station_row = (stations - first_row * cells).astype(jnp.int32)[None, :]
     weight_row = obs_weight[None, :]

time: 135 us -> 135 us (level)
  no operation moved by 1% of the time
where the time goes in v6:
time: 135 us
  Pallas kernels  53.2 us (39%)
  waiting for transfers between devices  50.2 us (37%)
  starting transfers between devices  25.8 us (19%)
  local copies, waits for them, and re-layouts  2.83 us (2%)
  blocking collectives  1.95 us (1%)
    ppermute x3, waiting for transfers between devices, local(): lows.append(lax.ppermute(going_up, 'space', up))  33.6 us
    pallas_call x3, Pallas kernels, local(): window(where, lows[c], highs[c], wet, coef, station_row, *[flat] * groups)  32.6 us
    ppermute x3, starting transfers between devices, local(): lows.append(lax.ppermute(going_up, 'space', up))  13.1 us
    ppermute x4, waiting for transfers between devices, spread_sum(): lax.ppermute(value, axis, [(i, i ^ step) for i in range(count)])  10 us
    ppermute x4, starting transfers between devices, spread_sum(): lax.ppermute(value, axis, [(i, i ^ step) for i in range(count)])  7.53 us
    pallas_call x3, Pallas kernels, local(): pl.pallas_call(functools.partial(pack_kernel, tile_rows=tile_rows, with_m...  6.77 us
    pallas_call x1, Pallas kernels, local(): pl.pallas_call(functools.partial(mix_kernel, columns=columns), grid=(6,),...  5.35 us
    pallas_call x1, Pallas kernels, local(): pl.pallas_call(functools.partial(factor_kernel, columns=columns), in_spec...  5.3 us
  transfers between devices with their start and end apart: 17, of which 12 were waited for; matrix products, arithmetic and copies ran while one was open for 0% of the time, Pallas kernels for 22%

profile of v6, /device:TPU:0, one launch (start us, length us, event | category | flops | bytes accessed | tf_op | source)
XLA Modules:
  0.0 135.1 jit_solution(7678409654758753406)
XLA Ops:
  0.6 2.3 %shard_map.77 = (bf16[43,16,256]{2,1,0:T(8,128)(2,1)}, bf16[43,16,256]{2,1,0:T(8,128)(2,1)S(1)}) custom-call(f32[6,16,128]{2,1,0:T(8,128)} %refs_0_.1, f32[6144,256]{1,0:T(8,128)} %bitcast.9, f32[6144,256]{1,0:T(8,128)} %bitcast.10), custom_call_target="tpu_custom_call" | custom-call | tf_op jit(solution)/shard_map/pallas_call | solution.py:525
  2.9 0.0 copy-start.3
  3.0 5.0 %collective-permute-start = (bf16[43,16,256]{2,1,0:T(8,128)(2,1)}, bf16[43,16,256]{2,1,0:T(8,128)(2,1)S(1)}, u32[]{:S(2)}, u32[]{:S(2)}) collective-permute-start(bf16[43,16,256]{2,1,0:T(8,128)(2,1)} %get-tuple-element.30), channel_id=1, source_target_pairs={{0,1},{1,2},{2,3},{3,4},{4,5},{5,6},{6,7},{7,8},{8,9},{9,10},{10,1... | collective-permute-start | bytes 1056776 | tf_op jit(solution)/shard_map/ppermute | solution.py:535
  8.0 1.3 collective-permute-start.1
  9.3 2.8 %shard_map.79 = (bf16[40,32,256]{2,1,0:T(8,128)(2,1)}, bf16[40,32,256]{2,1,0:T(8,128)(2,1)S(1)}) custom-call(f32[6144,256]{1,0:T(8,128)} %bitcast.11, f32[6144,256]{1,0:T(8,128)} %bitcast.12), custom_call_target="tpu_custom_call" | custom-call | tf_op jit(solution)/shard_map/pallas_call | solution.py:525
  12.1 4.6 %collective-permute-start.2 = (bf16[40,32,256]{2,1,0:T(8,128)(2,1)}, bf16[40,32,256]{2,1,0:T(8,128)(2,1)S(1)}, u32[]{:S(2)}, u32[]{:S(2)}) collective-permute-start(bf16[40,32,256]{2,1,0:T(8,128)(2,1)} %get-tuple-element.39), channel_id=1, source_target_pairs={{0,1},{1,2},{2,3},{3,4},{4,5},{5,6},{6,7},{7,8},{8,9},{9,10},{10,1... | collective-permute-start | bytes 1966088 | tf_op jit(solution)/shard_map/ppermute | solution.py:535
  16.6 1.3 collective-permute-start.3
  17.9 0.1 pad_add_fusion.where_ref
  18.0 20.5 %collective-permute-done.low_ref = bf16[43,16,256]{2,1,0:T(8,128)(2,1)S(1)} collective-permute-done((bf16[43,16,256]{2,1,0:T(8,128)(2,1)}, bf16[43,16,256]{2,1,0:T(8,128)(2,1)S(1)}, u32[]{:S(2)}, u32[]{:S(2)}) %collective-permute-start) | collective-permute-done | bytes 352288 | tf_op jit(solution)/shard_map/ppermute | solution.py:535
  38.5 0.0 collective-permute-done.1.high_ref
  38.6 1.9 %all_gather.3.mean_ref = f32[6,32,256]{2,1,0:T(8,128)S(1)} all-gather(f32[6,32,128]{2,1,0:T(8,128)S(1)} %pad_maximum_fusion), channel_id=1, replica_groups=mesh['cols'=2,'space'=16] {'cols'}, dimensions={2}, use_global_device_ids=true | all-gather | bytes 294912 | tf_op jit(solution)/shard_map/all_gather | solution.py:543
  40.5 2.4 %mean_window.1 = (f32[192,128]{1,0:T(8,128)S(1)}, f32[1536,128]{1,0:T(8,128)S(1)}, f32[6,16,256]{2,1,0:T(8,128)S(1)}, f32[8,128]{1,0:T(8,128)S(1)}) custom-call(s32[2]{0:T(128)S(1)} %pad_add_fusion.where_ref, f32[6,32,256]{2,1,0:T(8,128)S(1)} %all_gather.3.mean_ref, s32[256,256]{1,0:T(8,128)S(1)} %copy-done.1, ...), custom_call_target="tpu_custom_call" | custom-call | tf_op jit(solution)/shard_map/mean_window/pallas_call | solution.py:559
  42.9 8.5 %collective-permute-done.2.low_ref = bf16[40,32,256]{2,1,0:T(8,128)(2,1)S(1)} collective-permute-done((bf16[40,32,256]{2,1,0:T(8,128)(2,1)}, bf16[40,32,256]{2,1,0:T(8,128)(2,1)S(1)}, u32[]{:S(2)}, u32[]{:S(2)}) %collective-permute-start.2) | collective-permute-done | bytes 655392 | tf_op jit(solution)/shard_map/ppermute | solution.py:535
  51.4 1.8 %collective-permute-done.3.high_ref = bf16[40,32,256]{2,1,0:T(8,128)(2,1)S(1)} collective-permute-done((bf16[40,32,256]{2,1,0:T(8,128)(2,1)S(1)}, bf16[40,32,256]{2,1,0:T(8,128)(2,1)S(1)}, u32[]{:S(2)}, u32[]{:S(2)}) %collective-permute-start.3) | collective-permute-done | bytes 655392 | tf_op jit(solution)/shard_map/ppermute | solution.py:536
  53.2 2.8 %copy-done = f32[64,6,16,256]{3,2,1,0:T(8,128)S(1)} copy-done((f32[64,6,16,256]{3,2,1,0:T(8,128)S(1)}, f32[64,6,16,256]{3,2,1,0:T(8,128)}, u32[]{:S(2)}) %copy-start) | copy-done | bytes 6291480
  56.0 16.3 %shard_map.80 = (bf16[6,16,32,256]{3,2,1,0:T(8,128)(2,1)S(1)}, f32[32,128]{1,0:T(8,128)S(1)}) custom-call(s32[2]{0:T(128)S(1)} %pad_add_fusion.where_ref, bf16[40,32,256]{2,1,0:T(8,128)(2,1)S(1)} %collective-permute-done.2.low_ref, bf16[40,32,256]{2,1,0:T(8,128)(2,1)S(1)} %collective-permute-done.3.high_ref, f32[192,128]{1,0:T(8,128)S(1)} %get-tuple-element.33.wet_ref, ...), custom_call_target="tpu_custom_call" | custom-call | tf_op jit(solution)/shard_map/pallas_call | solution.py:589
  72.3 0.0 slice-start
  72.4 0.1 collective-permute-start.15
  72.4 1.7 %shard_map.81 = (bf16[40,16,256]{2,1,0:T(8,128)(2,1)S(1)}, bf16[40,16,256]{2,1,0:T(8,128)(2,1)S(1)}) custom-call(f32[6144,256]{1,0:T(8,128)} %bitcast.13, f32[6144,256]{1,0:T(8,128)} %bitcast.14), custom_call_target="tpu_custom_call" | custom-call | tf_op jit(solution)/shard_map/pallas_call | solution.py:525
  74.1 3.5 %collective-permute-start.4 = (bf16[40,16,256]{2,1,0:T(8,128)(2,1)S(1)}, bf16[40,16,256]{2,1,0:T(8,128)(2,1)S(1)}, u32[]{:S(2)}, u32[]{:S(2)}) collective-permute-start(bf16[40,16,256]{2,1,0:T(8,128)(2,1)S(1)} %get-tuple-element.45), channel_id=1, source_target_pairs={{0,1},{1,2},{2,3},{3,4},{4,5},{5,6},{6,7},{7,8},{8,9},{9,10},{10,1... | collective-permute-start | bytes 983048 | tf_op jit(solution)/shard_map/ppermute | solution.py:535
  77.7 1.5 %collective-permute-start.5 = (bf16[40,16,256]{2,1,0:T(8,128)(2,1)S(1)}, bf16[40,16,256]{2,1,0:T(8,128)(2,1)S(1)}, u32[]{:S(2)}, u32[]{:S(2)}) collective-permute-start(bf16[40,16,256]{2,1,0:T(8,128)(2,1)S(1)} %get-tuple-element.46), channel_id=1, source_target_pairs={{1,0},{2,1},{3,2},{4,3},{5,4},{6,5},{7,6},{8,7},{9,8},{10,9},{11,1... | collective-permute-start | bytes 983048 | tf_op jit(solution)/shard_map/ppermute | solution.py:536
  79.2 8.2 %shard_map.78 = (bf16[6,16,16,256]{3,2,1,0:T(8,128)(2,1)S(1)}, f32[16,128]{1,0:T(8,128)S(1)}) custom-call(s32[2]{0:T(128)S(1)} %pad_add_fusion.where_ref, bf16[43,16,256]{2,1,0:T(8,128)(2,1)S(1)} %collective-permute-done.low_ref, bf16[43,16,256]{2,1,0:T(8,128)(2,1)S(1)} %collective-permute-done.1.high_ref, f32[192,128]{1,0:T(8,128)S(1)} %get-tuple-element.33.wet_ref, ...), custom_call_target="tpu_custom_call" | custom-call | tf_op jit(solution)/shard_map/pallas_call | solution.py:589
  87.4 0.2 collective-permute-start.14
  87.6 4.6 %collective-permute-done.4.low_ref = bf16[40,16,256]{2,1,0:T(8,128)(2,1)S(1)} collective-permute-done((bf16[40,16,256]{2,1,0:T(8,128)(2,1)S(1)}, bf16[40,16,256]{2,1,0:T(8,128)(2,1)S(1)}, u32[]{:S(2)}, u32[]{:S(2)}) %collective-permute-start.4) | collective-permute-done | bytes 327712 | tf_op jit(solution)/shard_map/ppermute | solution.py:535
  92.3 0.7 collective-permute-done.5.high_ref
  93.0 8.2 %shard_map.82 = (bf16[6,16,16,256]{3,2,1,0:T(8,128)(2,1)S(1)}, f32[16,128]{1,0:T(8,128)S(1)}) custom-call(s32[2]{0:T(128)S(1)} %pad_add_fusion.where_ref, bf16[40,16,256]{2,1,0:T(8,128)(2,1)S(1)} %collective-permute-done.4.low_ref, bf16[40,16,256]{2,1,0:T(8,128)(2,1)S(1)} %collective-permute-done.5.high_ref, f32[192,128]{1,0:T(8,128)S(1)} %get-tuple-element.33.wet_ref, ...), custom_call_target="tpu_custom_call" | custom-call | tf_op jit(solution)/shard_map/pallas_call | solution.py:589
  101.2 0.1 collective-permute-start.16
  101.3 0.5 collective-permute-start.6
  101.8 0.1 collective-permute-start.7
  101.9 1.7 %collective-permute-done.6.refs_3_ = f32[16,128]{1,0:T(8,128)S(1)} collective-permute-done((f32[16,128]{1,0:T(8,128)S(1)}, f32[16,128]{1,0:T(8,128)S(1)}, u32[]{:S(2)}, u32[]{:S(2)}) %collective-permute-start.6) | collective-permute-done | bytes 8224 | tf_op jit(solution)/shard_map/ppermute | solution.py:468
  103.6 0.1 collective-permute-start.8
  103.7 1.0 collective-permute-done.8.refs_5_
  104.7 0.8 gram.1
  105.6 1.8 %collective-permute-start.9 = (f32[72,128]{1,0:T(8,128)S(1)}, f32[72,128]{1,0:T(8,128)S(1)}, u32[]{:S(2)}, u32[]{:S(2)}) collective-permute-start(f32[72,128]{1,0:T(8,128)S(1)} %gram.1), channel_id=1, source_target_pairs={{0,1},{1,0},{2,3},{3,2},{4,5},{5,4},{6,7},{7,6},{8,9},{9,8},{10,11... | collective-permute-start | bytes 110600 | tf_op jit(solution)/shard_map/ppermute | solution.py:460
  107.4 2.2 %collective-permute-done.9 = f32[72,128]{1,0:T(8,128)S(1)} collective-permute-done((f32[72,128]{1,0:T(8,128)S(1)}, f32[72,128]{1,0:T(8,128)S(1)}, u32[]{:S(2)}, u32[]{:S(2)}) %collective-permute-start.9) | collective-permute-done | bytes 36896 | tf_op jit(solution)/shard_map/ppermute | solution.py:460
  109.6 0.0 collective-permute-start.10
  109.6 3.9 %collective-permute-done.10 = f32[72,128]{1,0:T(8,128)S(1)} collective-permute-done((f32[72,128]{1,0:T(8,128)S(1)}, f32[72,128]{1,0:T(8,128)S(1)}, u32[]{:S(2)}, u32[]{:S(2)}) %collective-permute-start.10) | collective-permute-done | bytes 36896 | tf_op jit(solution)/shard_map/ppermute | solution.py:460
  113.5 2.7 %collective-permute-start.11 = (f32[72,128]{1,0:T(8,128)S(1)}, f32[72,128]{1,0:T(8,128)S(1)}, u32[]{:S(2)}, u32[]{:S(2)}) collective-permute-start(f32[72,128]{1,0:T(8,128)S(1)} %add.17), channel_id=1, source_target_pairs={{0,4},{1,5},{2,6},{3,7},{4,0},{5,1},{6,2},{7,3},{8,12},{9,13},{10,... | collective-permute-start | bytes 110600 | tf_op jit(solution)/shard_map/ppermute | solution.py:460
  116.2 1.9 %collective-permute-done.11 = f32[72,128]{1,0:T(8,128)S(1)} collective-permute-done((f32[72,128]{1,0:T(8,128)S(1)}, f32[72,128]{1,0:T(8,128)S(1)}, u32[]{:S(2)}, u32[]{:S(2)}) %collective-permute-start.11) | collective-permute-done | bytes 36896 | tf_op jit(solution)/shard_map/ppermute | solution.py:460
  118.2 3.0 %collective-permute-start.12 = (f32[72,128]{1,0:T(8,128)S(1)}, f32[72,128]{1,0:T(8,128)S(1)}, u32[]{:S(2)}, u32[]{:S(2)}) collective-permute-start(f32[72,128]{1,0:T(8,128)S(1)} %add.18), channel_id=1, source_target_pairs={{0,8},{1,9},{2,10},{3,11},{4,12},{5,13},{6,14},{7,15},{8,0},{9,1},... | collective-permute-start | bytes 110600 | tf_op jit(solution)/shard_map/ppermute | solution.py:460
  121.2 1.9 %collective-permute-done.12 = f32[72,128]{1,0:T(8,128)S(1)} collective-permute-done((f32[72,128]{1,0:T(8,128)S(1)}, f32[72,128]{1,0:T(8,128)S(1)}, u32[]{:S(2)}, u32[]{:S(2)}) %collective-permute-start.12) | collective-permute-done | bytes 36896 | tf_op jit(solution)/shard_map/ppermute | solution.py:460
  123.2 0.0 collective-permute-start.13
  123.2 1.2 collective-permute-done.13.refs_1_
  124.4 5.3 %factor.1.mix_ref = bf16[80,128]{1,0:T(8,128)(2,1)S(1)} custom-call(s32[2]{0:T(128)S(1)} %pad_add_fusion.where_ref, f32[72,128]{1,0:T(8,128)S(1)} %add.19.refs_0_, f32[72,128]{1,0:T(8,128)S(1)} %collective-permute-done.13.refs_1_), custom_call_target="tpu_custom_call" | custom-call | tf_op jit(solution)/shard_map/factor/pallas_call | solution.py:607
  129.7 0.0 collective-permute-done.14.refs_3_
  129.7 0.0 collective-permute-done.16.refs_5_
  129.7 0.0 collective-permute-done.15.refs_4_
  129.7 5.3 %mix.1 = (f32[64,6,16,256]{3,2,1,0:T(8,128)}, f32[6,16,128]{2,1,0:T(8,128)}) custom-call(s32[2]{0:T(128)S(1)} %pad_add_fusion.where_ref, bf16[80,128]{1,0:T(8,128)(2,1)S(1)} %factor.1.mix_ref, f32[6,16,256]{2,1,0:T(8,128)S(1)} %get-tuple-element.48.mean_ref, bf16[6,16,16,256]{3,2,1,0:T(8,128)(2,1)S(1)} %get-tuple-element.49.refs_0_, ...), custom_call_target="tpu_custom_call" | custom-call | tf_op jit(solution)/shard_map/mix/pallas_call | solution.py:618
  (27 shorter events, 0.1 us)
Async XLA Ops:
  2.9 15.1 %copy-start.5 = (s32[128]{0:T(128)S(1)}, s32[128]{0:T(128)}, u32[]{:S(2)}) copy-start(s32[128]{0:T(128)} %param.9) | copy-start | bytes 1540
  2.9 35.6 %copy-start.4 = (f32[6,16,128]{2,1,0:T(8,128)S(1)}, f32[6,16,128]{2,1,0:T(8,128)}, u32[]{:S(2)}) copy-start(f32[6,16,128]{2,1,0:T(8,128)} %refs_0_.1) | copy-start | bytes 147460
  2.9 37.6 %copy-start.1 = (s32[256,256]{1,0:T(8,128)S(1)}, s32[256,256]{1,0:T(8,128)}, u32[]{:S(2)}) copy-start(s32[256,256]{1,0:T(8,128)} %mask_ref.1) | copy-start | bytes 786436
  2.9 37.6 %copy-start.2 = (f32[128]{0:T(128)S(1)}, f32[128]{0:T(128)}, u32[]{:S(2)}) copy-start(f32[128]{0:T(128)} %param.11) | copy-start | bytes 1540
  2.9 37.6 %copy-start.3 = (f32[128]{0:T(128)S(1)}, f32[128]{0:T(128)}, u32[]{:S(2)}) copy-start(f32[128]{0:T(128)} %param.10) | copy-start | bytes 1540
  3.0 35.5 %collective-permute-start = (bf16[43,16,256]{2,1,0:T(8,128)(2,1)}, bf16[43,16,256]{2,1,0:T(8,128)(2,1)S(1)}, u32[]{:S(2)}, u32[]{:S(2)}) collective-permute-start(bf16[43,16,256]{2,1,0:T(8,128)(2,1)} %get-tuple-element.30), channel_id=1, source_target_pairs={{0,1},{1,2},{2,3},{3,4},{4,5},{5,6},{6,7},{7,8},{8,9},{9,10},{10,1... | collective-permute-start | bytes 1056776 | tf_op jit(solution)/shard_map/ppermute | solution.py:535
  8.0 30.5 %collective-permute-start.1 = (bf16[43,16,256]{2,1,0:T(8,128)(2,1)S(1)}, bf16[43,16,256]{2,1,0:T(8,128)(2,1)S(1)}, u32[]{:S(2)}, u32[]{:S(2)}) collective-permute-start(bf16[43,16,256]{2,1,0:T(8,128)(2,1)S(1)} %get-tuple-element.31), channel_id=1, source_target_pairs={{1,0},{2,1},{3,2},{4,3},{5,4},{6,5},{7,6},{8,7},{9,8},{10,9},{11,1... | collective-permute-start | bytes 1056776 | tf_op jit(solution)/shard_map/ppermute | solution.py:536
  12.1 39.3 %collective-permute-start.2 = (bf16[40,32,256]{2,1,0:T(8,128)(2,1)}, bf16[40,32,256]{2,1,0:T(8,128)(2,1)S(1)}, u32[]{:S(2)}, u32[]{:S(2)}) collective-permute-start(bf16[40,32,256]{2,1,0:T(8,128)(2,1)} %get-tuple-element.39), channel_id=1, source_target_pairs={{0,1},{1,2},{2,3},{3,4},{4,5},{5,6},{6,7},{7,8},{8,9},{9,10},{10,1... | collective-permute-start | bytes 1966088 | tf_op jit(solution)/shard_map/ppermute | solution.py:535
  16.6 36.6 %collective-permute-start.3 = (bf16[40,32,256]{2,1,0:T(8,128)(2,1)S(1)}, bf16[40,32,256]{2,1,0:T(8,128)(2,1)S(1)}, u32[]{:S(2)}, u32[]{:S(2)}) collective-permute-start(bf16[40,32,256]{2,1,0:T(8,128)(2,1)S(1)} %get-tuple-element.40), channel_id=1, source_target_pairs={{1,0},{2,1},{3,2},{4,3},{5,4},{6,5},{7,6},{8,7},{9,8},{10,9},{11,1... | collective-permute-start | bytes 1966088 | tf_op jit(solution)/shard_map/ppermute | solution.py:536
  53.2 2.8 %copy-start = (f32[64,6,16,256]{3,2,1,0:T(8,128)S(1)}, f32[64,6,16,256]{3,2,1,0:T(8,128)}, u32[]{:S(2)}) copy-start(f32[64,6,16,256]{3,2,1,0:T(8,128)} %param.7) | copy-start | bytes 18874372
  72.3 6.8 %slice-start = ((s8[6291456]{0:T(1024)(128)(4,1)}), s8[4194304]{0:T(1024)(128)(4,1)S(1)}, s32[]{:S(2)}) async-start(s8[6291456]{0:T(1024)(128)(4,1)} %bitcast.17), calls=%async_computation | async-start | bytes 8388608
  72.4 6.8 %slice-start.1 = ((s8[6291456]{0:T(1024)(128)(4,1)}), s8[2097152]{0:T(1024)(128)(4,1)S(1)}, s32[]{:S(2)}) async-start(s8[6291456]{0:T(1024)(128)(4,1)} %bitcast.17), calls=%async_computation.1 | async-start | bytes 4194304
  72.4 57.4 %collective-permute-start.15 = (bf16[6,16,32,256]{3,2,1,0:T(8,128)(2,1)S(1)}, bf16[6,16,32,256]{3,2,1,0:T(8,128)(2,1)S(1)}, u32[]{:S(2)}, u32[]{:S(2)}) collective-permute-start(bf16[6,16,32,256]{3,2,1,0:T(8,128)(2,1)S(1)} %get-tuple-element.50.refs_1_), channel_id=1, source_target_pairs={{16,0},{0,16},{17,1},{1,17},{18,2},{2,18},{19,3},{3,19},{20,4},{4,... | collective-permute-start | bytes 4718600 | tf_op jit(solution)/shard_map/ppermute | solution.py:468
  74.1 18.1 %collective-permute-start.4 = (bf16[40,16,256]{2,1,0:T(8,128)(2,1)S(1)}, bf16[40,16,256]{2,1,0:T(8,128)(2,1)S(1)}, u32[]{:S(2)}, u32[]{:S(2)}) collective-permute-start(bf16[40,16,256]{2,1,0:T(8,128)(2,1)S(1)} %get-tuple-element.45), channel_id=1, source_target_pairs={{0,1},{1,2},{2,3},{3,4},{4,5},{5,6},{6,7},{7,8},{8,9},{9,10},{10,1... | collective-permute-start | bytes 983048 | tf_op jit(solution)/shard_map/ppermute | solution.py:535
  77.7 15.3 %collective-permute-start.5 = (bf16[40,16,256]{2,1,0:T(8,128)(2,1)S(1)}, bf16[40,16,256]{2,1,0:T(8,128)(2,1)S(1)}, u32[]{:S(2)}, u32[]{:S(2)}) collective-permute-start(bf16[40,16,256]{2,1,0:T(8,128)(2,1)S(1)} %get-tuple-element.46), channel_id=1, source_target_pairs={{1,0},{2,1},{3,2},{4,3},{5,4},{6,5},{7,6},{8,7},{9,8},{10,9},{11,1... | collective-permute-start | bytes 983048 | tf_op jit(solution)/shard_map/ppermute | solution.py:536
  87.4 42.3 %collective-permute-start.14 = (bf16[6,16,16,256]{3,2,1,0:T(8,128)(2,1)S(1)}, bf16[6,16,16,256]{3,2,1,0:T(8,128)(2,1)S(1)}, u32[]{:S(2)}, u32[]{:S(2)}) collective-permute-start(bf16[6,16,16,256]{3,2,1,0:T(8,128)(2,1)S(1)} %get-tuple-element.49.refs_0_), channel_id=1, source_target_pairs={{16,0},{0,16},{17,1},{1,17},{18,2},{2,18},{19,3},{3,19},{20,4},{4,... | collective-permute-start | bytes 2359304 | tf_op jit(solution)/shard_map/ppermute | solution.py:468
  101.2 28.5 %collective-permute-start.16 = (bf16[6,16,16,256]{3,2,1,0:T(8,128)(2,1)S(1)}, bf16[6,16,16,256]{3,2,1,0:T(8,128)(2,1)S(1)}, u32[]{:S(2)}, u32[]{:S(2)}) collective-permute-start(bf16[6,16,16,256]{3,2,1,0:T(8,128)(2,1)S(1)} %get-tuple-element.51.refs_2_), channel_id=1, source_target_pairs={{16,0},{0,16},{17,1},{1,17},{18,2},{2,18},{19,3},{3,19},{20,4},{4,... | collective-permute-start | bytes 2359304 | tf_op jit(solution)/shard_map/ppermute | solution.py:468
  101.3 2.3 %collective-permute-start.6 = (f32[16,128]{1,0:T(8,128)S(1)}, f32[16,128]{1,0:T(8,128)S(1)}, u32[]{:S(2)}, u32[]{:S(2)}) collective-permute-start(f32[16,128]{1,0:T(8,128)S(1)} %get-tuple-element.35.refs_0_), channel_id=1, source_target_pairs={{16,0},{0,16},{17,1},{1,17},{18,2},{2,18},{19,3},{3,19},{20,4},{4,... | collective-permute-start | bytes 24584 | tf_op jit(solution)/shard_map/ppermute | solution.py:468
  101.8 3.0 %collective-permute-start.7 = (f32[32,128]{1,0:T(8,128)S(1)}, f32[32,128]{1,0:T(8,128)S(1)}, u32[]{:S(2)}, u32[]{:S(2)}) collective-permute-start(f32[32,128]{1,0:T(8,128)S(1)} %get-tuple-element.41.refs_1_), channel_id=1, source_target_pairs={{16,0},{0,16},{17,1},{1,17},{18,2},{2,18},{19,3},{3,19},{20,4},{4,... | collective-permute-start | bytes 49160 | tf_op jit(solution)/shard_map/ppermute | solution.py:468
  103.6 1.2 collective-permute-start.8
  105.6 4.0 %collective-permute-start.9 = (f32[72,128]{1,0:T(8,128)S(1)}, f32[72,128]{1,0:T(8,128)S(1)}, u32[]{:S(2)}, u32[]{:S(2)}) collective-permute-start(f32[72,128]{1,0:T(8,128)S(1)} %gram.1), channel_id=1, source_target_pairs={{0,1},{1,0},{2,3},{3,2},{4,5},{5,4},{6,7},{7,6},{8,9},{9,8},{10,11... | collective-permute-start | bytes 110600 | tf_op jit(solution)/shard_map/ppermute | solution.py:460
  109.6 4.0 %collective-permute-start.10 = (f32[72,128]{1,0:T(8,128)S(1)}, f32[72,128]{1,0:T(8,128)S(1)}, u32[]{:S(2)}, u32[]{:S(2)}) collective-permute-start(f32[72,128]{1,0:T(8,128)S(1)} %add.16), channel_id=1, source_target_pairs={{0,2},{1,3},{2,0},{3,1},{4,6},{5,7},{6,4},{7,5},{8,10},{9,11},{10,... | collective-permute-start | bytes 110600 | tf_op jit(solution)/shard_map/ppermute | solution.py:460
  113.5 4.6 %collective-permute-start.11 = (f32[72,128]{1,0:T(8,128)S(1)}, f32[72,128]{1,0:T(8,128)S(1)}, u32[]{:S(2)}, u32[]{:S(2)}) collective-permute-start(f32[72,128]{1,0:T(8,128)S(1)} %add.17), channel_id=1, source_target_pairs={{0,4},{1,5},{2,6},{3,7},{4,0},{5,1},{6,2},{7,3},{8,12},{9,13},{10,... | collective-permute-start | bytes 110600 | tf_op jit(solution)/shard_map/ppermute | solution.py:460
  118.2 5.0 %collective-permute-start.12 = (f32[72,128]{1,0:T(8,128)S(1)}, f32[72,128]{1,0:T(8,128)S(1)}, u32[]{:S(2)}, u32[]{:S(2)}) collective-permute-start(f32[72,128]{1,0:T(8,128)S(1)} %add.18), channel_id=1, source_target_pairs={{0,8},{1,9},{2,10},{3,11},{4,12},{5,13},{6,14},{7,15},{8,0},{9,1},... | collective-permute-start | bytes 110600 | tf_op jit(solution)/shard_map/ppermute | solution.py:460
  123.2 1.2 collective-permute-start.13
